TPU v7x, 512 devices: a whole 4x4x16 slice. The times are simulated.
512 devices in a mesh: bins: 32 (over z, core), nuis: 16 (over y, x).
Axes of the slice: x: 4, y: 4, z: 16, core: 2. Of those that a mesh axis runs over, the one named last changes fastest.
Arguments:
- log_nominal: float32 [8192, 8], P('bins'), may hold values from -1 to 3
- variations: bfloat16 [8192, 8, 2048], P('bins', None, 'nuis'), may hold values from -0.0625 to 0.0625
- observed: int32 [8192], P('bins'), may hold values from 0 to 95
- start: float32 [2048], P('nuis'), may hold values from -5 to 5
- direction: float32 [2048], P('nuis'), may hold values from -5 to 5
- step_lengths: float32 [3], replicated, may hold values from 0.05 to 0.6
Outputs:
- line_change: float32 [3], replicated
- gradient: float32 [2048], P('nuis')
- hessian: float32 [2048, 2048], P('bins', 'nuis')
All inputs are finite; a program needn't handle non-finite values.
Results may differ from a plain program's by a relative error of at most 0.022.
Values may be sent and summed in bfloat16 or wider, within the bound.
No kernel may reach another device: no remote copies, remote signals or barrier semaphores. Data moves between devices by JAX's collectives and lax.ppermute only.
A program may use at most 64 MiB of HBM per device.

v0:
```python
import jax
import jax.numpy as jnp
import numpy as np
from jax import lax
from jax.experimental import pallas as pl
from jax.experimental.pallas import tpu as pltpu
from jax.sharding import Mesh
from jax.sharding import PartitionSpec as P


F32 = jnp.float32
BF16 = jnp.bfloat16
SIDE = 4
PROC = 8
ROWS = 2048
BINS_DEV = 256
LANES = 128
CHUNKS = ROWS // LANES
BIN_TOTAL = 32 * BINS_DEV
DEPTH = ROWS + BINS_DEV
VMEM = pl.BlockSpec(memory_space=pltpu.VMEM)
SMEM = pl.BlockSpec(memory_space=pltpu.SMEM)
PARAMS = pltpu.CompilerParams(vmem_limit_bytes=48 * 1024 * 1024)


def cost(flops, moved):
    return pl.CostEstimate(flops=flops, bytes_accessed=moved, transcendentals=0)


def thirds(x):
    high = x.astype(BF16)
    rest = x - high.astype(F32)
    middle = rest.astype(BF16)
    low = (rest - middle.astype(F32)).astype(BF16)
    return [high, middle, low]


def rows_dot(a, b):
    return lax.dot_general(a, b, (((1,), (0,)), ((), ())), preferred_element_type=F32)


def packed(four):
    return jnp.concatenate(thirds(four) + [jnp.zeros((4, LANES), BF16)], 0)


def unpacked(rows):
    wide = rows.astype(F32)
    return wide[..., 0:4, :] + wide[..., 4:8, :] + wide[..., 8:12, :]


def project_kernel(v_ref, start_ref, dir_ref, steps_ref, out_ref, flat):
    start, direction = start_ref[...], dir_ref[...]
    parts = jnp.concatenate(thirds(start) + thirds(direction), 0)
    six = lax.dot_general(
        parts, v_ref[...], (((1,), (1,)), ((), ())), preferred_element_type=F32
    )
    along_start = six[0:1] + six[1:2] + six[2:3]
    along_dir = six[3:4] + six[4:5] + six[5:6]
    for c in range(CHUNKS):
        span = slice(c * LANES, (c + 1) * LANES)
        flat[c : c + 1, :] = along_start[:, span]
        flat[CHUNKS + c : CHUNKS + c + 1, :] = along_dir[:, span]
    flat[2 * CHUNKS : 2 * CHUNKS + 8, :] = jnp.zeros((8, LANES), F32)
    flat[2 * CHUNKS : 2 * CHUNKS + 1, :] = start * start
    for j in range(3):
        point = start + steps_ref[j] * direction
        flat[2 * CHUNKS + 1 + j : 2 * CHUNKS + 2 + j, :] = point * point
    whole = flat[...]
    for i in range(out_ref.shape[0]):
        out_ref[i] = whole


def lane_groups_sum(x, lane):
    for k in (1, 2, 4):
        up = pltpu.roll(x, k, 1)
        down = pltpu.roll(x, LANES - k, 1)
        x = x + jnp.where((lane & k) != 0, up, down)
    return x


def weights_kernel(got_ref, nominal_ref, counts_ref, steps_ref, v_ref, w_ref, bins_ref, sq_ref):
    total = jnp.sum(got_ref[...], axis=0)
    along_start = total[0:CHUNKS]
    along_dir = total[CHUNKS : 2 * CHUNKS]
    sq_ref[...] = total[2 * CHUNKS : 2 * CHUNKS + 8]
    nominal, counts = nominal_ref[...], counts_ref[...]
    lane = lax.broadcasted_iota(jnp.int32, (CHUNKS, LANES), 1)
    base = jnp.exp(nominal + along_start)
    base_total = lane_groups_sum(base, lane)
    base_log = jnp.log(base_total)
    part = [None] * 3
    for j in range(3):
        shifted = jnp.exp(nominal + (along_start + steps_ref[j] * along_dir))
        expected = lane_groups_sum(shifted, lane)
        change = (expected - base_total) - counts * (jnp.log(expected) - base_log)
        part[j] = jnp.sum(change, axis=0, keepdims=True) * (1.0 / PROC)
    residual = 1.0 - counts / base_total
    left = residual * base
    w_ref[0] = base
    w_ref[1] = left
    w_ref[2] = (counts / (base_total * base_total)) * base
    grad = jnp.zeros((3, LANES), F32)
    for c in range(CHUNKS):
        row = jnp.concatenate(thirds(left[c : c + 1]), 0)
        grad = grad + rows_dot(row, v_ref[c * LANES : (c + 1) * LANES, :])
    grad = jnp.sum(grad, axis=0, keepdims=True)
    bins_ref[...] = packed(jnp.concatenate([grad] + part, 0))


def hessian_kernel(pos_ref, w_ref, extra_ref, own, x1, x3, x2, y1, y3, y2, out_ref, rights, lefts):
    px, py = pos_ref[0], pos_ref[1]
    mine = lax.broadcasted_iota(jnp.int32, (16, LANES), 1) // PROC
    mine = mine == lax.broadcasted_iota(jnp.int32, (16, LANES), 0)
    columns = w_ref[1].T
    for c in range(CHUNKS):
        span = slice(c * LANES, (c + 1) * LANES)
        jac_span = slice(ROWS + c * 16, ROWS + (c + 1) * 16)
        both = []
        for k in (0, 2):
            spread = jnp.where(mine, w_ref[k, c : c + 1, :], 0.0)
            both.append(jnp.concatenate(thirds(spread), 0))
        scale = columns[:, c : c + 1]
        for step, ref in enumerate((own, x1, x2, x3)):
            at = lax.rem(px + step, SIDE)
            rows = ref[span, :]
            rights[at, span, :] = rows
            jac = rows_dot(both[0], rows)
            rights[at, jac_span, :] = (jac[0:16] + jac[16:32] + jac[32:48]).astype(BF16)
        for step, ref in enumerate((own, y1, y2, y3)):
            at = lax.rem(py + step, SIDE)
            rows = ref[span, :]
            lefts[at, span, :] = (scale * rows.astype(F32)).astype(BF16)
            jac = rows_dot(both[1], rows)
            lefts[at, jac_span, :] = (jac[0:16] + jac[16:32] + jac[32:48]).astype(BF16)
    right = jnp.concatenate([rights[k] for k in range(SIDE)], 1)
    for j in range(SIDE):
        term = lax.dot_general(
            right, lefts[j], (((0,), (0,)), ((), ())), preferred_element_type=F32
        ).astype(BF16)
        for half in range(2):
            for i in range(SIDE):
                at = i * LANES + half * 64
                out_ref[half * SIDE + j, i * 64 : (i + 1) * 64, :] = term[at : at + 64]
            out_ref[half * SIDE + j, SIDE * 64 :, :] = extra_ref[...]


def fold_kernel(pos_ref, got_ref, out_ref):
    py = pos_ref[1]
    extra = unpacked(got_ref[py, SIDE * 64 :, :]) + unpacked(got_ref[SIDE + py, SIDE * 64 :, :])
    extra = packed(extra)
    for k in range(SIDE):
        for i in range(SIDE):
            span = slice(i * 64, (i + 1) * 64)
            both = got_ref[k, span, :].astype(F32) + got_ref[SIDE + k, span, :].astype(F32)
            out_ref[k * SIDE + i, 0:64, :] = both.astype(BF16)
            out_ref[k * SIDE + i, 64:, :] = extra


def finish_kernel(pos_ref, got_ref, sq_ref, start_ref, line_ref, grad_ref, hess_ref):
    scale = 1.0 / BIN_TOTAL
    tile = jnp.sum(got_ref[:, 0:64, :].astype(F32), axis=0)
    extra = jnp.sum(unpacked(got_ref[:, 64:, :]), axis=0)
    row = lax.broadcasted_iota(jnp.int32, (64, LANES), 0) + pos_ref[2] * 64
    col = lax.broadcasted_iota(jnp.int32, (64, LANES), 1) + pos_ref[3] * LANES
    hess_ref[...] = (tile + (row == col).astype(F32)) * scale
    grad_ref[...] = (extra[0:1] + start_ref[...]) * scale
    for j in range(3):
        squares = sq_ref[1 + j : 2 + j, :] - sq_ref[0:1, :]
        line_ref[j] = jnp.sum(extra[1 + j : 2 + j, :] + 0.5 * squares) * scale


def arrays_of(*shapes):
    return tuple(jax.ShapeDtypeStruct(s, d) for s, d in shapes)


def from_ahead(array, axis, step):
    return lax.ppermute(array, axis, [((i + step) % SIDE, i) for i in range(SIDE)])


def exchanged(array, axes):
    return lax.all_to_all(array, axes, 0, 0, tiled=True)


def body(log_nominal, variations, observed, start, direction, step_lengths):
    own = variations.reshape(ROWS, LANES)
    y3, x3, y1, x1, y2, x2 = (
        from_ahead(own, axis, k) for k in (3, 1, 2) for axis in ("y", "x")
    )
    sent = pl.pallas_call(
        project_kernel,
        out_shape=jax.ShapeDtypeStruct((16, 40, LANES), F32),
        in_specs=[VMEM, VMEM, VMEM, SMEM],
        out_specs=VMEM,
        scratch_shapes=[pltpu.VMEM((40, LANES), F32)],
        compiler_params=PARAMS,
        cost_estimate=cost(10_000_000, 1_000_000),
        name="project",
    )(own, start[None, :], direction[None, :], step_lengths)
    got = exchanged(sent, ("y", "x"))
    nominal = log_nominal.reshape(CHUNKS, LANES)
    counts = jnp.repeat(observed.astype(F32), PROC).reshape(CHUNKS, LANES)
    weights, extra, squares = pl.pallas_call(
        weights_kernel,
        out_shape=arrays_of(
            ((3, CHUNKS, LANES), F32), ((16, LANES), BF16), ((8, LANES), F32)
        ),
        in_specs=[VMEM, VMEM, VMEM, SMEM, VMEM],
        out_specs=(VMEM, VMEM, VMEM),
        compiler_params=PARAMS,
        cost_estimate=cost(10_000_000, 1_000_000),
        name="weights",
    )(got, nominal, counts, step_lengths, own)
    px, py = lax.axis_index("x"), lax.axis_index("y")
    block = lax.axis_index("z") * 2 + lax.axis_index("core")
    position = jnp.stack([px, py, block, py * SIDE + px]).astype(jnp.int32)
    term = pl.pallas_call(
        hessian_kernel,
        out_shape=jax.ShapeDtypeStruct((8, SIDE * 64 + 16, LANES), BF16),
        in_specs=[SMEM] + [VMEM] * 9,
        out_specs=VMEM,
        scratch_shapes=[
            pltpu.VMEM((SIDE, DEPTH, LANES), BF16),
            pltpu.VMEM((SIDE, DEPTH, LANES), BF16),
        ],
        compiler_params=PARAMS,
        cost_estimate=cost(2_000_000_000, 5_000_000),
        name="hessian",
    )(position, weights, extra, own, x1, x3, x2, y1, y3, y2)
    pair = pl.pallas_call(
        fold_kernel,
        out_shape=jax.ShapeDtypeStruct((16, 80, LANES), BF16),
        in_specs=[SMEM, VMEM],
        out_specs=VMEM,
        compiler_params=PARAMS,
        cost_estimate=cost(1_000_000, 1_000_000),
        name="fold",
    )(position, exchanged(term, ("core", "y")))
    line_change, gradient, hessian = pl.pallas_call(
        finish_kernel,
        out_shape=arrays_of(((3,), F32), ((1, LANES), F32), ((64, LANES), F32)),
        in_specs=[SMEM, VMEM, VMEM, VMEM],
        out_specs=(SMEM, VMEM, VMEM),
        compiler_params=PARAMS,
        cost_estimate=cost(1_000_000, 1_000_000),
        name="finish",
    )(position, exchanged(pair, "z"), squares, start[None, :])
    return line_change, gradient[0], hessian


def solution(mesh):
    split = Mesh(
        np.asarray(mesh.devices).reshape(16, 2, SIDE, SIDE), ("z", "core", "y", "x")
    )
    bins, nuis = ("z", "core"), ("y", "x")
    placed = (P(bins, None), P(bins, None, nuis), P(bins), P(nuis), P(nuis), P())
    return jax.shard_map(
        body,
        mesh=split,
        in_specs=placed,
        out_specs=(P(), P(nuis), P(bins, nuis)),
        check_vma=False,
    )
```

profile of v0, /device:TPU:2, one launch (start us, length us, event | category | flops | bytes accessed | tf_op | source)
XLA Modules:
  0.0 103.1 jit_solution(13138637235933150714)
XLA Ops:
  0.6 5.1 %collective-permute-start.5 = (bf16[2048,128]{1,0:T(8,128)(2,1)}, bf16[2048,128]{1,0:T(8,128)(2,1)S(1)}, u32[]{:S(2)}, u32[]{:S(2)}) collective-permute-start(bf16[2048,128]{1,0:T(8,128)(2,1)} %bitcast.10), channel_id=1, source_target_pairs={{8,0},{12,4},{0,8},{4,12},{9,1},{13,5},{1,9},{5,13},{10,2},{14,6},... | collective-permute-start | bytes 1572872 | tf_op jit(solution)/shard_map/ppermute | solution.py:177
  5.7 2.6 %collective-permute-start.4 = (bf16[2048,128]{1,0:T(8,128)(2,1)}, bf16[2048,128]{1,0:T(8,128)(2,1)S(1)}, u32[]{:S(2)}, u32[]{:S(2)}) collective-permute-start(bf16[2048,128]{1,0:T(8,128)(2,1)} %bitcast.11), channel_id=1, source_target_pairs={{12,0},{0,4},{4,8},{8,12},{13,1},{1,5},{5,9},{9,13},{14,2},{2,6},{... | collective-permute-start | bytes 1572872 | tf_op jit(solution)/shard_map/ppermute | solution.py:177
  8.3 4.5 %collective-permute-start.3 = (bf16[2048,128]{1,0:T(8,128)(2,1)}, bf16[2048,128]{1,0:T(8,128)(2,1)S(1)}, u32[]{:S(2)}, u32[]{:S(2)}) collective-permute-start(bf16[2048,128]{1,0:T(8,128)(2,1)} %bitcast.12), channel_id=1, source_target_pairs={{4,0},{8,4},{12,8},{0,12},{5,1},{9,5},{13,9},{1,13},{6,2},{10,6},{... | collective-permute-start | bytes 1572872 | tf_op jit(solution)/shard_map/ppermute | solution.py:177
  12.8 4.0 %collective-permute-start.2 = (bf16[2048,128]{1,0:T(8,128)(2,1)}, bf16[2048,128]{1,0:T(8,128)(2,1)S(1)}, u32[]{:S(2)}, u32[]{:S(2)}) collective-permute-start(bf16[2048,128]{1,0:T(8,128)(2,1)} %bitcast.13), channel_id=1, source_target_pairs={{2,0},{3,1},{0,2},{1,3},{6,4},{7,5},{4,6},{5,7},{10,8},{11,9},{8,1... | collective-permute-start | bytes 1572872 | tf_op jit(solution)/shard_map/ppermute | solution.py:177
  16.9 3.9 %collective-permute-start.1 = (bf16[2048,128]{1,0:T(8,128)(2,1)}, bf16[2048,128]{1,0:T(8,128)(2,1)S(1)}, u32[]{:S(2)}, u32[]{:S(2)}) collective-permute-start(bf16[2048,128]{1,0:T(8,128)(2,1)} %bitcast.14), channel_id=1, source_target_pairs={{3,0},{0,1},{1,2},{2,3},{7,4},{4,5},{5,6},{6,7},{11,8},{8,9},{9,10... | collective-permute-start | bytes 1572872 | tf_op jit(solution)/shard_map/ppermute | solution.py:177
  20.8 0.0 collective-permute-done.5.y2
  20.8 5.1 %collective-permute-start = (bf16[2048,128]{1,0:T(8,128)(2,1)}, bf16[2048,128]{1,0:T(8,128)(2,1)}, u32[]{:S(2)}, u32[]{:S(2)}) collective-permute-start(bf16[2048,128]{1,0:T(8,128)(2,1)} %bitcast.15), channel_id=1, source_target_pairs={{1,0},{2,1},{3,2},{0,3},{5,4},{6,5},{7,6},{4,7},{9,8},{10,9},{11,1... | collective-permute-start | bytes 1572872 | tf_op jit(solution)/shard_map/ppermute | solution.py:177
  25.9 0.0 copy-start.2
  25.9 0.0 copy-start.3
  25.9 0.0 copy-start.4
  26.0 0.6 copy-done.2
  26.6 0.0 copy-done.3
  26.6 0.0 copy-done.4
  26.6 0.0 copy-start
  26.6 1.0 %copy-done = bf16[256,8,128]{2,1,0:T(8,128)(2,1)S(1)} copy-done((bf16[256,8,128]{2,1,0:T(8,128)(2,1)S(1)}, bf16[256,8,128]{2,1,0:T(8,128)(2,1)}, u32[]{:S(2)}) %copy-start) | copy-done | bytes 524312
  27.7 1.5 %project.1 = f32[16,40,128]{2,1,0:T(8,128)} custom-call(bf16[2048,128]{1,0:T(8,128)(2,1)S(1)} %bitcast.16, f32[1,128]{1,0:T(1,128)S(1)} %bitcast.19, f32[1,128]{1,0:T(1,128)S(1)} %bitcast.21, f32[3]{0:T(128)S(1)} %copy-done.2), custom_call_target="tpu_custom_call" | custom-call | flops 10000000 | bytes 1000000 | tf_op jit(solution)/shard_map/project/pallas_call | solution.py:189
  29.2 0.0 copy-start.1
  29.2 4.1 %all-to-all-start = ((f32[16,40,128]{2,1,0:T(8,128)}), f32[16,40,128]{2,1,0:T(8,128)S(1)}, u32[]{:S(2)}, u32[]{:S(2)}) async-start(f32[16,40,128]{2,1,0:T(8,128)} %project.1), calls=%async_computation | async-start | bytes 655360 | tf_op jit(solution)/shard_map/all_to_all | solution.py:181
  33.3 0.0 copy-start.6
  33.3 0.7 copy-done.6
  33.9 0.1 broadcast_in_dim.16
  34.0 0.1 copy.13
  34.1 0.6 broadcast_bitcast_fusion
  34.7 0.0 copy-start.5
  34.7 0.9 copy.14.counts_ref
  35.6 0.0 copy-done.5
  35.6 0.8 copy.12
  36.4 1.0 reshape.15.nominal_ref
  37.5 0.1 pad_add_fusion.pos_ref
  37.5 6.2 %all-to-all-done.got_ref = f32[16,40,128]{2,1,0:T(8,128)S(1)} async-done(((f32[16,40,128]{2,1,0:T(8,128)}), f32[16,40,128]{2,1,0:T(8,128)S(1)}, u32[]{:S(2)}, u32[]{:S(2)}) %all-to-all-start) | async-done | bytes 327712 | tf_op jit(solution)/shard_map/all_to_all | solution.py:181
  43.8 0.0 copy-done.1
  43.8 1.0 %weights.1 = (f32[3,16,128]{2,1,0:T(8,128)S(1)}, bf16[16,128]{1,0:T(8,128)(2,1)S(1)}, f32[8,128]{1,0:T(8,128)S(1)}) custom-call(f32[16,40,128]{2,1,0:T(8,128)S(1)} %all-to-all-done.got_ref, f32[16,128]{1,0:T(8,128)S(1)} %reshape.15.nominal_ref, f32[16,128]{1,0:T(8,128)S(1)} %copy.14.counts_ref, f32[3]{0:T(128)S(1)} %copy-done.2, bf16[2048,128]{1,0:T(8,128)(2,1)S(1)} %bitcast.17), custom_call_target="tpu_custom_call" | custom-call | flops 10000000 | bytes 1000000 | tf_op jit(solution)/shard_map/weights/pallas_call | solution.py:202
  44.8 0.0 collective-permute-done.4.y3
  44.8 0.0 collective-permute-done.3.y1
  44.8 0.0 collective-permute-done.2.x2
  44.9 0.0 collective-permute-done.1.x3
  44.9 0.0 collective-permute-done.x1
  44.9 5.6 %hessian.1 = bf16[8,272,128]{2,1,0:T(8,128)(2,1)S(1)} custom-call(s32[4]{0:T(128)S(1)} %pad_add_fusion.pos_ref, f32[3,16,128]{2,1,0:T(8,128)S(1)} %get-tuple-element.9.w_ref, bf16[16,128]{1,0:T(8,128)(2,1)S(1)} %get-tuple-element.10.extra_ref, bf16[2048,128]{1,0:T(8,128)(2,1)S(1)} %bitcast.18, bf16[2048,128]{1,0:T(8,128)(2,1)} %collective-permute-done.x1, ...), custom_call_target="tpu_custom_call" | custom-call | flops 2000000000 | bytes 5000000 | tf_op jit(solution)/shard_map/hessian/pallas_call | solution.py:216
  50.5 14.4 %all_to_all.15.got_ref = bf16[8,272,128]{2,1,0:T(8,128)(2,1)S(1)} all-to-all(bf16[8,272,128]{2,1,0:T(8,128)(2,1)S(1)} %hessian.1), channel_id=1, replica_groups=mesh['z'=16,'core'=2,'y'=4,'x'=4] {'core','y'}, dimensions={0} | all-to-all | bytes 1114112 | tf_op jit(solution)/shard_map/all_to_all | solution.py:181
  64.9 0.6 fold.1
  65.5 36.3 %all_to_all.16.got_ref = bf16[16,80,128]{2,1,0:T(8,128)(2,1)S(1)} all-to-all(bf16[16,80,128]{2,1,0:T(8,128)(2,1)S(1)} %fold.1), channel_id=1, replica_groups=mesh['z'=16,'core'=2,'y'=4,'x'=4] {'z'}, dimensions={0} | all-to-all | bytes 655360 | tf_op jit(solution)/shard_map/all_to_all | solution.py:181
  101.8 1.2 %finish.1 = (f32[3]{0:T(128)}, f32[1,128]{1,0:T(1,128)}, f32[64,128]{1,0:T(8,128)}) custom-call(s32[4]{0:T(128)S(1)} %pad_add_fusion.pos_ref, bf16[16,80,128]{2,1,0:T(8,128)(2,1)S(1)} %all_to_all.16.got_ref, f32[8,128]{1,0:T(8,128)S(1)} %get-tuple-element.11.sq_ref, f32[1,128]{1,0:T(1,128)S(1)} %bitcast.20), custom_call_target="tpu_custom_call" | custom-call | flops 1000000 | bytes 1000000 | tf_op jit(solution)/shard_map/finish/pallas_call | solution.py:238
  (1 shorter events, 0.0 us)
Async XLA Ops:
  0.6 20.2 %collective-permute-start.5 = (bf16[2048,128]{1,0:T(8,128)(2,1)}, bf16[2048,128]{1,0:T(8,128)(2,1)S(1)}, u32[]{:S(2)}, u32[]{:S(2)}) collective-permute-start(bf16[2048,128]{1,0:T(8,128)(2,1)} %bitcast.10), channel_id=1, source_target_pairs={{8,0},{12,4},{0,8},{4,12},{9,1},{13,5},{1,9},{5,13},{10,2},{14,6},... | collective-permute-start | bytes 1572872 | tf_op jit(solution)/shard_map/ppermute | solution.py:177
  5.7 39.1 %collective-permute-start.4 = (bf16[2048,128]{1,0:T(8,128)(2,1)}, bf16[2048,128]{1,0:T(8,128)(2,1)S(1)}, u32[]{:S(2)}, u32[]{:S(2)}) collective-permute-start(bf16[2048,128]{1,0:T(8,128)(2,1)} %bitcast.11), channel_id=1, source_target_pairs={{12,0},{0,4},{4,8},{8,12},{13,1},{1,5},{5,9},{9,13},{14,2},{2,6},{... | collective-permute-start | bytes 1572872 | tf_op jit(solution)/shard_map/ppermute | solution.py:177
  8.3 36.5 %collective-permute-start.3 = (bf16[2048,128]{1,0:T(8,128)(2,1)}, bf16[2048,128]{1,0:T(8,128)(2,1)S(1)}, u32[]{:S(2)}, u32[]{:S(2)}) collective-permute-start(bf16[2048,128]{1,0:T(8,128)(2,1)} %bitcast.12), channel_id=1, source_target_pairs={{4,0},{8,4},{12,8},{0,12},{5,1},{9,5},{13,9},{1,13},{6,2},{10,6},{... | collective-permute-start | bytes 1572872 | tf_op jit(solution)/shard_map/ppermute | solution.py:177
  12.8 32.0 %collective-permute-start.2 = (bf16[2048,128]{1,0:T(8,128)(2,1)}, bf16[2048,128]{1,0:T(8,128)(2,1)S(1)}, u32[]{:S(2)}, u32[]{:S(2)}) collective-permute-start(bf16[2048,128]{1,0:T(8,128)(2,1)} %bitcast.13), channel_id=1, source_target_pairs={{2,0},{3,1},{0,2},{1,3},{6,4},{7,5},{4,6},{5,7},{10,8},{11,9},{8,1... | collective-permute-start | bytes 1572872 | tf_op jit(solution)/shard_map/ppermute | solution.py:177
  16.9 28.0 %collective-permute-start.1 = (bf16[2048,128]{1,0:T(8,128)(2,1)}, bf16[2048,128]{1,0:T(8,128)(2,1)S(1)}, u32[]{:S(2)}, u32[]{:S(2)}) collective-permute-start(bf16[2048,128]{1,0:T(8,128)(2,1)} %bitcast.14), channel_id=1, source_target_pairs={{3,0},{0,1},{1,2},{2,3},{7,4},{4,5},{5,6},{6,7},{11,8},{8,9},{9,10... | collective-permute-start | bytes 1572872 | tf_op jit(solution)/shard_map/ppermute | solution.py:177
  20.8 24.0 %collective-permute-start = (bf16[2048,128]{1,0:T(8,128)(2,1)}, bf16[2048,128]{1,0:T(8,128)(2,1)}, u32[]{:S(2)}, u32[]{:S(2)}) collective-permute-start(bf16[2048,128]{1,0:T(8,128)(2,1)} %bitcast.15), channel_id=1, source_target_pairs={{1,0},{2,1},{3,2},{0,3},{5,4},{6,5},{7,6},{4,7},{9,8},{10,9},{11,1... | collective-permute-start | bytes 1572872 | tf_op jit(solution)/shard_map/ppermute | solution.py:177
  25.9 0.7 copy-start.2
  25.9 0.7 copy-start.3
  25.9 0.7 copy-start.4
  26.6 1.0 %copy-start = (bf16[256,8,128]{2,1,0:T(8,128)(2,1)S(1)}, bf16[256,8,128]{2,1,0:T(8,128)(2,1)}, u32[]{:S(2)}) copy-start(bf16[256,8,128]{2,1,0:T(8,128)(2,1)} %param.7) | copy-start | bytes 1572868
  29.2 14.6 %copy-start.1 = (bf16[256,8,128]{2,1,0:T(8,128)(2,1)S(1)}, bf16[256,8,128]{2,1,0:T(8,128)(2,1)}, u32[]{:S(2)}) copy-start(bf16[256,8,128]{2,1,0:T(8,128)(2,1)} %param.7) | copy-start | bytes 1572868
  29.2 14.6 %all-to-all-start = ((f32[16,40,128]{2,1,0:T(8,128)}), f32[16,40,128]{2,1,0:T(8,128)S(1)}, u32[]{:S(2)}, u32[]{:S(2)}) async-start(f32[16,40,128]{2,1,0:T(8,128)} %project.1), calls=%async_computation | async-start | bytes 655360 | tf_op jit(solution)/shard_map/all_to_all | solution.py:181
  33.3 0.7 copy-start.6
  34.7 0.9 copy-start.5
where the time goes:
time: 104 us; the launch traced here: 103 us
  blocking collectives  50.7 us (49%)
  starting transfers between devices  29.3 us (28%)
  Pallas kernels  10 us (10%)
  waiting for transfers between devices  6.24 us (6%)
  local copies, waits for them, and re-layouts  5.88 us (6%)
    all_to_all x2, blocking collectives, exchanged(): return lax.all_to_all(array, axes, 0, 0, tiled=True)  50.7 us
    ppermute x6, starting transfers between devices, from_ahead(): lax.ppermute(array, axis, [((i + step) % SIDE, i) for i in range(SIDE)])  25.2 us
    all_to_all x1, waiting for transfers between devices, exchanged(): return lax.all_to_all(array, axes, 0, 0, tiled=True)  6.23 us
    pallas_call x1, Pallas kernels, body(): pl.pallas_call(hessian_kernel, out_shape=jax.ShapeDtypeStruct((8, SIDE *...  5.61 us
    all_to_all x1, starting transfers between devices, exchanged(): return lax.all_to_all(array, axes, 0, 0, tiled=True)  4.08 us
    unnamed x15, local copies, waits for them, and re-layouts  3.19 us
  transfers between devices with their start and end apart: 7, of which 1 were waited for; matrix products, arithmetic and copies ran while one was open for 3% of the time, Pallas kernels for 2%

commit v1 on v0

--- a/solution.py
+++ b/solution.py
@@ -16,6 +16,7 @@
 BINS_DEV = 256
 LANES = 128
 CHUNKS = ROWS // LANES
+PIECES = SIDE * SIDE
 BIN_TOTAL = 32 * BINS_DEV
 DEPTH = ROWS + BINS_DEV
 VMEM = pl.BlockSpec(memory_space=pltpu.VMEM)
@@ -107,8 +108,10 @@
     bins_ref[...] = packed(jnp.concatenate([grad] + part, 0))
 
 
-def hessian_kernel(pos_ref, w_ref, extra_ref, own, x1, x3, x2, y1, y3, y2, out_ref, rights, lefts):
-    px, py = pos_ref[0], pos_ref[1]
+def hessian_kernel(
+    pos_ref, w_ref, extra_ref, own, x1, y1, x3, y3, x2, y2, kept_ref, sent_ref, rights, lefts
+):
+    px, py, core = pos_ref[0], pos_ref[1], pos_ref[4]
     mine = lax.broadcasted_iota(jnp.int32, (16, LANES), 1) // PROC
     mine = mine == lax.broadcasted_iota(jnp.int32, (16, LANES), 0)
     columns = w_ref[1].T
@@ -136,24 +139,37 @@
     for j in range(SIDE):
         term = lax.dot_general(
             right, lefts[j], (((0,), (0,)), ((), ())), preferred_element_type=F32
-        ).astype(BF16)
-        for half in range(2):
-            for i in range(SIDE):
-                at = i * LANES + half * 64
-                out_ref[half * SIDE + j, i * 64 : (i + 1) * 64, :] = term[at : at + 64]
-            out_ref[half * SIDE + j, SIDE * 64 :, :] = extra_ref[...]
-
-
-def fold_kernel(pos_ref, got_ref, out_ref):
+        )
+        for i in range(SIDE):
+            first = term[i * LANES : i * LANES + 64]
+            second = term[i * LANES + 64 : (i + 1) * LANES]
+            at = (i * SIDE + j) * 64
+            kept_ref[at : at + 64, :] = jnp.where(core == 0, first, second)
+            sent_ref[at : at + 64, :] = jnp.where(core == 0, second, first).astype(BF16)
+    sent_ref[PIECES * 64 :, :] = extra_ref[...]
+
+
+def pair_kernel(kept_ref, extra_ref, got_ref, out_ref):
+    extra = packed(unpacked(extra_ref[...]) + unpacked(got_ref[PIECES * 64 :, :]))
+    for k in range(PIECES):
+        span = slice(k * 64, (k + 1) * 64)
+        both = kept_ref[span, :] + got_ref[span, :].astype(F32)
+        out_ref[k, 0:64, :] = both.astype(BF16)
+        out_ref[k, 64:, :] = extra
+
+
+def plane_kernel(pos_ref, got_ref, out_ref):
     py = pos_ref[1]
-    extra = unpacked(got_ref[py, SIDE * 64 :, :]) + unpacked(got_ref[SIDE + py, SIDE * 64 :, :])
+    extra = unpacked(got_ref[py, 64:, :])
+    for k in range(1, SIDE):
+        extra = extra + unpacked(got_ref[k * SIDE + py, 64:, :])
     extra = packed(extra)
-    for k in range(SIDE):
-        for i in range(SIDE):
-            span = slice(i * 64, (i + 1) * 64)
-            both = got_ref[k, span, :].astype(F32) + got_ref[SIDE + k, span, :].astype(F32)
-            out_ref[k * SIDE + i, 0:64, :] = both.astype(BF16)
-            out_ref[k * SIDE + i, 64:, :] = extra
+    for j in range(SIDE):
+        tile = got_ref[j, 0:64, :].astype(F32)
+        for k in range(1, SIDE):
+            tile = tile + got_ref[k * SIDE + j, 0:64, :].astype(F32)
+        out_ref[j, 0:64, :] = tile.astype(BF16)
+        out_ref[j, 64:, :] = extra
 
 
 def finish_kernel(pos_ref, got_ref, sq_ref, start_ref, line_ref, grad_ref, hess_ref):
@@ -211,13 +227,16 @@
         name="weights",
     )(got, nominal, counts, step_lengths, own)
     px, py = lax.axis_index("x"), lax.axis_index("y")
-    block = lax.axis_index("z") * 2 + lax.axis_index("core")
-    position = jnp.stack([px, py, block, py * SIDE + px]).astype(jnp.int32)
-    term = pl.pallas_call(
+    core = lax.axis_index("core")
+    block = lax.axis_index(("zh", "zl", "core"))
+    position = jnp.stack([px, py, block, py * SIDE + px, core]).astype(jnp.int32)
+    kept, other = pl.pallas_call(
         hessian_kernel,
-        out_shape=jax.ShapeDtypeStruct((8, SIDE * 64 + 16, LANES), BF16),
+        out_shape=arrays_of(
+            ((PIECES * 64, LANES), F32), ((PIECES * 64 + 16, LANES), BF16)
+        ),
         in_specs=[SMEM] + [VMEM] * 9,
-        out_specs=VMEM,
+        out_specs=(VMEM, VMEM),
         scratch_shapes=[
             pltpu.VMEM((SIDE, DEPTH, LANES), BF16),
             pltpu.VMEM((SIDE, DEPTH, LANES), BF16),
@@ -225,16 +244,26 @@
         compiler_params=PARAMS,
         cost_estimate=cost(2_000_000_000, 5_000_000),
         name="hessian",
-    )(position, weights, extra, own, x1, x3, x2, y1, y3, y2)
+    )(position, weights, extra, own, x1, y1, x3, y3, x2, y2)
+    swapped = lax.ppermute(other, "core", [(0, 1), (1, 0)])
     pair = pl.pallas_call(
-        fold_kernel,
-        out_shape=jax.ShapeDtypeStruct((16, 80, LANES), BF16),
+        pair_kernel,
+        out_shape=jax.ShapeDtypeStruct((PIECES, 80, LANES), BF16),
+        in_specs=[VMEM] * 3,
+        out_specs=VMEM,
+        compiler_params=PARAMS,
+        cost_estimate=cost(1_000_000, 1_000_000),
+        name="pair",
+    )(kept, extra, swapped)
+    near = pl.pallas_call(
+        plane_kernel,
+        out_shape=jax.ShapeDtypeStruct((SIDE, 80, LANES), BF16),
         in_specs=[SMEM, VMEM],
         out_specs=VMEM,
         compiler_params=PARAMS,
         cost_estimate=cost(1_000_000, 1_000_000),
-        name="fold",
-    )(position, exchanged(term, ("core", "y")))
+        name="plane",
+    )(position, exchanged(pair, ("zl", "y")))
     line_change, gradient, hessian = pl.pallas_call(
         finish_kernel,
         out_shape=arrays_of(((3,), F32), ((1, LANES), F32), ((64, LANES), F32)),
@@ -243,15 +272,16 @@
         compiler_params=PARAMS,
         cost_estimate=cost(1_000_000, 1_000_000),
         name="finish",
-    )(position, exchanged(pair, "z"), squares, start[None, :])
+    )(position, exchanged(near, "zh"), squares, start[None, :])
     return line_change, gradient[0], hessian
 
 
 def solution(mesh):
     split = Mesh(
-        np.asarray(mesh.devices).reshape(16, 2, SIDE, SIDE), ("z", "core", "y", "x")
-    )
-    bins, nuis = ("z", "core"), ("y", "x")
+        np.asarray(mesh.devices).reshape(SIDE, SIDE, 2, SIDE, SIDE),
+        ("zh", "zl", "core", "y", "x"),
+    )
+    bins, nuis = ("zh", "zl", "core"), ("y", "x")
     placed = (P(bins, None), P(bins, None, nuis), P(bins), P(nuis), P(nuis), P())
     return jax.shard_map(
         body,

time: 104 us -> 97.4 us (0.937)
  the two profiles are of different devices: /device:TPU:2 before, /device:TPU:38 now
where the time goes in v1:
time: 97.4 us; the launch traced here: 96.8 us
  blocking collectives  44.8 us (46%)
  starting transfers between devices  30.3 us (31%)
  Pallas kernels  10.1 us (10%)
  local copies, waits for them, and re-layouts  5.97 us (6%)
  waiting for transfers between devices  4.83 us (5%)
    all_to_all x2, blocking collectives, exchanged(): return lax.all_to_all(array, axes, 0, 0, tiled=True)  44.8 us
    ppermute x6, starting transfers between devices, from_ahead(): lax.ppermute(array, axis, [((i + step) % SIDE, i) for i in range(SIDE)])  21.4 us
    all_to_all x1, starting transfers between devices, exchanged(): return lax.all_to_all(array, axes, 0, 0, tiled=True)  7.01 us
    pallas_call x1, Pallas kernels, body(): pl.pallas_call(hessian_kernel, out_shape=arrays_of(((PIECES * 64, LANES),...  5.64 us
    all_to_all x1, waiting for transfers between devices, exchanged(): return lax.all_to_all(array, axes, 0, 0, tiled=True)  3.31 us
    unnamed x15, local copies, waits for them, and re-layouts  3.19 us
  transfers between devices with their start and end apart: 8, of which 2 were waited for; matrix products, arithmetic and copies ran while one was open for 4% of the time, Pallas kernels for 3%

profile of v1, /device:TPU:38, one launch (start us, length us, event | category | flops | bytes accessed | tf_op | source)
XLA Modules:
  0.0 96.8 jit_solution(9065182142483278767)
XLA Ops:
  0.6 5.1 %collective-permute-start.5 = (bf16[2048,128]{1,0:T(8,128)(2,1)}, bf16[2048,128]{1,0:T(8,128)(2,1)S(1)}, u32[]{:S(2)}, u32[]{:S(2)}) collective-permute-start(bf16[2048,128]{1,0:T(8,128)(2,1)} %bitcast.11), channel_id=1, source_target_pairs={{8,0},{12,4},{0,8},{4,12},{9,1},{13,5},{1,9},{5,13},{10,2},{14,6},... | collective-permute-start | bytes 1572872 | tf_op jit(solution)/shard_map/ppermute | solution.py:193
  5.7 3.3 %collective-permute-start.4 = (bf16[2048,128]{1,0:T(8,128)(2,1)}, bf16[2048,128]{1,0:T(8,128)(2,1)S(1)}, u32[]{:S(2)}, u32[]{:S(2)}) collective-permute-start(bf16[2048,128]{1,0:T(8,128)(2,1)} %bitcast.12), channel_id=1, source_target_pairs={{2,0},{3,1},{0,2},{1,3},{6,4},{7,5},{4,6},{5,7},{10,8},{11,9},{8,1... | collective-permute-start | bytes 1572872 | tf_op jit(solution)/shard_map/ppermute | solution.py:193
  9.1 2.6 %collective-permute-start.3 = (bf16[2048,128]{1,0:T(8,128)(2,1)}, bf16[2048,128]{1,0:T(8,128)(2,1)S(1)}, u32[]{:S(2)}, u32[]{:S(2)}) collective-permute-start(bf16[2048,128]{1,0:T(8,128)(2,1)} %bitcast.13), channel_id=1, source_target_pairs={{12,0},{0,4},{4,8},{8,12},{13,1},{1,5},{5,9},{9,13},{14,2},{2,6},{... | collective-permute-start | bytes 1572872 | tf_op jit(solution)/shard_map/ppermute | solution.py:193
  11.7 4.0 %collective-permute-start.2 = (bf16[2048,128]{1,0:T(8,128)(2,1)}, bf16[2048,128]{1,0:T(8,128)(2,1)S(1)}, u32[]{:S(2)}, u32[]{:S(2)}) collective-permute-start(bf16[2048,128]{1,0:T(8,128)(2,1)} %bitcast.14), channel_id=1, source_target_pairs={{3,0},{0,1},{1,2},{2,3},{7,4},{4,5},{5,6},{6,7},{11,8},{8,9},{9,10... | collective-permute-start | bytes 1572872 | tf_op jit(solution)/shard_map/ppermute | solution.py:193
  15.7 4.5 %collective-permute-start.1 = (bf16[2048,128]{1,0:T(8,128)(2,1)}, bf16[2048,128]{1,0:T(8,128)(2,1)S(1)}, u32[]{:S(2)}, u32[]{:S(2)}) collective-permute-start(bf16[2048,128]{1,0:T(8,128)(2,1)} %bitcast.15), channel_id=1, source_target_pairs={{4,0},{8,4},{12,8},{0,12},{5,1},{9,5},{13,9},{1,13},{6,2},{10,6},{... | collective-permute-start | bytes 1572872 | tf_op jit(solution)/shard_map/ppermute | solution.py:193
  20.2 0.0 collective-permute-done.5.y2
  20.2 1.9 %collective-permute-start = (bf16[2048,128]{1,0:T(8,128)(2,1)}, bf16[2048,128]{1,0:T(8,128)(2,1)}, u32[]{:S(2)}, u32[]{:S(2)}) collective-permute-start(bf16[2048,128]{1,0:T(8,128)(2,1)} %bitcast.16), channel_id=1, source_target_pairs={{1,0},{2,1},{3,2},{0,3},{5,4},{6,5},{7,6},{4,7},{9,8},{10,9},{11,1... | collective-permute-start | bytes 1572872 | tf_op jit(solution)/shard_map/ppermute | solution.py:193
  22.1 0.0 copy-start.2
  22.1 0.0 copy-start.3
  22.1 0.0 copy-start.4
  22.1 0.6 copy-done.2
  22.8 0.0 copy-done.3
  22.8 0.0 copy-done.4
  22.8 0.0 copy-start
  22.8 1.0 %copy-done = bf16[256,8,128]{2,1,0:T(8,128)(2,1)S(1)} copy-done((bf16[256,8,128]{2,1,0:T(8,128)(2,1)S(1)}, bf16[256,8,128]{2,1,0:T(8,128)(2,1)}, u32[]{:S(2)}) %copy-start) | copy-done | bytes 524312
  23.8 1.5 %project.1 = f32[16,40,128]{2,1,0:T(8,128)} custom-call(bf16[2048,128]{1,0:T(8,128)(2,1)S(1)} %bitcast.17, f32[1,128]{1,0:T(1,128)S(1)} %bitcast.20, f32[1,128]{1,0:T(1,128)S(1)} %bitcast.22, f32[3]{0:T(128)S(1)} %copy-done.2), custom_call_target="tpu_custom_call" | custom-call | flops 10000000 | bytes 1000000 | tf_op jit(solution)/shard_map/project/pallas_call | solution.py:205
  25.4 0.0 copy-start.1
  25.4 7.0 %all-to-all-start = ((f32[16,40,128]{2,1,0:T(8,128)}), f32[16,40,128]{2,1,0:T(8,128)S(1)}, u32[]{:S(2)}, u32[]{:S(2)}) async-start(f32[16,40,128]{2,1,0:T(8,128)} %project.1), calls=%async_computation | async-start | bytes 655360 | tf_op jit(solution)/shard_map/all_to_all | solution.py:197
  32.4 0.0 copy-start.6
  32.4 0.7 copy-done.6
  33.1 0.1 broadcast_in_dim.16
  33.1 0.1 copy.13
  33.2 0.6 broadcast_bitcast_fusion
  33.8 0.0 copy-start.5
  33.9 0.9 copy.14.counts_ref
  34.8 0.0 copy-done.5
  34.8 0.8 copy.12
  35.6 1.0 %reshape.15.nominal_ref = f32[16,128]{1,0:T(8,128)S(1)} reshape(f32[256,8]{1,0:T(8,128)} %copy.12) | data formatting | bytes 16384 | tf_op jit(solution)/shard_map/reshape | solution.py:216
  36.6 0.1 stack.23.pos_ref
  36.7 3.3 %all-to-all-done.got_ref = f32[16,40,128]{2,1,0:T(8,128)S(1)} async-done(((f32[16,40,128]{2,1,0:T(8,128)}), f32[16,40,128]{2,1,0:T(8,128)S(1)}, u32[]{:S(2)}, u32[]{:S(2)}) %all-to-all-start) | async-done | bytes 327712 | tf_op jit(solution)/shard_map/all_to_all | solution.py:197
  40.0 0.0 copy-done.1
  40.0 1.0 %weights.1 = (f32[3,16,128]{2,1,0:T(8,128)S(1)}, bf16[16,128]{1,0:T(8,128)(2,1)S(1)}, f32[8,128]{1,0:T(8,128)S(1)}) custom-call(f32[16,40,128]{2,1,0:T(8,128)S(1)} %all-to-all-done.got_ref, f32[16,128]{1,0:T(8,128)S(1)} %reshape.15.nominal_ref, f32[16,128]{1,0:T(8,128)S(1)} %copy.14.counts_ref, f32[3]{0:T(128)S(1)} %copy-done.2, bf16[2048,128]{1,0:T(8,128)(2,1)S(1)} %bitcast.18), custom_call_target="tpu_custom_call" | custom-call | flops 10000000 | bytes 1000000 | tf_op jit(solution)/shard_map/weights/pallas_call | solution.py:218
  41.0 0.0 collective-permute-done.4.x2
  41.0 0.0 collective-permute-done.3.y3
  41.1 0.0 collective-permute-done.2.x3
  41.1 0.0 collective-permute-done.1.y1
  41.1 0.0 collective-permute-done.x1
  41.1 5.6 %hessian.1 = (f32[1024,128]{1,0:T(8,128)S(1)}, bf16[1040,128]{1,0:T(8,128)(2,1)S(1)}) custom-call(s32[5]{0:T(128)S(1)} %stack.23.pos_ref, f32[3,16,128]{2,1,0:T(8,128)S(1)} %get-tuple-element.11.w_ref, bf16[16,128]{1,0:T(8,128)(2,1)S(1)} %get-tuple-element.12.extra_ref, bf16[2048,128]{1,0:T(8,128)(2,1)S(1)} %bitcast.19, ...), custom_call_target="tpu_custom_call" | custom-call | flops 2000000000 | bytes 5000000 | tf_op jit(solution)/shard_map/hessian/pallas_call | solution.py:233
  46.7 1.9 %collective-permute-start.6 = (bf16[1040,128]{1,0:T(8,128)(2,1)S(1)}, bf16[1040,128]{1,0:T(8,128)(2,1)S(1)}, u32[]{:S(2)}, u32[]{:S(2)}) collective-permute-start(bf16[1040,128]{1,0:T(8,128)(2,1)S(1)} %get-tuple-element.14), channel_id=1, source_target_pairs={{0,16},{16,0},{1,17},{17,1},{2,18},{18,2},{3,19},{19,3},{4,20},{20... | collective-permute-start | bytes 798728 | tf_op jit(solution)/shard_map/ppermute | solution.py:248
  48.7 1.5 %collective-permute-done.6.got_ref = bf16[1040,128]{1,0:T(8,128)(2,1)S(1)} collective-permute-done((bf16[1040,128]{1,0:T(8,128)(2,1)S(1)}, bf16[1040,128]{1,0:T(8,128)(2,1)S(1)}, u32[]{:S(2)}, u32[]{:S(2)}) %collective-permute-start.6) | collective-permute-done | bytes 266272 | tf_op jit(solution)/shard_map/ppermute | solution.py:248
  50.2 0.1 pair.1
  50.2 18.3 %all_to_all.15.got_ref = bf16[16,80,128]{2,1,0:T(8,128)(2,1)S(1)} all-to-all(bf16[16,80,128]{2,1,0:T(8,128)(2,1)S(1)} %pair.1), channel_id=1, replica_groups=mesh['zh'=4,'zl'=4,'core'=2,'y'=4,'x'=4] {'zl','y'}, dimensions={0} | all-to-all | bytes 655360 | tf_op jit(solution)/shard_map/all_to_all | solution.py:197
  68.5 0.6 plane.1
  69.1 26.5 %all_to_all.16.got_ref = bf16[4,80,128]{2,1,0:T(8,128)(2,1)S(1)} all-to-all(bf16[4,80,128]{2,1,0:T(8,128)(2,1)S(1)} %plane.1), channel_id=1, replica_groups=mesh['zh'=4,'zl'=4,'core'=2,'y'=4,'x'=4] {'zh'}, dimensions={0} | all-to-all | bytes 163840 | tf_op jit(solution)/shard_map/all_to_all | solution.py:197
  95.6 1.2 %finish.1 = (f32[3]{0:T(128)}, f32[1,128]{1,0:T(1,128)}, f32[64,128]{1,0:T(8,128)}) custom-call(s32[5]{0:T(128)S(1)} %stack.23.pos_ref, bf16[4,80,128]{2,1,0:T(8,128)(2,1)S(1)} %all_to_all.16.got_ref, f32[8,128]{1,0:T(8,128)S(1)} %get-tuple-element.15.sq_ref, f32[1,128]{1,0:T(1,128)S(1)} %bitcast.21), custom_call_target="tpu_custom_call" | custom-call | flops 1000000 | bytes 1000000 | tf_op jit(solution)/shard_map/finish/pallas_call | solution.py:267
  (1 shorter events, 0.0 us)
Async XLA Ops:
  0.6 19.5 %collective-permute-start.5 = (bf16[2048,128]{1,0:T(8,128)(2,1)}, bf16[2048,128]{1,0:T(8,128)(2,1)S(1)}, u32[]{:S(2)}, u32[]{:S(2)}) collective-permute-start(bf16[2048,128]{1,0:T(8,128)(2,1)} %bitcast.11), channel_id=1, source_target_pairs={{8,0},{12,4},{0,8},{4,12},{9,1},{13,5},{1,9},{5,13},{10,2},{14,6},... | collective-permute-start | bytes 1572872 | tf_op jit(solution)/shard_map/ppermute | solution.py:193
  5.7 35.3 %collective-permute-start.4 = (bf16[2048,128]{1,0:T(8,128)(2,1)}, bf16[2048,128]{1,0:T(8,128)(2,1)S(1)}, u32[]{:S(2)}, u32[]{:S(2)}) collective-permute-start(bf16[2048,128]{1,0:T(8,128)(2,1)} %bitcast.12), channel_id=1, source_target_pairs={{2,0},{3,1},{0,2},{1,3},{6,4},{7,5},{4,6},{5,7},{10,8},{11,9},{8,1... | collective-permute-start | bytes 1572872 | tf_op jit(solution)/shard_map/ppermute | solution.py:193
  9.1 32.0 %collective-permute-start.3 = (bf16[2048,128]{1,0:T(8,128)(2,1)}, bf16[2048,128]{1,0:T(8,128)(2,1)S(1)}, u32[]{:S(2)}, u32[]{:S(2)}) collective-permute-start(bf16[2048,128]{1,0:T(8,128)(2,1)} %bitcast.13), channel_id=1, source_target_pairs={{12,0},{0,4},{4,8},{8,12},{13,1},{1,5},{5,9},{9,13},{14,2},{2,6},{... | collective-permute-start | bytes 1572872 | tf_op jit(solution)/shard_map/ppermute | solution.py:193
  11.7 29.4 %collective-permute-start.2 = (bf16[2048,128]{1,0:T(8,128)(2,1)}, bf16[2048,128]{1,0:T(8,128)(2,1)S(1)}, u32[]{:S(2)}, u32[]{:S(2)}) collective-permute-start(bf16[2048,128]{1,0:T(8,128)(2,1)} %bitcast.14), channel_id=1, source_target_pairs={{3,0},{0,1},{1,2},{2,3},{7,4},{4,5},{5,6},{6,7},{11,8},{8,9},{9,10... | collective-permute-start | bytes 1572872 | tf_op jit(solution)/shard_map/ppermute | solution.py:193
  15.7 25.4 %collective-permute-start.1 = (bf16[2048,128]{1,0:T(8,128)(2,1)}, bf16[2048,128]{1,0:T(8,128)(2,1)S(1)}, u32[]{:S(2)}, u32[]{:S(2)}) collective-permute-start(bf16[2048,128]{1,0:T(8,128)(2,1)} %bitcast.15), channel_id=1, source_target_pairs={{4,0},{8,4},{12,8},{0,12},{5,1},{9,5},{13,9},{1,13},{6,2},{10,6},{... | collective-permute-start | bytes 1572872 | tf_op jit(solution)/shard_map/ppermute | solution.py:193
  20.2 20.9 %collective-permute-start = (bf16[2048,128]{1,0:T(8,128)(2,1)}, bf16[2048,128]{1,0:T(8,128)(2,1)}, u32[]{:S(2)}, u32[]{:S(2)}) collective-permute-start(bf16[2048,128]{1,0:T(8,128)(2,1)} %bitcast.16), channel_id=1, source_target_pairs={{1,0},{2,1},{3,2},{0,3},{5,4},{6,5},{7,6},{4,7},{9,8},{10,9},{11,1... | collective-permute-start | bytes 1572872 | tf_op jit(solution)/shard_map/ppermute | solution.py:193
  22.1 0.7 copy-start.2
  22.1 0.7 copy-start.3
  22.1 0.7 copy-start.4
  22.8 1.0 %copy-start = (bf16[256,8,128]{2,1,0:T(8,128)(2,1)S(1)}, bf16[256,8,128]{2,1,0:T(8,128)(2,1)}, u32[]{:S(2)}) copy-start(bf16[256,8,128]{2,1,0:T(8,128)(2,1)} %param.7) | copy-start | bytes 1572868
  25.4 14.6 %copy-start.1 = (bf16[256,8,128]{2,1,0:T(8,128)(2,1)S(1)}, bf16[256,8,128]{2,1,0:T(8,128)(2,1)}, u32[]{:S(2)}) copy-start(bf16[256,8,128]{2,1,0:T(8,128)(2,1)} %param.7) | copy-start | bytes 1572868
  25.4 14.6 %all-to-all-start = ((f32[16,40,128]{2,1,0:T(8,128)}), f32[16,40,128]{2,1,0:T(8,128)S(1)}, u32[]{:S(2)}, u32[]{:S(2)}) async-start(f32[16,40,128]{2,1,0:T(8,128)} %project.1), calls=%async_computation | async-start | bytes 655360 | tf_op jit(solution)/shard_map/all_to_all | solution.py:197
  32.4 0.7 copy-start.6
  33.8 0.9 copy-start.5
  46.7 3.4 %collective-permute-start.6 = (bf16[1040,128]{1,0:T(8,128)(2,1)S(1)}, bf16[1040,128]{1,0:T(8,128)(2,1)S(1)}, u32[]{:S(2)}, u32[]{:S(2)}) collective-permute-start(bf16[1040,128]{1,0:T(8,128)(2,1)S(1)} %get-tuple-element.14), channel_id=1, source_target_pairs={{0,16},{16,0},{1,17},{17,1},{2,18},{18,2},{3,19},{19,3},{4,20},{20... | collective-permute-start | bytes 798728 | tf_op jit(solution)/shard_map/ppermute | solution.py:248

commit v2 on v1

--- a/solution.py
+++ b/solution.py
@@ -79,13 +79,30 @@
     return x
 
 
+def by_row(nominal, counts, lane):
+    place = lax.broadcasted_iota(jnp.int32, (CHUNKS, BINS_DEV), 1)
+    line = lax.broadcasted_iota(jnp.int32, (CHUNKS, BINS_DEV), 0)
+    mine = place // CHUNKS == line
+    each = [nominal[p : p + 1] for p in range(PROC)] + [counts]
+    spread = jnp.concatenate([jnp.where(mine, row, 0.0) for row in each], 0)
+    source = lax.broadcasted_iota(jnp.int32, (BINS_DEV, LANES), 0) % CHUNKS
+    target = lax.broadcasted_iota(jnp.int32, (BINS_DEV, LANES), 1) // PROC
+    pick = (source == target).astype(F32).astype(BF16)
+    high, middle, low = (rows_dot(part, pick) for part in thirds(spread))
+    moved = high + middle + low
+    out = jnp.zeros((CHUNKS, LANES), F32)
+    for p in range(PROC):
+        out = jnp.where(lane % PROC == p, moved[p * CHUNKS : (p + 1) * CHUNKS], out)
+    return out, moved[PROC * CHUNKS :]
+
+
 def weights_kernel(got_ref, nominal_ref, counts_ref, steps_ref, v_ref, w_ref, bins_ref, sq_ref):
     total = jnp.sum(got_ref[...], axis=0)
     along_start = total[0:CHUNKS]
     along_dir = total[CHUNKS : 2 * CHUNKS]
     sq_ref[...] = total[2 * CHUNKS : 2 * CHUNKS + 8]
-    nominal, counts = nominal_ref[...], counts_ref[...]
     lane = lax.broadcasted_iota(jnp.int32, (CHUNKS, LANES), 1)
+    nominal, counts = by_row(nominal_ref[...], counts_ref[...].astype(F32), lane)
     base = jnp.exp(nominal + along_start)
     base_total = lane_groups_sum(base, lane)
     base_log = jnp.log(base_total)
@@ -109,43 +126,56 @@
 
 
 def hessian_kernel(
-    pos_ref, w_ref, extra_ref, own, x1, y1, x3, y3, x2, y2, kept_ref, sent_ref, rights, lefts
+    pos_ref, w_ref, extra_ref, own, x1, y1, x3, y3, x2, y2, kept_ref, sent_ref,
+    right_t, left, jac_rows,
 ):
     px, py, core = pos_ref[0], pos_ref[1], pos_ref[4]
     mine = lax.broadcasted_iota(jnp.int32, (16, LANES), 1) // PROC
     mine = mine == lax.broadcasted_iota(jnp.int32, (16, LANES), 0)
-    columns = w_ref[1].T
-    for c in range(CHUNKS):
-        span = slice(c * LANES, (c + 1) * LANES)
-        jac_span = slice(ROWS + c * 16, ROWS + (c + 1) * 16)
-        both = []
-        for k in (0, 2):
-            spread = jnp.where(mine, w_ref[k, c : c + 1, :], 0.0)
-            both.append(jnp.concatenate(thirds(spread), 0))
-        scale = columns[:, c : c + 1]
-        for step, ref in enumerate((own, x1, x2, x3)):
+
+    def spot(at):
+        return pl.ds(pl.multiple_of(at * LANES, LANES), LANES)
+
+    def chunk(c, carry):
+        span = spot(c)
+        jac_span = pl.ds(pl.multiple_of(ROWS + c * 16, 16), 16)
+
+        def spread(k):
+            return jnp.concatenate(thirds(jnp.where(mine, w_ref[k, pl.ds(c, 1), :], 0.0)), 0)
+
+        def summed(jac):
+            return (jac[0:16] + jac[16:32] + jac[32:48]).astype(BF16)
+
+        across = [ref[span, :] for ref in (own, x1, x2, x3)]
+        jac = summed(rows_dot(spread(0), jnp.concatenate(across, 1)))
+        for step, rows in enumerate(across):
             at = lax.rem(px + step, SIDE)
-            rows = ref[span, :]
-            rights[at, span, :] = rows
-            jac = rows_dot(both[0], rows)
-            rights[at, jac_span, :] = (jac[0:16] + jac[16:32] + jac[32:48]).astype(BF16)
-        for step, ref in enumerate((own, y1, y2, y3)):
-            at = lax.rem(py + step, SIDE)
-            rows = ref[span, :]
-            lefts[at, span, :] = (scale * rows.astype(F32)).astype(BF16)
-            jac = rows_dot(both[1], rows)
-            lefts[at, jac_span, :] = (jac[0:16] + jac[16:32] + jac[32:48]).astype(BF16)
-    right = jnp.concatenate([rights[k] for k in range(SIDE)], 1)
-    for j in range(SIDE):
-        term = lax.dot_general(
-            right, lefts[j], (((0,), (0,)), ((), ())), preferred_element_type=F32
-        )
+            right_t[spot(at), span] = rows.T
+            jac_at = pl.ds(pl.multiple_of(at * BINS_DEV + c * 16, 16), 16)
+            jac_rows[jac_at, :] = jac[:, step * LANES : (step + 1) * LANES]
+        down = [ref[span, :] for ref in (own, y1, y2, y3)]
+        jac = summed(rows_dot(spread(2), jnp.concatenate(down, 1)))
+        scale = jnp.broadcast_to(w_ref[1, pl.ds(c, 1), :], (LANES, LANES)).T
+        for step, rows in enumerate(down):
+            at = spot(lax.rem(py + step, SIDE))
+            left[span, at] = (scale * rows.astype(F32)).astype(BF16)
+            left[jac_span, at] = jac[:, step * LANES : (step + 1) * LANES]
+        return carry
+
+    lax.fori_loop(0, CHUNKS, chunk, 0, unroll=2)
+    for i in range(SIDE):
+        rows = jac_rows[i * BINS_DEV : (i + 1) * BINS_DEV, :]
+        right_t[i * LANES : (i + 1) * LANES, ROWS:] = rows.T
+    for n in range(2):
+        term = rows_dot(right_t[...], left[:, n * 2 * LANES : (n + 1) * 2 * LANES])
         for i in range(SIDE):
-            first = term[i * LANES : i * LANES + 64]
-            second = term[i * LANES + 64 : (i + 1) * LANES]
-            at = (i * SIDE + j) * 64
-            kept_ref[at : at + 64, :] = jnp.where(core == 0, first, second)
-            sent_ref[at : at + 64, :] = jnp.where(core == 0, second, first).astype(BF16)
+            for half in range(2):
+                part = term[:, half * LANES : (half + 1) * LANES]
+                first = part[i * LANES : i * LANES + 64]
+                second = part[i * LANES + 64 : (i + 1) * LANES]
+                at = (i * SIDE + 2 * n + half) * 64
+                kept_ref[at : at + 64, :] = jnp.where(core == 0, first, second)
+                sent_ref[at : at + 64, :] = jnp.where(core == 0, second, first).astype(BF16)
     sent_ref[PIECES * 64 :, :] = extra_ref[...]
 
 
@@ -213,8 +243,6 @@
         name="project",
     )(own, start[None, :], direction[None, :], step_lengths)
     got = exchanged(sent, ("y", "x"))
-    nominal = log_nominal.reshape(CHUNKS, LANES)
-    counts = jnp.repeat(observed.astype(F32), PROC).reshape(CHUNKS, LANES)
     weights, extra, squares = pl.pallas_call(
         weights_kernel,
         out_shape=arrays_of(
@@ -225,7 +253,7 @@
         compiler_params=PARAMS,
         cost_estimate=cost(10_000_000, 1_000_000),
         name="weights",
-    )(got, nominal, counts, step_lengths, own)
+    )(got, log_nominal.T, observed[None, :], step_lengths, own)
     px, py = lax.axis_index("x"), lax.axis_index("y")
     core = lax.axis_index("core")
     block = lax.axis_index(("zh", "zl", "core"))
@@ -238,8 +266,9 @@
         in_specs=[SMEM] + [VMEM] * 9,
         out_specs=(VMEM, VMEM),
         scratch_shapes=[
-            pltpu.VMEM((SIDE, DEPTH, LANES), BF16),
-            pltpu.VMEM((SIDE, DEPTH, LANES), BF16),
+            pltpu.VMEM((SIDE * LANES, DEPTH), BF16),
+            pltpu.VMEM((DEPTH, SIDE * LANES), BF16),
+            pltpu.VMEM((SIDE * BINS_DEV, LANES), BF16),
         ],
         compiler_params=PARAMS,
         cost_estimate=cost(2_000_000_000, 5_000_000),

time: 97.4 us -> 97.1 us (level)
  waiting for transfers between devices: 4.83 us -> 9.04 us
  local copies, waits for them, and re-layouts: 5.97 us -> 2.47 us
  Pallas kernels: 10.1 us -> 9.11 us
    all_to_all x1, waiting for transfers between devices: 3.31 us -> 7.52 us  [exchanged(): return lax.all_to_all(array, axes, 0, 0, tiled=True)]
    broadcast_in_dim x4 -> x0, local copies, waits for them, and re-layouts: 1.69 us -> none  [body(): counts = jnp.repeat(observed.astype(F32), PROC).reshape(CHUNKS, LANES)]
    pallas_call x1, Pallas kernels: 5.64 us -> 4.39 us  [body(): pl.pallas_call(hessian_kernel, out_shape=arrays_of(((PIECES * 64, LANES),...]
    reshape x1 -> x0, local copies, waits for them, and re-layouts: 1.01 us -> none  [body(): nominal = log_nominal.reshape(CHUNKS, LANES)]
    unnamed x15 -> x14, local copies, waits for them, and re-layouts: 3.19 us -> 2.39 us
  transfers between devices with their start and end apart: 8 -> 8, of which waited for: 2 -> 2; matrix products, arithmetic and copies ran while one was open for 4% -> 0% of each run, Pallas kernels for 3% -> 3%
where the time goes in v2:
time: 97.1 us; the launch traced here: 96.5 us
  blocking collectives  44.8 us (46%)
  starting transfers between devices  30.3 us (31%)
  Pallas kernels  9.11 us (9%)
  waiting for transfers between devices  9.04 us (9%)
  local copies, waits for them, and re-layouts  2.47 us (3%)
    all_to_all x2, blocking collectives, exchanged(): return lax.all_to_all(array, axes, 0, 0, tiled=True)  44.8 us
    ppermute x6, starting transfers between devices, from_ahead(): lax.ppermute(array, axis, [((i + step) % SIDE, i) for i in range(SIDE)])  21.4 us
    all_to_all x1, waiting for transfers between devices, exchanged(): return lax.all_to_all(array, axes, 0, 0, tiled=True)  7.52 us
    all_to_all x1, starting transfers between devices, exchanged(): return lax.all_to_all(array, axes, 0, 0, tiled=True)  7.01 us
    pallas_call x1, Pallas kernels, body(): pl.pallas_call(hessian_kernel, out_shape=arrays_of(((PIECES * 64, LANES),...  4.39 us
    unnamed x14, local copies, waits for them, and re-layouts  2.39 us
  transfers between devices with their start and end apart: 8, of which 2 were waited for; matrix products, arithmetic and copies ran while one was open for 0% of the time, Pallas kernels for 3%

profile of v2, /device:TPU:38, one launch (start us, length us, event | category | flops | bytes accessed | tf_op | source)
XLA Modules:
  0.0 96.5 jit_solution(4248392199375839166)
XLA Ops:
  0.6 5.1 %collective-permute-start.5 = (bf16[2048,128]{1,0:T(8,128)(2,1)}, bf16[2048,128]{1,0:T(8,128)(2,1)S(1)}, u32[]{:S(2)}, u32[]{:S(2)}) collective-permute-start(bf16[2048,128]{1,0:T(8,128)(2,1)} %bitcast.11), channel_id=1, source_target_pairs={{8,0},{12,4},{0,8},{4,12},{9,1},{13,5},{1,9},{5,13},{10,2},{14,6},... | collective-permute-start | bytes 1572872 | tf_op jit(solution)/shard_map/ppermute | solution.py:223
  5.7 3.3 %collective-permute-start.4 = (bf16[2048,128]{1,0:T(8,128)(2,1)}, bf16[2048,128]{1,0:T(8,128)(2,1)S(1)}, u32[]{:S(2)}, u32[]{:S(2)}) collective-permute-start(bf16[2048,128]{1,0:T(8,128)(2,1)} %bitcast.12), channel_id=1, source_target_pairs={{2,0},{3,1},{0,2},{1,3},{6,4},{7,5},{4,6},{5,7},{10,8},{11,9},{8,1... | collective-permute-start | bytes 1572872 | tf_op jit(solution)/shard_map/ppermute | solution.py:223
  9.1 2.6 %collective-permute-start.3 = (bf16[2048,128]{1,0:T(8,128)(2,1)}, bf16[2048,128]{1,0:T(8,128)(2,1)S(1)}, u32[]{:S(2)}, u32[]{:S(2)}) collective-permute-start(bf16[2048,128]{1,0:T(8,128)(2,1)} %bitcast.13), channel_id=1, source_target_pairs={{12,0},{0,4},{4,8},{8,12},{13,1},{1,5},{5,9},{9,13},{14,2},{2,6},{... | collective-permute-start | bytes 1572872 | tf_op jit(solution)/shard_map/ppermute | solution.py:223
  11.7 4.0 %collective-permute-start.2 = (bf16[2048,128]{1,0:T(8,128)(2,1)}, bf16[2048,128]{1,0:T(8,128)(2,1)S(1)}, u32[]{:S(2)}, u32[]{:S(2)}) collective-permute-start(bf16[2048,128]{1,0:T(8,128)(2,1)} %bitcast.14), channel_id=1, source_target_pairs={{3,0},{0,1},{1,2},{2,3},{7,4},{4,5},{5,6},{6,7},{11,8},{8,9},{9,10... | collective-permute-start | bytes 1572872 | tf_op jit(solution)/shard_map/ppermute | solution.py:223
  15.7 4.5 %collective-permute-start.1 = (bf16[2048,128]{1,0:T(8,128)(2,1)}, bf16[2048,128]{1,0:T(8,128)(2,1)S(1)}, u32[]{:S(2)}, u32[]{:S(2)}) collective-permute-start(bf16[2048,128]{1,0:T(8,128)(2,1)} %bitcast.15), channel_id=1, source_target_pairs={{4,0},{8,4},{12,8},{0,12},{5,1},{9,5},{13,9},{1,13},{6,2},{10,6},{... | collective-permute-start | bytes 1572872 | tf_op jit(solution)/shard_map/ppermute | solution.py:223
  20.2 0.0 collective-permute-done.5.y2
  20.2 1.9 %collective-permute-start = (bf16[2048,128]{1,0:T(8,128)(2,1)}, bf16[2048,128]{1,0:T(8,128)(2,1)}, u32[]{:S(2)}, u32[]{:S(2)}) collective-permute-start(bf16[2048,128]{1,0:T(8,128)(2,1)} %bitcast.16), channel_id=1, source_target_pairs={{1,0},{2,1},{3,2},{0,3},{5,4},{6,5},{7,6},{4,7},{9,8},{10,9},{11,1... | collective-permute-start | bytes 1572872 | tf_op jit(solution)/shard_map/ppermute | solution.py:223
  22.1 0.0 copy-start.3
  22.1 0.0 copy-start.4
  22.1 0.0 copy-start.6
  22.1 0.6 copy-done.3
  22.8 0.0 copy-done.4
  22.8 0.0 copy-done.6
  22.8 0.0 copy-start
  22.8 1.0 %copy-done = bf16[256,8,128]{2,1,0:T(8,128)(2,1)S(1)} copy-done((bf16[256,8,128]{2,1,0:T(8,128)(2,1)S(1)}, bf16[256,8,128]{2,1,0:T(8,128)(2,1)}, u32[]{:S(2)}) %copy-start) | copy-done | bytes 524312
  23.8 1.5 %project.1 = f32[16,40,128]{2,1,0:T(8,128)} custom-call(bf16[2048,128]{1,0:T(8,128)(2,1)S(1)} %bitcast.17, f32[1,128]{1,0:T(1,128)S(1)} %bitcast.21, f32[1,128]{1,0:T(1,128)S(1)} %bitcast.24, f32[3]{0:T(128)S(1)} %copy-done.3), custom_call_target="tpu_custom_call" | custom-call | flops 10000000 | bytes 1000000 | tf_op jit(solution)/shard_map/project/pallas_call | solution.py:235
  25.4 0.0 copy-start.1
  25.4 7.0 %all-to-all-start = ((f32[16,40,128]{2,1,0:T(8,128)}), f32[16,40,128]{2,1,0:T(8,128)S(1)}, u32[]{:S(2)}, u32[]{:S(2)}) async-start(f32[16,40,128]{2,1,0:T(8,128)} %project.1), calls=%async_computation | async-start | bytes 655360 | tf_op jit(solution)/shard_map/all_to_all | solution.py:227
  32.4 0.0 copy-start.2
  32.4 0.1 stack.23.pos_ref
  32.5 7.5 %all-to-all-done.got_ref = f32[16,40,128]{2,1,0:T(8,128)S(1)} async-done(((f32[16,40,128]{2,1,0:T(8,128)}), f32[16,40,128]{2,1,0:T(8,128)S(1)}, u32[]{:S(2)}, u32[]{:S(2)}) %all-to-all-start) | async-done | bytes 327712 | tf_op jit(solution)/shard_map/all_to_all | solution.py:227
  40.0 0.0 copy-start.5
  40.0 0.0 copy-done.1
  40.0 0.0 copy-done.2
  40.0 0.7 copy-done.5
  40.7 1.3 %weights.1 = (f32[3,16,128]{2,1,0:T(8,128)S(1)}, bf16[16,128]{1,0:T(8,128)(2,1)S(1)}, f32[8,128]{1,0:T(8,128)S(1)}) custom-call(f32[16,40,128]{2,1,0:T(8,128)S(1)} %all-to-all-done.got_ref, f32[8,256]{1,0:T(8,128)S(1)} %bitcast.20, s32[1,256]{1,0:T(1,128)S(1)} %bitcast.23, f32[3]{0:T(128)S(1)} %copy-done.3, bf16[2048,128]{1,0:T(8,128)(2,1)S(1)} %bitcast.18), custom_call_target="tpu_custom_call" | custom-call | flops 10000000 | bytes 1000000 | tf_op jit(solution)/shard_map/weights/pallas_call | solution.py:246
  42.0 0.0 collective-permute-done.4.x2
  42.0 0.0 collective-permute-done.3.y3
  42.0 0.0 collective-permute-done.2.x3
  42.0 0.0 collective-permute-done.1.y1
  42.1 0.0 collective-permute-done.x1
  42.1 4.4 %hessian.1 = (f32[1024,128]{1,0:T(8,128)S(1)}, bf16[1040,128]{1,0:T(8,128)(2,1)S(1)}) custom-call(s32[5]{0:T(128)S(1)} %stack.23.pos_ref, f32[3,16,128]{2,1,0:T(8,128)S(1)} %get-tuple-element.11.w_ref, bf16[16,128]{1,0:T(8,128)(2,1)S(1)} %get-tuple-element.12.extra_ref, bf16[2048,128]{1,0:T(8,128)(2,1)S(1)} %bitcast.19, ...), custom_call_target="tpu_custom_call" | custom-call | flops 2000000000 | bytes 5000000 | tf_op jit(solution)/shard_map/hessian/pallas_call | solution.py:261
  46.5 1.9 %collective-permute-start.6 = (bf16[1040,128]{1,0:T(8,128)(2,1)S(1)}, bf16[1040,128]{1,0:T(8,128)(2,1)S(1)}, u32[]{:S(2)}, u32[]{:S(2)}) collective-permute-start(bf16[1040,128]{1,0:T(8,128)(2,1)S(1)} %get-tuple-element.14), channel_id=1, source_target_pairs={{0,16},{16,0},{1,17},{17,1},{2,18},{18,2},{3,19},{19,3},{4,20},{20... | collective-permute-start | bytes 798728 | tf_op jit(solution)/shard_map/ppermute | solution.py:277
  48.4 1.5 %collective-permute-done.6.got_ref = bf16[1040,128]{1,0:T(8,128)(2,1)S(1)} collective-permute-done((bf16[1040,128]{1,0:T(8,128)(2,1)S(1)}, bf16[1040,128]{1,0:T(8,128)(2,1)S(1)}, u32[]{:S(2)}, u32[]{:S(2)}) %collective-permute-start.6) | collective-permute-done | bytes 266272 | tf_op jit(solution)/shard_map/ppermute | solution.py:277
  49.9 0.1 pair.1
  50.0 18.3 %all_to_all.15.got_ref = bf16[16,80,128]{2,1,0:T(8,128)(2,1)S(1)} all-to-all(bf16[16,80,128]{2,1,0:T(8,128)(2,1)S(1)} %pair.1), channel_id=1, replica_groups=mesh['zh'=4,'zl'=4,'core'=2,'y'=4,'x'=4] {'zl','y'}, dimensions={0} | all-to-all | bytes 655360 | tf_op jit(solution)/shard_map/all_to_all | solution.py:227
  68.2 0.6 plane.1
  68.8 26.5 %all_to_all.16.got_ref = bf16[4,80,128]{2,1,0:T(8,128)(2,1)S(1)} all-to-all(bf16[4,80,128]{2,1,0:T(8,128)(2,1)S(1)} %plane.1), channel_id=1, replica_groups=mesh['zh'=4,'zl'=4,'core'=2,'y'=4,'x'=4] {'zh'}, dimensions={0} | all-to-all | bytes 163840 | tf_op jit(solution)/shard_map/all_to_all | solution.py:227
  95.3 1.2 %finish.1 = (f32[3]{0:T(128)}, f32[1,128]{1,0:T(1,128)}, f32[64,128]{1,0:T(8,128)}) custom-call(s32[5]{0:T(128)S(1)} %stack.23.pos_ref, bf16[4,80,128]{2,1,0:T(8,128)(2,1)S(1)} %all_to_all.16.got_ref, f32[8,128]{1,0:T(8,128)S(1)} %get-tuple-element.15.sq_ref, f32[1,128]{1,0:T(1,128)S(1)} %bitcast.22), custom_call_target="tpu_custom_call" | custom-call | flops 1000000 | bytes 1000000 | tf_op jit(solution)/shard_map/finish/pallas_call | solution.py:296
Async XLA Ops:
  0.6 19.5 %collective-permute-start.5 = (bf16[2048,128]{1,0:T(8,128)(2,1)}, bf16[2048,128]{1,0:T(8,128)(2,1)S(1)}, u32[]{:S(2)}, u32[]{:S(2)}) collective-permute-start(bf16[2048,128]{1,0:T(8,128)(2,1)} %bitcast.11), channel_id=1, source_target_pairs={{8,0},{12,4},{0,8},{4,12},{9,1},{13,5},{1,9},{5,13},{10,2},{14,6},... | collective-permute-start | bytes 1572872 | tf_op jit(solution)/shard_map/ppermute | solution.py:223
  5.7 36.3 %collective-permute-start.4 = (bf16[2048,128]{1,0:T(8,128)(2,1)}, bf16[2048,128]{1,0:T(8,128)(2,1)S(1)}, u32[]{:S(2)}, u32[]{:S(2)}) collective-permute-start(bf16[2048,128]{1,0:T(8,128)(2,1)} %bitcast.12), channel_id=1, source_target_pairs={{2,0},{3,1},{0,2},{1,3},{6,4},{7,5},{4,6},{5,7},{10,8},{11,9},{8,1... | collective-permute-start | bytes 1572872 | tf_op jit(solution)/shard_map/ppermute | solution.py:223
  9.1 33.0 %collective-permute-start.3 = (bf16[2048,128]{1,0:T(8,128)(2,1)}, bf16[2048,128]{1,0:T(8,128)(2,1)S(1)}, u32[]{:S(2)}, u32[]{:S(2)}) collective-permute-start(bf16[2048,128]{1,0:T(8,128)(2,1)} %bitcast.13), channel_id=1, source_target_pairs={{12,0},{0,4},{4,8},{8,12},{13,1},{1,5},{5,9},{9,13},{14,2},{2,6},{... | collective-permute-start | bytes 1572872 | tf_op jit(solution)/shard_map/ppermute | solution.py:223
  11.7 30.4 %collective-permute-start.2 = (bf16[2048,128]{1,0:T(8,128)(2,1)}, bf16[2048,128]{1,0:T(8,128)(2,1)S(1)}, u32[]{:S(2)}, u32[]{:S(2)}) collective-permute-start(bf16[2048,128]{1,0:T(8,128)(2,1)} %bitcast.14), channel_id=1, source_target_pairs={{3,0},{0,1},{1,2},{2,3},{7,4},{4,5},{5,6},{6,7},{11,8},{8,9},{9,10... | collective-permute-start | bytes 1572872 | tf_op jit(solution)/shard_map/ppermute | solution.py:223
  15.7 26.4 %collective-permute-start.1 = (bf16[2048,128]{1,0:T(8,128)(2,1)}, bf16[2048,128]{1,0:T(8,128)(2,1)S(1)}, u32[]{:S(2)}, u32[]{:S(2)}) collective-permute-start(bf16[2048,128]{1,0:T(8,128)(2,1)} %bitcast.15), channel_id=1, source_target_pairs={{4,0},{8,4},{12,8},{0,12},{5,1},{9,5},{13,9},{1,13},{6,2},{10,6},{... | collective-permute-start | bytes 1572872 | tf_op jit(solution)/shard_map/ppermute | solution.py:223
  20.2 21.9 %collective-permute-start = (bf16[2048,128]{1,0:T(8,128)(2,1)}, bf16[2048,128]{1,0:T(8,128)(2,1)}, u32[]{:S(2)}, u32[]{:S(2)}) collective-permute-start(bf16[2048,128]{1,0:T(8,128)(2,1)} %bitcast.16), channel_id=1, source_target_pairs={{1,0},{2,1},{3,2},{0,3},{5,4},{6,5},{7,6},{4,7},{9,8},{10,9},{11,1... | collective-permute-start | bytes 1572872 | tf_op jit(solution)/shard_map/ppermute | solution.py:223
  22.1 0.7 copy-start.3
  22.1 0.7 copy-start.4
  22.1 0.7 copy-start.6
  22.8 1.0 %copy-start = (bf16[256,8,128]{2,1,0:T(8,128)(2,1)S(1)}, bf16[256,8,128]{2,1,0:T(8,128)(2,1)}, u32[]{:S(2)}) copy-start(bf16[256,8,128]{2,1,0:T(8,128)(2,1)} %param.7) | copy-start | bytes 1572868
  25.4 14.6 %copy-start.1 = (bf16[256,8,128]{2,1,0:T(8,128)(2,1)S(1)}, bf16[256,8,128]{2,1,0:T(8,128)(2,1)}, u32[]{:S(2)}) copy-start(bf16[256,8,128]{2,1,0:T(8,128)(2,1)} %param.7) | copy-start | bytes 1572868
  25.4 14.6 %all-to-all-start = ((f32[16,40,128]{2,1,0:T(8,128)}), f32[16,40,128]{2,1,0:T(8,128)S(1)}, u32[]{:S(2)}, u32[]{:S(2)}) async-start(f32[16,40,128]{2,1,0:T(8,128)} %project.1), calls=%async_computation | async-start | bytes 655360 | tf_op jit(solution)/shard_map/all_to_all | solution.py:227
  32.4 7.6 %copy-start.2 = (f32[256,8]{0,1:T(8,128)S(1)}, f32[256,8]{0,1:T(8,128)}, u32[]{:S(2)}) copy-start(f32[256,8]{0,1:T(8,128)} %param.6) | copy-start | bytes 24580
  40.0 0.7 copy-start.5
  46.5 3.4 %collective-permute-start.6 = (bf16[1040,128]{1,0:T(8,128)(2,1)S(1)}, bf16[1040,128]{1,0:T(8,128)(2,1)S(1)}, u32[]{:S(2)}, u32[]{:S(2)}) collective-permute-start(bf16[1040,128]{1,0:T(8,128)(2,1)S(1)} %get-tuple-element.14), channel_id=1, source_target_pairs={{0,16},{16,0},{1,17},{17,1},{2,18},{18,2},{3,19},{19,3},{4,20},{20... | collective-permute-start | bytes 798728 | tf_op jit(solution)/shard_map/ppermute | solution.py:277

commit v3 on v2

--- a/solution.py
+++ b/solution.py
@@ -21,7 +21,7 @@
 DEPTH = ROWS + BINS_DEV
 VMEM = pl.BlockSpec(memory_space=pltpu.VMEM)
 SMEM = pl.BlockSpec(memory_space=pltpu.SMEM)
-PARAMS = pltpu.CompilerParams(vmem_limit_bytes=48 * 1024 * 1024)
+PARAMS = pltpu.CompilerParams(vmem_limit_bytes=16 * 1024 * 1024)
 
 
 def cost(flops, moved):
@@ -49,11 +49,18 @@
     return wide[..., 0:4, :] + wide[..., 4:8, :] + wide[..., 8:12, :]
 
 
-def project_kernel(v_ref, start_ref, dir_ref, steps_ref, out_ref, flat):
-    start, direction = start_ref[...], dir_ref[...]
-    parts = jnp.concatenate(thirds(start) + thirds(direction), 0)
+def pack_kernel(v_ref, start_ref, dir_ref, out_ref):
+    out_ref[0:ROWS, :] = v_ref[...]
+    parts = thirds(start_ref[...]) + thirds(dir_ref[...]) + [jnp.zeros((10, LANES), BF16)]
+    out_ref[ROWS:, :] = jnp.concatenate(parts, 0)
+
+
+def project_kernel(steps_ref, own, x1, x3, x2, out_ref, flat):
+    refs = (own, x1, x2, x3)
+    parts = jnp.concatenate([ref[ROWS:, :] for ref in refs], 1)
+    blocks = jnp.concatenate([ref[0:ROWS, :] for ref in refs], 1)
     six = lax.dot_general(
-        parts, v_ref[...], (((1,), (1,)), ((), ())), preferred_element_type=F32
+        parts, blocks, (((1,), (1,)), ((), ())), preferred_element_type=F32
     )
     along_start = six[0:1] + six[1:2] + six[2:3]
     along_dir = six[3:4] + six[4:5] + six[5:6]
@@ -61,14 +68,30 @@
         span = slice(c * LANES, (c + 1) * LANES)
         flat[c : c + 1, :] = along_start[:, span]
         flat[CHUNKS + c : CHUNKS + c + 1, :] = along_dir[:, span]
-    flat[2 * CHUNKS : 2 * CHUNKS + 8, :] = jnp.zeros((8, LANES), F32)
-    flat[2 * CHUNKS : 2 * CHUNKS + 1, :] = start * start
-    for j in range(3):
-        point = start + steps_ref[j] * direction
-        flat[2 * CHUNKS + 1 + j : 2 * CHUNKS + 2 + j, :] = point * point
+    squares = jnp.zeros((8, LANES), F32)
+    line = lax.broadcasted_iota(jnp.int32, (8, LANES), 0)
+    for ref in refs:
+        wide = ref[ROWS:, :].astype(F32)
+        start = wide[0:1] + wide[1:2] + wide[2:3]
+        direction = wide[3:4] + wide[4:5] + wide[5:6]
+        squares = squares + jnp.where(line == 0, start * start, 0.0)
+        for j in range(3):
+            point = start + steps_ref[j] * direction
+            squares = squares + jnp.where(line == 1 + j, point * point, 0.0)
+    flat[2 * CHUNKS :, :] = squares
     whole = flat[...]
     for i in range(out_ref.shape[0]):
         out_ref[i] = whole
+
+
+def turn_kernel(own, x1, x3, x2, out_ref):
+    def chunk(c, carry):
+        span = pl.ds(pl.multiple_of(c * LANES, LANES), LANES)
+        for step, ref in enumerate((own, x1, x2, x3)):
+            out_ref[step * LANES : (step + 1) * LANES, span] = ref[span, :].T
+        return carry
+
+    lax.fori_loop(0, CHUNKS, chunk, 0, unroll=4)
 
 
 def lane_groups_sum(x, lane):
@@ -126,56 +149,45 @@
 
 
 def hessian_kernel(
-    pos_ref, w_ref, extra_ref, own, x1, y1, x3, y3, x2, y2, kept_ref, sent_ref,
-    right_t, left, jac_rows,
+    pos_ref, w_ref, extra_ref, turned, own, x1, y1, x3, y3, x2, y2, kept_ref, sent_ref,
+    right, jac_rows, jac_cols,
 ):
     px, py, core = pos_ref[0], pos_ref[1], pos_ref[4]
     mine = lax.broadcasted_iota(jnp.int32, (16, LANES), 1) // PROC
     mine = mine == lax.broadcasted_iota(jnp.int32, (16, LANES), 0)
-
-    def spot(at):
-        return pl.ds(pl.multiple_of(at * LANES, LANES), LANES)
+    down = (own, y1, y2, y3)
 
     def chunk(c, carry):
-        span = spot(c)
-        jac_span = pl.ds(pl.multiple_of(ROWS + c * 16, 16), 16)
-
-        def spread(k):
-            return jnp.concatenate(thirds(jnp.where(mine, w_ref[k, pl.ds(c, 1), :], 0.0)), 0)
-
-        def summed(jac):
+        span = pl.ds(pl.multiple_of(c * LANES, LANES), LANES)
+        jac_span = pl.ds(pl.multiple_of(c * 16, 16), 16)
+
+        def jacobian(k, refs):
+            spread = jnp.where(mine, w_ref[k, pl.ds(c, 1), :], 0.0)
+            blocks = jnp.concatenate([ref[span, :] for ref in refs], 1)
+            jac = rows_dot(jnp.concatenate(thirds(spread), 0), blocks)
             return (jac[0:16] + jac[16:32] + jac[32:48]).astype(BF16)
 
-        across = [ref[span, :] for ref in (own, x1, x2, x3)]
-        jac = summed(rows_dot(spread(0), jnp.concatenate(across, 1)))
-        for step, rows in enumerate(across):
-            at = lax.rem(px + step, SIDE)
-            right_t[spot(at), span] = rows.T
-            jac_at = pl.ds(pl.multiple_of(at * BINS_DEV + c * 16, 16), 16)
-            jac_rows[jac_at, :] = jac[:, step * LANES : (step + 1) * LANES]
-        down = [ref[span, :] for ref in (own, y1, y2, y3)]
-        jac = summed(rows_dot(spread(2), jnp.concatenate(down, 1)))
-        scale = jnp.broadcast_to(w_ref[1, pl.ds(c, 1), :], (LANES, LANES)).T
-        for step, rows in enumerate(down):
-            at = spot(lax.rem(py + step, SIDE))
-            left[span, at] = (scale * rows.astype(F32)).astype(BF16)
-            left[jac_span, at] = jac[:, step * LANES : (step + 1) * LANES]
+        jac_rows[jac_span, :] = jacobian(2, (own, x1, x2, x3))
+        jac_cols[jac_span, :] = jacobian(0, down)
+        scaled = turned[:, span].astype(F32) * w_ref[1, pl.ds(c, 1), :]
+        right[:, span] = scaled.astype(BF16)
         return carry
 
-    lax.fori_loop(0, CHUNKS, chunk, 0, unroll=2)
-    for i in range(SIDE):
-        rows = jac_rows[i * BINS_DEV : (i + 1) * BINS_DEV, :]
-        right_t[i * LANES : (i + 1) * LANES, ROWS:] = rows.T
+    lax.fori_loop(0, CHUNKS, chunk, 0, unroll=4)
+    right[:, ROWS:] = jac_rows[...].T
     for n in range(2):
-        term = rows_dot(right_t[...], left[:, n * 2 * LANES : (n + 1) * 2 * LANES])
+        pair = jnp.concatenate([down[2 * n][0:ROWS, :], down[2 * n + 1][0:ROWS, :]], 1)
+        both = jnp.concatenate([pair, jac_cols[:, n * 2 * LANES : (n + 1) * 2 * LANES]], 0)
+        term = rows_dot(right[...], both)
         for i in range(SIDE):
+            row = lax.rem(px + i, SIDE)
             for half in range(2):
-                part = term[:, half * LANES : (half + 1) * LANES]
-                first = part[i * LANES : i * LANES + 64]
-                second = part[i * LANES + 64 : (i + 1) * LANES]
-                at = (i * SIDE + 2 * n + half) * 64
-                kept_ref[at : at + 64, :] = jnp.where(core == 0, first, second)
-                sent_ref[at : at + 64, :] = jnp.where(core == 0, second, first).astype(BF16)
+                part = term[i * LANES : (i + 1) * LANES, half * LANES : (half + 1) * LANES]
+                first, second = part[0:64], part[64:]
+                col = lax.rem(py + 2 * n + half, SIDE)
+                at = pl.ds(pl.multiple_of((row * SIDE + col) * 64, 64), 64)
+                kept_ref[at, :] = jnp.where(core == 0, first, second)
+                sent_ref[at, :] = jnp.where(core == 0, second, first).astype(BF16)
     sent_ref[PIECES * 64 :, :] = extra_ref[...]
 
 
@@ -229,20 +241,37 @@
 
 def body(log_nominal, variations, observed, start, direction, step_lengths):
     own = variations.reshape(ROWS, LANES)
-    y3, x3, y1, x1, y2, x2 = (
-        from_ahead(own, axis, k) for k in (3, 1, 2) for axis in ("y", "x")
-    )
+    packed_own = pl.pallas_call(
+        pack_kernel,
+        out_shape=jax.ShapeDtypeStruct((ROWS + 16, LANES), BF16),
+        in_specs=[VMEM, VMEM, VMEM],
+        out_specs=VMEM,
+        compiler_params=PARAMS,
+        cost_estimate=cost(1_000_000, 1_000_000),
+        name="pack",
+    )(own, start[None, :], direction[None, :])
+    x1, x3, x2 = (from_ahead(packed_own, "x", k) for k in (1, 3, 2))
+    y1, y3, y2 = (from_ahead(own, "y", k) for k in (1, 3, 2))
     sent = pl.pallas_call(
         project_kernel,
-        out_shape=jax.ShapeDtypeStruct((16, 40, LANES), F32),
-        in_specs=[VMEM, VMEM, VMEM, SMEM],
+        out_shape=jax.ShapeDtypeStruct((SIDE, 40, LANES), F32),
+        in_specs=[SMEM] + [VMEM] * 4,
         out_specs=VMEM,
         scratch_shapes=[pltpu.VMEM((40, LANES), F32)],
         compiler_params=PARAMS,
-        cost_estimate=cost(10_000_000, 1_000_000),
+        cost_estimate=cost(40_000_000, 2_000_000),
         name="project",
-    )(own, start[None, :], direction[None, :], step_lengths)
-    got = exchanged(sent, ("y", "x"))
+    )(step_lengths, packed_own, x1, x3, x2)
+    got = exchanged(sent, "y")
+    turned = pl.pallas_call(
+        turn_kernel,
+        out_shape=jax.ShapeDtypeStruct((SIDE * LANES, ROWS), BF16),
+        in_specs=[VMEM] * 4,
+        out_specs=VMEM,
+        compiler_params=PARAMS,
+        cost_estimate=cost(100_000_000, 4_000_000),
+        name="turn",
+    )(packed_own, x1, x3, x2)
     weights, extra, squares = pl.pallas_call(
         weights_kernel,
         out_shape=arrays_of(
@@ -253,7 +282,7 @@
         compiler_params=PARAMS,
         cost_estimate=cost(10_000_000, 1_000_000),
         name="weights",
-    )(got, log_nominal.T, observed[None, :], step_lengths, own)
+    )(got, log_nominal.T, observed[None, :], step_lengths, packed_own)
     px, py = lax.axis_index("x"), lax.axis_index("y")
     core = lax.axis_index("core")
     block = lax.axis_index(("zh", "zl", "core"))
@@ -263,17 +292,17 @@
         out_shape=arrays_of(
             ((PIECES * 64, LANES), F32), ((PIECES * 64 + 16, LANES), BF16)
         ),
-        in_specs=[SMEM] + [VMEM] * 9,
+        in_specs=[SMEM] + [VMEM] * 10,
         out_specs=(VMEM, VMEM),
         scratch_shapes=[
             pltpu.VMEM((SIDE * LANES, DEPTH), BF16),
-            pltpu.VMEM((DEPTH, SIDE * LANES), BF16),
-            pltpu.VMEM((SIDE * BINS_DEV, LANES), BF16),
+            pltpu.VMEM((BINS_DEV, SIDE * LANES), BF16),
+            pltpu.VMEM((BINS_DEV, SIDE * LANES), BF16),
         ],
         compiler_params=PARAMS,
         cost_estimate=cost(2_000_000_000, 5_000_000),
         name="hessian",
-    )(position, weights, extra, own, x1, y1, x3, y3, x2, y2)
+    )(position, weights, extra, turned, packed_own, x1, y1, x3, y3, x2, y2)
     swapped = lax.ppermute(other, "core", [(0, 1), (1, 0)])
     pair = pl.pallas_call(
         pair_kernel,

time: 97.1 us -> 103 us (1.061)
  the two profiles are of different devices: /device:TPU:38 before, /device:TPU:32 now
where the time goes in v3:
time: 103 us; the launch traced here: 102 us
  blocking collectives  45.2 us (44%)
  starting transfers between devices  30.5 us (30%)
  Pallas kernels  11.2 us (11%)
  waiting for transfers between devices  9.34 us (9%)
  local copies, waits for them, and re-layouts  4.98 us (5%)
    all_to_all x2, blocking collectives, exchanged(): return lax.all_to_all(array, axes, 0, 0, tiled=True)  45.2 us
    ppermute x6, starting transfers between devices, from_ahead(): lax.ppermute(array, axis, [((i + step) % SIDE, i) for i in range(SIDE)])  24.1 us
    unnamed x18, local copies, waits for them, and re-layouts  4.89 us
    all_to_all x1, starting transfers between devices, exchanged(): return lax.all_to_all(array, axes, 0, 0, tiled=True)  4.46 us
    ppermute x6, waiting for transfers between devices, from_ahead(): lax.ppermute(array, axis, [((i + step) % SIDE, i) for i in range(SIDE)])  4.4 us
    pallas_call x1, Pallas kernels, body(): pl.pallas_call(hessian_kernel, out_shape=arrays_of(((PIECES * 64, LANES),...  4.25 us
    all_to_all x1, waiting for transfers between devices, exchanged(): return lax.all_to_all(array, axes, 0, 0, tiled=True)  3.43 us
  transfers between devices with their start and end apart: 8, of which 4 were waited for; matrix products, arithmetic and copies ran while one was open for 0% of the time, Pallas kernels for 4%

profile of v3, /device:TPU:32, one launch (start us, length us, event | category | flops | bytes accessed | tf_op | source)
XLA Modules:
  0.0 102.1 jit_solution(5676160579667145237)
XLA Ops:
  0.6 0.0 copy-start.3
  0.6 0.6 copy-done.3
  1.3 0.0 copy-start.8
  1.3 0.7 copy-done.8
  1.9 1.1 %pack.1.own.v_ref = bf16[2064,128]{1,0:T(8,128)(2,1)S(1)} custom-call(bf16[2048,128]{1,0:T(8,128)(2,1)} %bitcast.5.v_ref, f32[1,128]{1,0:T(1,128)S(1)} %bitcast.12, f32[1,128]{1,0:T(1,128)S(1)} %bitcast.15), custom_call_target="tpu_custom_call" | custom-call | flops 1000000 | bytes 1000000 | tf_op jit(solution)/shard_map/pack/pallas_call | solution.py:244
  3.0 4.9 %collective-permute-start.2 = (bf16[2064,128]{1,0:T(8,128)(2,1)S(1)}, bf16[2064,128]{1,0:T(8,128)(2,1)S(1)}, u32[]{:S(2)}, u32[]{:S(2)}) collective-permute-start(bf16[2064,128]{1,0:T(8,128)(2,1)S(1)} %pack.1.own.v_ref), channel_id=1, source_target_pairs={{2,0},{3,1},{0,2},{1,3},{6,4},{7,5},{4,6},{5,7},{10,8},{11,9},{8,1... | collective-permute-start | bytes 1585160 | tf_op jit(solution)/shard_map/ppermute | solution.py:235
  8.0 2.5 %collective-permute-start.1 = (bf16[2064,128]{1,0:T(8,128)(2,1)S(1)}, bf16[2064,128]{1,0:T(8,128)(2,1)S(1)}, u32[]{:S(2)}, u32[]{:S(2)}) collective-permute-start(bf16[2064,128]{1,0:T(8,128)(2,1)S(1)} %pack.1.own.v_ref), channel_id=1, source_target_pairs={{3,0},{0,1},{1,2},{2,3},{7,4},{4,5},{5,6},{6,7},{11,8},{8,9},{9,10... | collective-permute-start | bytes 1585160 | tf_op jit(solution)/shard_map/ppermute | solution.py:235
  10.5 4.6 %collective-permute-start = (bf16[2064,128]{1,0:T(8,128)(2,1)S(1)}, bf16[2064,128]{1,0:T(8,128)(2,1)S(1)}, u32[]{:S(2)}, u32[]{:S(2)}) collective-permute-start(bf16[2064,128]{1,0:T(8,128)(2,1)S(1)} %pack.1.own.v_ref), channel_id=1, source_target_pairs={{1,0},{2,1},{3,2},{0,3},{5,4},{6,5},{7,6},{4,7},{9,8},{10,9},{11,1... | collective-permute-start | bytes 1585160 | tf_op jit(solution)/shard_map/ppermute | solution.py:235
  15.0 5.1 %collective-permute-start.5 = (bf16[2048,128]{1,0:T(8,128)(2,1)}, bf16[2048,128]{1,0:T(8,128)(2,1)S(1)}, u32[]{:S(2)}, u32[]{:S(2)}) collective-permute-start(bf16[2048,128]{1,0:T(8,128)(2,1)} %bitcast.5.v_ref), channel_id=1, source_target_pairs={{8,0},{12,4},{0,8},{4,12},{9,1},{13,5},{1,9},{5,13},{10,2},{14,6},... | collective-permute-start | bytes 1572872 | tf_op jit(solution)/shard_map/ppermute | solution.py:235
  20.2 2.6 %collective-permute-start.4 = (bf16[2048,128]{1,0:T(8,128)(2,1)}, bf16[2048,128]{1,0:T(8,128)(2,1)S(1)}, u32[]{:S(2)}, u32[]{:S(2)}) collective-permute-start(bf16[2048,128]{1,0:T(8,128)(2,1)} %bitcast.5.v_ref), channel_id=1, source_target_pairs={{12,0},{0,4},{4,8},{8,12},{13,1},{1,5},{5,9},{9,13},{14,2},{2,6},{... | collective-permute-start | bytes 1572872 | tf_op jit(solution)/shard_map/ppermute | solution.py:235
  22.8 0.0 collective-permute-done.2.x2
  22.8 4.5 %collective-permute-start.3 = (bf16[2048,128]{1,0:T(8,128)(2,1)}, bf16[2048,128]{1,0:T(8,128)(2,1)}, u32[]{:S(2)}, u32[]{:S(2)}) collective-permute-start(bf16[2048,128]{1,0:T(8,128)(2,1)} %bitcast.5.v_ref), channel_id=1, source_target_pairs={{4,0},{8,4},{12,8},{0,12},{5,1},{9,5},{13,9},{1,13},{6,2},{10,6},{... | collective-permute-start | bytes 1572872 | tf_op jit(solution)/shard_map/ppermute | solution.py:235
  27.2 4.3 %collective-permute-done.1.x3 = bf16[2064,128]{1,0:T(8,128)(2,1)S(1)} collective-permute-done((bf16[2064,128]{1,0:T(8,128)(2,1)S(1)}, bf16[2064,128]{1,0:T(8,128)(2,1)S(1)}, u32[]{:S(2)}, u32[]{:S(2)}) %collective-permute-start.1) | collective-permute-done | bytes 528416 | tf_op jit(solution)/shard_map/ppermute | solution.py:235
  31.5 0.1 collective-permute-done.x1
  31.6 0.0 copy-start.5
  31.6 0.7 copy-done.5
  32.3 1.9 %project.1 = f32[4,40,128]{2,1,0:T(8,128)} custom-call(f32[3]{0:T(128)S(1)} %copy-done.5, bf16[2064,128]{1,0:T(8,128)(2,1)S(1)} %pack.1.own.v_ref, bf16[2064,128]{1,0:T(8,128)(2,1)S(1)} %collective-permute-done.x1, bf16[2064,128]{1,0:T(8,128)(2,1)S(1)} %collective-permute-done.1.x3, bf16[2064,128]{1,0:T(8,128)(2,1)S(1)} %collective-permute-done.2.x2), custom_call_target="tpu_custom_call" | custom-call | flops 40000000 | bytes 2000000 | tf_op jit(solution)/shard_map/project/pallas_call | solution.py:255
  34.1 4.5 %all-to-all-start = ((f32[4,40,128]{2,1,0:T(8,128)}), f32[4,40,128]{2,1,0:T(8,128)S(1)}, u32[]{:S(2)}, u32[]{:S(2)}) async-start(f32[4,40,128]{2,1,0:T(8,128)} %project.1), calls=%async_computation | async-start | bytes 163840 | tf_op jit(solution)/shard_map/all_to_all | solution.py:239
  38.6 0.1 stack.23.pos_ref
  38.7 0.0 copy-start.2
  38.7 0.0 copy-start.6
  38.7 0.0 copy-start.7
  38.7 0.8 turn.1.turned
  39.6 0.0 copy-start
  39.6 1.3 %copy-done = bf16[512,2048]{1,0:T(8,128)(2,1)} copy-done((bf16[512,2048]{1,0:T(8,128)(2,1)}, bf16[512,2048]{1,0:T(8,128)(2,1)S(1)}, u32[]{:S(2)}) %copy-start) | copy-done | bytes 2097176
  40.9 3.4 %all-to-all-done.got_ref = f32[4,40,128]{2,1,0:T(8,128)S(1)} async-done(((f32[4,40,128]{2,1,0:T(8,128)}), f32[4,40,128]{2,1,0:T(8,128)S(1)}, u32[]{:S(2)}, u32[]{:S(2)}) %all-to-all-start) | async-done | bytes 81952 | tf_op jit(solution)/shard_map/all_to_all | solution.py:239
  44.3 0.0 copy-done.2
  44.3 0.0 copy-done.6
  44.3 0.0 copy-done.7
  44.3 1.3 %weights.1 = (f32[3,16,128]{2,1,0:T(8,128)S(1)}, bf16[16,128]{1,0:T(8,128)(2,1)S(1)}, f32[8,128]{1,0:T(8,128)S(1)}) custom-call(f32[4,40,128]{2,1,0:T(8,128)S(1)} %all-to-all-done.got_ref, f32[8,256]{1,0:T(8,128)S(1)} %bitcast.11, s32[1,256]{1,0:T(1,128)S(1)} %bitcast.14, f32[3]{0:T(128)S(1)} %copy-done.6, bf16[2064,128]{1,0:T(8,128)(2,1)S(1)} %pack.1.own.v_ref), custom_call_target="tpu_custom_call" | custom-call | flops 10000000 | bytes 1000000 | tf_op jit(solution)/shard_map/weights/pallas_call | solution.py:275
  45.7 0.0 collective-permute-done.5.y2
  45.7 0.0 collective-permute-done.4.y3
  45.7 0.0 collective-permute-done.3.y1
  45.7 0.0 copy-start.1
  45.7 1.6 %copy-done.1 = bf16[512,2048]{1,0:T(8,128)(2,1)S(1)} copy-done((bf16[512,2048]{1,0:T(8,128)(2,1)S(1)}, bf16[512,2048]{1,0:T(8,128)(2,1)}, u32[]{:S(2)}) %copy-start.1) | copy-done | bytes 2097176
  47.3 4.3 %hessian.1 = (f32[1024,128]{1,0:T(8,128)S(1)}, bf16[1040,128]{1,0:T(8,128)(2,1)S(1)}) custom-call(s32[5]{0:T(128)S(1)} %stack.23.pos_ref, f32[3,16,128]{2,1,0:T(8,128)S(1)} %get-tuple-element.11.w_ref, bf16[16,128]{1,0:T(8,128)(2,1)S(1)} %get-tuple-element.12.extra_ref, bf16[512,2048]{1,0:T(8,128)(2,1)S(1)} %copy-done.1, ...), custom_call_target="tpu_custom_call" | custom-call | flops 2000000000 | bytes 5000000 | tf_op jit(solution)/shard_map/hessian/pallas_call | solution.py:290
  51.6 0.0 copy-start.4
  51.6 1.9 %collective-permute-start.6 = (bf16[1040,128]{1,0:T(8,128)(2,1)S(1)}, bf16[1040,128]{1,0:T(8,128)(2,1)S(1)}, u32[]{:S(2)}, u32[]{:S(2)}) collective-permute-start(bf16[1040,128]{1,0:T(8,128)(2,1)S(1)} %get-tuple-element.14), channel_id=1, source_target_pairs={{0,16},{16,0},{1,17},{17,1},{2,18},{18,2},{3,19},{19,3},{4,20},{20... | collective-permute-start | bytes 798728 | tf_op jit(solution)/shard_map/ppermute | solution.py:306
  53.5 1.5 %collective-permute-done.6.got_ref = bf16[1040,128]{1,0:T(8,128)(2,1)S(1)} collective-permute-done((bf16[1040,128]{1,0:T(8,128)(2,1)S(1)}, bf16[1040,128]{1,0:T(8,128)(2,1)S(1)}, u32[]{:S(2)}, u32[]{:S(2)}) %collective-permute-start.6) | collective-permute-done | bytes 266272 | tf_op jit(solution)/shard_map/ppermute | solution.py:306
  55.0 0.1 pair.1
  55.1 18.8 %all_to_all.15.got_ref = bf16[16,80,128]{2,1,0:T(8,128)(2,1)S(1)} all-to-all(bf16[16,80,128]{2,1,0:T(8,128)(2,1)S(1)} %pair.1), channel_id=1, replica_groups=mesh['zh'=4,'zl'=4,'core'=2,'y'=4,'x'=4] {'zl','y'}, dimensions={0} | all-to-all | bytes 655360 | tf_op jit(solution)/shard_map/all_to_all | solution.py:239
  73.8 0.6 plane.1
  74.4 26.5 %all_to_all.16.got_ref = bf16[4,80,128]{2,1,0:T(8,128)(2,1)S(1)} all-to-all(bf16[4,80,128]{2,1,0:T(8,128)(2,1)S(1)} %plane.1), channel_id=1, replica_groups=mesh['zh'=4,'zl'=4,'core'=2,'y'=4,'x'=4] {'zh'}, dimensions={0} | all-to-all | bytes 163840 | tf_op jit(solution)/shard_map/all_to_all | solution.py:239
  100.9 0.0 copy-done.4
  100.9 1.2 %finish.1 = (f32[3]{0:T(128)}, f32[1,128]{1,0:T(1,128)}, f32[64,128]{1,0:T(8,128)}) custom-call(s32[5]{0:T(128)S(1)} %stack.23.pos_ref, bf16[4,80,128]{2,1,0:T(8,128)(2,1)S(1)} %all_to_all.16.got_ref, f32[8,128]{1,0:T(8,128)S(1)} %get-tuple-element.15.sq_ref, f32[1,128]{1,0:T(1,128)S(1)} %bitcast.13), custom_call_target="tpu_custom_call" | custom-call | flops 1000000 | bytes 1000000 | tf_op jit(solution)/shard_map/finish/pallas_call | solution.py:325
Async XLA Ops:
  0.6 0.7 copy-start.3
  1.3 0.7 copy-start.8
  3.0 19.7 %collective-permute-start.2 = (bf16[2064,128]{1,0:T(8,128)(2,1)S(1)}, bf16[2064,128]{1,0:T(8,128)(2,1)S(1)}, u32[]{:S(2)}, u32[]{:S(2)}) collective-permute-start(bf16[2064,128]{1,0:T(8,128)(2,1)S(1)} %pack.1.own.v_ref), channel_id=1, source_target_pairs={{2,0},{3,1},{0,2},{1,3},{6,4},{7,5},{4,6},{5,7},{10,8},{11,9},{8,1... | collective-permute-start | bytes 1585160 | tf_op jit(solution)/shard_map/ppermute | solution.py:235
  8.0 23.5 %collective-permute-start.1 = (bf16[2064,128]{1,0:T(8,128)(2,1)S(1)}, bf16[2064,128]{1,0:T(8,128)(2,1)S(1)}, u32[]{:S(2)}, u32[]{:S(2)}) collective-permute-start(bf16[2064,128]{1,0:T(8,128)(2,1)S(1)} %pack.1.own.v_ref), channel_id=1, source_target_pairs={{3,0},{0,1},{1,2},{2,3},{7,4},{4,5},{5,6},{6,7},{11,8},{8,9},{9,10... | collective-permute-start | bytes 1585160 | tf_op jit(solution)/shard_map/ppermute | solution.py:235
  10.5 21.2 %collective-permute-start = (bf16[2064,128]{1,0:T(8,128)(2,1)S(1)}, bf16[2064,128]{1,0:T(8,128)(2,1)S(1)}, u32[]{:S(2)}, u32[]{:S(2)}) collective-permute-start(bf16[2064,128]{1,0:T(8,128)(2,1)S(1)} %pack.1.own.v_ref), channel_id=1, source_target_pairs={{1,0},{2,1},{3,2},{0,3},{5,4},{6,5},{7,6},{4,7},{9,8},{10,9},{11,1... | collective-permute-start | bytes 1585160 | tf_op jit(solution)/shard_map/ppermute | solution.py:235
  15.0 30.6 %collective-permute-start.5 = (bf16[2048,128]{1,0:T(8,128)(2,1)}, bf16[2048,128]{1,0:T(8,128)(2,1)S(1)}, u32[]{:S(2)}, u32[]{:S(2)}) collective-permute-start(bf16[2048,128]{1,0:T(8,128)(2,1)} %bitcast.5.v_ref), channel_id=1, source_target_pairs={{8,0},{12,4},{0,8},{4,12},{9,1},{13,5},{1,9},{5,13},{10,2},{14,6},... | collective-permute-start | bytes 1572872 | tf_op jit(solution)/shard_map/ppermute | solution.py:235
  20.2 25.5 %collective-permute-start.4 = (bf16[2048,128]{1,0:T(8,128)(2,1)}, bf16[2048,128]{1,0:T(8,128)(2,1)S(1)}, u32[]{:S(2)}, u32[]{:S(2)}) collective-permute-start(bf16[2048,128]{1,0:T(8,128)(2,1)} %bitcast.5.v_ref), channel_id=1, source_target_pairs={{12,0},{0,4},{4,8},{8,12},{13,1},{1,5},{5,9},{9,13},{14,2},{2,6},{... | collective-permute-start | bytes 1572872 | tf_op jit(solution)/shard_map/ppermute | solution.py:235
  22.8 22.9 %collective-permute-start.3 = (bf16[2048,128]{1,0:T(8,128)(2,1)}, bf16[2048,128]{1,0:T(8,128)(2,1)}, u32[]{:S(2)}, u32[]{:S(2)}) collective-permute-start(bf16[2048,128]{1,0:T(8,128)(2,1)} %bitcast.5.v_ref), channel_id=1, source_target_pairs={{4,0},{8,4},{12,8},{0,12},{5,1},{9,5},{13,9},{1,13},{6,2},{10,6},{... | collective-permute-start | bytes 1572872 | tf_op jit(solution)/shard_map/ppermute | solution.py:235
  31.6 0.7 copy-start.5
  34.1 10.2 %all-to-all-start = ((f32[4,40,128]{2,1,0:T(8,128)}), f32[4,40,128]{2,1,0:T(8,128)S(1)}, u32[]{:S(2)}, u32[]{:S(2)}) async-start(f32[4,40,128]{2,1,0:T(8,128)} %project.1), calls=%async_computation | async-start | bytes 163840 | tf_op jit(solution)/shard_map/all_to_all | solution.py:239
  38.7 5.6 %copy-start.2 = (f32[256,8]{0,1:T(8,128)S(1)}, f32[256,8]{0,1:T(8,128)}, u32[]{:S(2)}) copy-start(f32[256,8]{0,1:T(8,128)} %param.6) | copy-start | bytes 24580
  38.7 5.6 %copy-start.6 = (f32[3]{0:T(128)S(1)}, f32[3]{0:T(128)}, u32[]{:S(2)}) copy-start(f32[3]{0:T(128)} %steps_ref.3) | copy-start | bytes 40
  38.7 5.6 %copy-start.7 = (s32[256]{0:T(256)S(1)}, s32[256]{0:T(256)}, u32[]{:S(2)}) copy-start(s32[256]{0:T(256)} %param.8) | copy-start | bytes 3076
  39.6 1.3 %copy-start = (bf16[512,2048]{1,0:T(8,128)(2,1)}, bf16[512,2048]{1,0:T(8,128)(2,1)S(1)}, u32[]{:S(2)}) copy-start(bf16[512,2048]{1,0:T(8,128)(2,1)S(1)} %turn.1.turned) | copy-start | bytes 6291460
  45.7 1.6 %copy-start.1 = (bf16[512,2048]{1,0:T(8,128)(2,1)S(1)}, bf16[512,2048]{1,0:T(8,128)(2,1)}, u32[]{:S(2)}) copy-start(bf16[512,2048]{1,0:T(8,128)(2,1)} %copy-done) | copy-start | bytes 6291460
  51.6 49.4 %copy-start.4 = (f32[128]{0:T(128)S(1)}, f32[128]{0:T(128)}, u32[]{:S(2)}) copy-start(f32[128]{0:T(128)} %param.9) | copy-start | bytes 1540
  51.6 3.4 %collective-permute-start.6 = (bf16[1040,128]{1,0:T(8,128)(2,1)S(1)}, bf16[1040,128]{1,0:T(8,128)(2,1)S(1)}, u32[]{:S(2)}, u32[]{:S(2)}) collective-permute-start(bf16[1040,128]{1,0:T(8,128)(2,1)S(1)} %get-tuple-element.14), channel_id=1, source_target_pairs={{0,16},{16,0},{1,17},{17,1},{2,18},{18,2},{3,19},{19,3},{4,20},{20... | collective-permute-start | bytes 798728 | tf_op jit(solution)/shard_map/ppermute | solution.py:306

commit v4 on v2

v4 whole, which is shorter than its diff:
```python
import jax
import jax.numpy as jnp
import numpy as np
from jax import lax
from jax.experimental import pallas as pl
from jax.experimental.pallas import tpu as pltpu
from jax.sharding import Mesh
from jax.sharding import PartitionSpec as P


F32 = jnp.float32
BF16 = jnp.bfloat16
SIDE = 4
PROC = 8
ROWS = 2048
BINS_DEV = 256
LANES = 128
CHUNKS = ROWS // LANES
PIECES = SIDE * SIDE
BIN_TOTAL = 32 * BINS_DEV
DEPTH = ROWS + BINS_DEV
VMEM = pl.BlockSpec(memory_space=pltpu.VMEM)
HBM = pl.BlockSpec(memory_space=pltpu.HBM)
SMEM = pl.BlockSpec(memory_space=pltpu.SMEM)
PARAMS = pltpu.CompilerParams(vmem_limit_bytes=12 * 1024 * 1024)


def cost(flops, moved):
    return pl.CostEstimate(flops=flops, bytes_accessed=moved, transcendentals=0)


def thirds(x):
    high = x.astype(BF16)
    rest = x - high.astype(F32)
    middle = rest.astype(BF16)
    low = (rest - middle.astype(F32)).astype(BF16)
    return [high, middle, low]


def rows_dot(a, b):
    return lax.dot_general(a, b, (((1,), (0,)), ((), ())), preferred_element_type=F32)


def packed(four):
    return jnp.concatenate(thirds(four) + [jnp.zeros((4, LANES), BF16)], 0)


def unpacked(rows):
    wide = rows.astype(F32)
    return wide[..., 0:4, :] + wide[..., 4:8, :] + wide[..., 8:12, :]


def project_kernel(v_ref, start_ref, dir_ref, out_ref, flat, rows, ends, sems):
    moves = [
        pltpu.make_async_copy(start_ref, ends.at[0:1], sems.at[0]),
        pltpu.make_async_copy(dir_ref, ends.at[1:2], sems.at[1]),
        pltpu.make_async_copy(v_ref, rows, sems.at[2]),
    ]
    for move in moves:
        move.start()
    for move in moves:
        move.wait()
    start, direction = ends[0:1, :], ends[1:2, :]
    parts = jnp.concatenate(thirds(start) + thirds(direction), 0)
    six = lax.dot_general(
        parts, rows[...], (((1,), (1,)), ((), ())), preferred_element_type=F32
    )
    along_start = six[0:1] + six[1:2] + six[2:3]
    along_dir = six[3:4] + six[4:5] + six[5:6]
    for c in range(CHUNKS):
        span = slice(c * LANES, (c + 1) * LANES)
        flat[c : c + 1, :] = along_start[:, span]
        flat[CHUNKS + c : CHUNKS + c + 1, :] = along_dir[:, span]
    tail = [start * direction, direction * direction, jnp.zeros((6, LANES), F32)]
    flat[2 * CHUNKS :, :] = jnp.concatenate(tail, 0)
    whole = flat[...]
    for i in range(out_ref.shape[0]):
        out_ref[i] = whole


def lane_groups_sum(x, lane):
    for k in (1, 2, 4):
        up = pltpu.roll(x, k, 1)
        down = pltpu.roll(x, LANES - k, 1)
        x = x + jnp.where((lane & k) != 0, up, down)
    return x


def layout_kernel(nominal_ref, counts_ref, steps_ref, out_ref):
    lane = lax.broadcasted_iota(jnp.int32, (CHUNKS, LANES), 1)
    place = lax.broadcasted_iota(jnp.int32, (CHUNKS, BINS_DEV), 1)
    line = lax.broadcasted_iota(jnp.int32, (CHUNKS, BINS_DEV), 0)
    mine = place // CHUNKS == line
    each = [nominal_ref[p : p + 1, :] for p in range(PROC)] + [counts_ref[...].astype(F32)]
    spread = jnp.concatenate([jnp.where(mine, row, 0.0) for row in each], 0)
    source = lax.broadcasted_iota(jnp.int32, (BINS_DEV, LANES), 0) % CHUNKS
    target = lax.broadcasted_iota(jnp.int32, (BINS_DEV, LANES), 1) // PROC
    pick = (source == target).astype(F32).astype(BF16)
    high, middle, low = (rows_dot(part, pick) for part in thirds(spread))
    moved = high + middle + low
    out = jnp.zeros((CHUNKS, LANES), F32)
    for p in range(PROC):
        out = jnp.where(lane % PROC == p, moved[p * CHUNKS : (p + 1) * CHUNKS], out)
    out_ref[0:CHUNKS, :] = out
    out_ref[CHUNKS : 2 * CHUNKS, :] = moved[PROC * CHUNKS :]
    for j in range(3):
        at = 2 * CHUNKS + j
        out_ref[at : at + 1, :] = jnp.full((1, LANES), steps_ref[j], F32)


def weights_kernel(got_ref, local_ref, v_ref, w_ref, bins_ref, sq_ref):
    total = jnp.sum(got_ref[...], axis=0)
    along_start = total[0:CHUNKS]
    along_dir = total[CHUNKS : 2 * CHUNKS]
    cross, square = total[2 * CHUNKS : 2 * CHUNKS + 1], total[2 * CHUNKS + 1 : 2 * CHUNKS + 2]
    lane = lax.broadcasted_iota(jnp.int32, (CHUNKS, LANES), 1)
    nominal, counts = local_ref[0:CHUNKS, :], local_ref[CHUNKS : 2 * CHUNKS, :]
    base = jnp.exp(nominal + along_start)
    base_total = lane_groups_sum(base, lane)
    base_log = jnp.log(base_total)
    part, norms = [], []
    for j in range(3):
        step = local_ref[2 * CHUNKS + j : 2 * CHUNKS + j + 1, :]
        shifted = jnp.exp(nominal + (along_start + step * along_dir))
        expected = lane_groups_sum(shifted, lane)
        change = (expected - base_total) - counts * (jnp.log(expected) - base_log)
        part.append(jnp.sum(change, axis=0, keepdims=True) * (1.0 / PROC))
        norms.append(step * (2.0 * cross + step * square))
    sq_ref[...] = jnp.concatenate(norms + [jnp.zeros((5, LANES), F32)], 0)
    residual = 1.0 - counts / base_total
    left = residual * base
    w_ref[0] = base
    w_ref[1] = left
    w_ref[2] = (counts / (base_total * base_total)) * base
    grad = jnp.zeros((3, LANES), F32)
    for c in range(CHUNKS):
        row = jnp.concatenate(thirds(left[c : c + 1]), 0)
        grad = grad + rows_dot(row, v_ref[c * LANES : (c + 1) * LANES, :])
    grad = jnp.sum(grad, axis=0, keepdims=True)
    bins_ref[...] = packed(jnp.concatenate([grad] + part, 0))


def bin_mask():
    mine = lax.broadcasted_iota(jnp.int32, (16, LANES), 1) // PROC
    return mine == lax.broadcasted_iota(jnp.int32, (16, LANES), 0)


def jacobian(weight, mine, blocks):
    spread = jnp.concatenate(thirds(jnp.where(mine, weight, 0.0)), 0)
    jac = rows_dot(spread, jnp.concatenate(blocks, 1))
    return (jac[0:16] + jac[16:32] + jac[32:48]).astype(BF16)


def rows_kernel(w_ref, own, x1, x3, x2, y3, y2, right, jac_cols, jac_rows):
    mine = bin_mask()

    def chunk(c, carry):
        span = pl.ds(pl.multiple_of(c * LANES, LANES), LANES)
        jac_span = pl.ds(pl.multiple_of(c * 16, 16), 16)
        base, left, curve = (w_ref[k, pl.ds(c, 1), :] for k in range(3))
        across = [ref[span, :] for ref in (own, x1, x2, x3)]
        jac_rows[jac_span, :] = jacobian(curve, mine, across)
        jac_cols[jac_span, :] = jacobian(base, mine, [ref[span, :] for ref in (own, y2, y3)])
        for step, rows in enumerate(across):
            scaled = rows.T.astype(F32) * left
            right[step * LANES : (step + 1) * LANES, span] = scaled.astype(BF16)
        return carry

    lax.fori_loop(0, CHUNKS, chunk, 0, unroll=4)
    right[:, ROWS:] = jac_rows[...].T


def hessian_kernel(
    pos_ref, w_ref, extra_ref, right, jac_ref, own, y2, y3, y1, kept_ref, sent_ref, jac_last
):
    px, py, core = pos_ref[0], pos_ref[1], pos_ref[4]
    mine = bin_mask()
    for c in range(CHUNKS):
        rows = y1[c * LANES : (c + 1) * LANES, :]
        jac_last[c * 16 : (c + 1) * 16, :] = jacobian(w_ref[0, c : c + 1, :], mine, [rows])
    jacs = [jac_ref[:, k * LANES : (k + 1) * LANES] for k in range(3)] + [jac_last[...]]
    steps = ((own, 0), (y2, 2), (y3, 3), (y1, 1))
    for n in range(2):
        cols = [
            jnp.concatenate([steps[k][0][...], jacs[k]], 0) for k in (2 * n, 2 * n + 1)
        ]
        term = rows_dot(right[...], jnp.concatenate(cols, 1))
        for i in range(SIDE):
            row_at = lax.rem(px + i, SIDE)
            for half in range(2):
                part = term[i * LANES : (i + 1) * LANES, half * LANES : (half + 1) * LANES]
                first, second = part[0:64], part[64:]
                col_at = lax.rem(py + steps[2 * n + half][1], SIDE)
                at = pl.ds(pl.multiple_of((row_at * SIDE + col_at) * 64, 64), 64)
                kept_ref[at, :] = jnp.where(core == 0, first, second)
                sent_ref[at, :] = jnp.where(core == 0, second, first).astype(BF16)
    sent_ref[PIECES * 64 :, :] = extra_ref[...]


def pair_kernel(kept_ref, extra_ref, got_ref, out_ref):
    extra = packed(unpacked(extra_ref[...]) + unpacked(got_ref[PIECES * 64 :, :]))
    for k in range(PIECES):
        span = slice(k * 64, (k + 1) * 64)
        both = kept_ref[span, :] + got_ref[span, :].astype(F32)
        out_ref[k, 0:64, :] = both.astype(BF16)
        out_ref[k, 64:, :] = extra


def plane_kernel(pos_ref, got_ref, out_ref):
    py = pos_ref[1]
    extra = unpacked(got_ref[py, 64:, :])
    for k in range(1, SIDE):
        extra = extra + unpacked(got_ref[k * SIDE + py, 64:, :])
    extra = packed(extra)
    for j in range(SIDE):
        tile = got_ref[j, 0:64, :].astype(F32)
        for k in range(1, SIDE):
            tile = tile + got_ref[k * SIDE + j, 0:64, :].astype(F32)
        out_ref[j, 0:64, :] = tile.astype(BF16)
        out_ref[j, 64:, :] = extra


def finish_kernel(pos_ref, got_ref, sq_ref, start_ref, line_ref, grad_ref, hess_ref):
    scale = 1.0 / BIN_TOTAL
    tile = jnp.sum(got_ref[:, 0:64, :].astype(F32), axis=0)
    extra = jnp.sum(unpacked(got_ref[:, 64:, :]), axis=0)
    row = lax.broadcasted_iota(jnp.int32, (64, LANES), 0) + pos_ref[2] * 64
    col = lax.broadcasted_iota(jnp.int32, (64, LANES), 1) + pos_ref[3] * LANES
    hess_ref[...] = (tile + (row == col).astype(F32)) * scale
    grad_ref[...] = (extra[0:1] + start_ref[...]) * scale
    for j in range(3):
        line_ref[j] = jnp.sum(extra[1 + j : 2 + j, :] + 0.5 * sq_ref[j : j + 1, :]) * scale


def arrays_of(*shapes):
    return tuple(jax.ShapeDtypeStruct(s, d) for s, d in shapes)


def from_ahead(array, axis, step):
    return lax.ppermute(array, axis, [((i + step) % SIDE, i) for i in range(SIDE)])


def exchanged(array, axes):
    return lax.all_to_all(array, axes, 0, 0, tiled=True)


def body(log_nominal, variations, observed, start, direction, step_lengths):
    own = variations.reshape(ROWS, LANES)
    sent = pl.pallas_call(
        project_kernel,
        out_shape=jax.ShapeDtypeStruct((16, 40, LANES), F32),
        in_specs=[HBM, HBM, HBM],
        out_specs=VMEM,
        scratch_shapes=[
            pltpu.VMEM((40, LANES), F32),
            pltpu.VMEM((ROWS, LANES), BF16),
            pltpu.VMEM((8, LANES), F32),
            pltpu.SemaphoreType.DMA((3,)),
        ],
        compiler_params=pltpu.CompilerParams(vmem_limit_bytes=62 * 1024 * 1024),
        cost_estimate=cost(10_000_000, 1_000_000),
        name="project",
    )(own, start[None, :], direction[None, :])
    own, sent = lax.optimization_barrier((own, sent))
    x2, y2, x3, y3, x1, y1 = (from_ahead(own, axis, k) for k in (2, 3, 1) for axis in ("x", "y"))
    got = exchanged(sent, ("y", "x"))
    local = pl.pallas_call(
        layout_kernel,
        out_shape=jax.ShapeDtypeStruct((40, LANES), F32),
        in_specs=[VMEM, VMEM, SMEM],
        out_specs=VMEM,
        compiler_params=PARAMS,
        cost_estimate=cost(10_000_000, 1_000_000),
        name="layout",
    )(log_nominal.T, observed[None, :], step_lengths)
    weights, extra, squares = pl.pallas_call(
        weights_kernel,
        out_shape=arrays_of(
            ((3, CHUNKS, LANES), F32), ((16, LANES), BF16), ((8, LANES), F32)
        ),
        in_specs=[VMEM, VMEM, VMEM],
        out_specs=(VMEM, VMEM, VMEM),
        compiler_params=PARAMS,
        cost_estimate=cost(10_000_000, 1_000_000),
        name="weights",
    )(got, local, own)
    px, py = lax.axis_index("x"), lax.axis_index("y")
    core = lax.axis_index("core")
    block = lax.axis_index(("zh", "zl", "core"))
    position = jnp.stack([px, py, block, py * SIDE + px, core]).astype(jnp.int32)
    right, jac_cols = pl.pallas_call(
        rows_kernel,
        out_shape=arrays_of(
            ((SIDE * LANES, DEPTH), BF16), ((BINS_DEV, 3 * LANES), BF16)
        ),
        in_specs=[VMEM] * 7,
        out_specs=(VMEM, VMEM),
        scratch_shapes=[pltpu.VMEM((BINS_DEV, SIDE * LANES), BF16)],
        compiler_params=PARAMS,
        cost_estimate=cost(1_000_000_000, 5_000_000),
        name="rows",
    )(weights, own, x1, x3, x2, y3, y2)
    kept, other = pl.pallas_call(
        hessian_kernel,
        out_shape=arrays_of(
            ((PIECES * 64, LANES), F32), ((PIECES * 64 + 16, LANES), BF16)
        ),
        in_specs=[SMEM] + [VMEM] * 8,
        out_specs=(VMEM, VMEM),
        scratch_shapes=[pltpu.VMEM((BINS_DEV, LANES), BF16)],
        compiler_params=PARAMS,
        cost_estimate=cost(1_000_000_000, 5_000_000),
        name="hessian",
    )(position, weights, extra, right, jac_cols, own, y2, y3, y1)
    swapped = lax.ppermute(other, "core", [(0, 1), (1, 0)])
    pair = pl.pallas_call(
        pair_kernel,
        out_shape=jax.ShapeDtypeStruct((PIECES, 80, LANES), BF16),
        in_specs=[VMEM] * 3,
        out_specs=VMEM,
        compiler_params=PARAMS,
        cost_estimate=cost(1_000_000, 1_000_000),
        name="pair",
    )(kept, extra, swapped)
    near = pl.pallas_call(
        plane_kernel,
        out_shape=jax.ShapeDtypeStruct((SIDE, 80, LANES), BF16),
        in_specs=[SMEM, VMEM],
        out_specs=VMEM,
        compiler_params=PARAMS,
        cost_estimate=cost(1_000_000, 1_000_000),
        name="plane",
    )(position, exchanged(pair, ("zl", "y")))
    line_change, gradient, hessian = pl.pallas_call(
        finish_kernel,
        out_shape=arrays_of(((3,), F32), ((1, LANES), F32), ((64, LANES), F32)),
        in_specs=[SMEM, VMEM, VMEM, VMEM],
        out_specs=(SMEM, VMEM, VMEM),
        compiler_params=PARAMS,
        cost_estimate=cost(1_000_000, 1_000_000),
        name="finish",
    )(position, exchanged(near, "zh"), squares, start[None, :])
    return line_change, gradient[0], hessian


def solution(mesh):
    split = Mesh(
        np.asarray(mesh.devices).reshape(SIDE, SIDE, 2, SIDE, SIDE),
        ("zh", "zl", "core", "y", "x"),
    )
    bins, nuis = ("zh", "zl", "core"), ("y", "x")
    placed = (P(bins, None), P(bins, None, nuis), P(bins), P(nuis), P(nuis), P())
    return jax.shard_map(
        body,
        mesh=split,
        in_specs=placed,
        out_specs=(P(), P(nuis), P(bins, nuis)),
        check_vma=False,
    )
```

time: 97.1 us -> 103 us (1.061)
  the two profiles are of different devices: /device:TPU:38 before, /device:TPU:32 now
where the time goes in v4:
time: 103 us; the launch traced here: 102 us
  blocking collectives  44.6 us (43%)
  starting transfers between devices  37.3 us (36%)
  Pallas kernels  8.61 us (8%)
  waiting for transfers between devices  7.69 us (7%)
  local copies, waits for them, and re-layouts  3.16 us (3%)
    all_to_all x2, blocking collectives, exchanged(): return lax.all_to_all(array, axes, 0, 0, tiled=True)  44.6 us
    ppermute x6, starting transfers between devices, from_ahead(): lax.ppermute(array, axis, [((i + step) % SIDE, i) for i in range(SIDE)])  22.3 us
    all_to_all x1, starting transfers between devices, exchanged(): return lax.all_to_all(array, axes, 0, 0, tiled=True)  13.1 us
    all_to_all x1, waiting for transfers between devices, exchanged(): return lax.all_to_all(array, axes, 0, 0, tiled=True)  6.16 us
    unnamed x10, local copies, waits for them, and re-layouts  3.08 us
    pallas_call x1, Pallas kernels, body(): pl.pallas_call(hessian_kernel, out_shape=arrays_of(((PIECES * 64, LANES),...  2.14 us
    pallas_call x1, Pallas kernels, body(): pl.pallas_call(project_kernel, out_shape=jax.ShapeDtypeStruct((16, 40, LA...  2.09 us
  transfers between devices with their start and end apart: 8, of which 2 were waited for; matrix products, arithmetic and copies ran while one was open for 0% of the time, Pallas kernels for 2%

profile of v4, /device:TPU:32, one launch (start us, length us, event | category | flops | bytes accessed | tf_op | source)
XLA Modules:
  0.0 102.2 jit_solution(8289352925950403672)
XLA Ops:
  0.6 2.1 %project.1 = f32[16,40,128]{2,1,0:T(8,128)} custom-call(bf16[2048,128]{1,0:T(8,128)(2,1)} %bitcast.11, f32[1,128]{1,0:T(1,128)} %bitcast.21, f32[1,128]{1,0:T(1,128)} %bitcast.25), custom_call_target="tpu_custom_call" | custom-call | flops 10000000 | bytes 1000000 | tf_op jit(solution)/shard_map/project/pallas_call | solution.py:249
  2.7 3.5 %collective-permute-start.3 = (bf16[2048,128]{1,0:T(8,128)(2,1)}, bf16[2048,128]{1,0:T(8,128)(2,1)S(1)}, u32[]{:S(2)}, u32[]{:S(2)}) collective-permute-start(bf16[2048,128]{1,0:T(8,128)(2,1)} %bitcast.12), channel_id=1, source_target_pairs={{12,0},{0,4},{4,8},{8,12},{13,1},{1,5},{5,9},{9,13},{14,2},{2,6},{... | collective-permute-start | bytes 1572872 | tf_op jit(solution)/shard_map/ppermute | solution.py:240
  6.2 4.8 %collective-permute-start.4 = (bf16[2048,128]{1,0:T(8,128)(2,1)}, bf16[2048,128]{1,0:T(8,128)(2,1)S(1)}, u32[]{:S(2)}, u32[]{:S(2)}) collective-permute-start(bf16[2048,128]{1,0:T(8,128)(2,1)} %bitcast.13), channel_id=1, source_target_pairs={{8,0},{12,4},{0,8},{4,12},{9,1},{13,5},{1,9},{5,13},{10,2},{14,6},... | collective-permute-start | bytes 1572872 | tf_op jit(solution)/shard_map/ppermute | solution.py:240
  11.0 4.7 %collective-permute-start = (bf16[2048,128]{1,0:T(8,128)(2,1)}, bf16[2048,128]{1,0:T(8,128)(2,1)S(1)}, u32[]{:S(2)}, u32[]{:S(2)}) collective-permute-start(bf16[2048,128]{1,0:T(8,128)(2,1)} %bitcast.14), channel_id=1, source_target_pairs={{1,0},{2,1},{3,2},{0,3},{5,4},{6,5},{7,6},{4,7},{9,8},{10,9},{11,1... | collective-permute-start | bytes 1572872 | tf_op jit(solution)/shard_map/ppermute | solution.py:240
  15.7 1.9 %collective-permute-start.1 = (bf16[2048,128]{1,0:T(8,128)(2,1)}, bf16[2048,128]{1,0:T(8,128)(2,1)S(1)}, u32[]{:S(2)}, u32[]{:S(2)}) collective-permute-start(bf16[2048,128]{1,0:T(8,128)(2,1)} %bitcast.15), channel_id=1, source_target_pairs={{3,0},{0,1},{1,2},{2,3},{7,4},{4,5},{5,6},{6,7},{11,8},{8,9},{9,10... | collective-permute-start | bytes 1572872 | tf_op jit(solution)/shard_map/ppermute | solution.py:240
  17.6 4.2 %collective-permute-start.2 = (bf16[2048,128]{1,0:T(8,128)(2,1)}, bf16[2048,128]{1,0:T(8,128)(2,1)S(1)}, u32[]{:S(2)}, u32[]{:S(2)}) collective-permute-start(bf16[2048,128]{1,0:T(8,128)(2,1)} %bitcast.16), channel_id=1, source_target_pairs={{2,0},{3,1},{0,2},{1,3},{6,4},{7,5},{4,6},{5,7},{10,8},{11,9},{8,1... | collective-permute-start | bytes 1572872 | tf_op jit(solution)/shard_map/ppermute | solution.py:240
  21.8 0.0 collective-permute-done.3.y3
  21.9 3.3 %collective-permute-start.5 = (bf16[2048,128]{1,0:T(8,128)(2,1)}, bf16[2048,128]{1,0:T(8,128)(2,1)S(1)}, u32[]{:S(2)}, u32[]{:S(2)}) collective-permute-start(bf16[2048,128]{1,0:T(8,128)(2,1)} %bitcast.17), channel_id=1, source_target_pairs={{4,0},{8,4},{12,8},{0,12},{5,1},{9,5},{13,9},{1,13},{6,2},{10,6},{... | collective-permute-start | bytes 1572872 | tf_op jit(solution)/shard_map/ppermute | solution.py:240
  25.1 13.1 %all-to-all-start = ((f32[16,40,128]{2,1,0:T(8,128)}), f32[16,40,128]{2,1,0:T(8,128)S(1)}, u32[]{:S(2)}, u32[]{:S(2)}) async-start(f32[16,40,128]{2,1,0:T(8,128)} %project.1), calls=%async_computation | async-start | bytes 655360 | tf_op jit(solution)/shard_map/all_to_all | solution.py:244
  38.2 0.1 stack.23.pos_ref
  38.3 0.0 copy-start.2
  38.3 0.7 copy-done.2
  39.0 0.0 copy-start.3
  39.0 0.7 copy-done.3
  39.7 0.0 copy-start.4
  39.7 0.7 copy-done.4
  40.3 0.7 layout.1.local_ref
  41.1 6.2 %all-to-all-done.got_ref = f32[16,40,128]{2,1,0:T(8,128)S(1)} async-done(((f32[16,40,128]{2,1,0:T(8,128)}), f32[16,40,128]{2,1,0:T(8,128)S(1)}, u32[]{:S(2)}, u32[]{:S(2)}) %all-to-all-start) | async-done | bytes 327712 | tf_op jit(solution)/shard_map/all_to_all | solution.py:244
  47.3 0.0 copy-start
  47.3 1.0 %copy-done = bf16[256,8,128]{2,1,0:T(8,128)(2,1)S(1)} copy-done((bf16[256,8,128]{2,1,0:T(8,128)(2,1)S(1)}, bf16[256,8,128]{2,1,0:T(8,128)(2,1)}, u32[]{:S(2)}) %copy-start) | copy-done | bytes 524312
  48.3 0.5 weights.1
  48.8 0.0 collective-permute-done.4.y2
  48.8 0.0 collective-permute-done.x1
  48.8 0.0 collective-permute-done.1.x3
  48.8 0.0 collective-permute-done.2.x2
  48.8 1.3 %rows.1 = (bf16[512,2304]{1,0:T(8,128)(2,1)S(1)}, bf16[256,384]{1,0:T(8,128)(2,1)S(1)}) custom-call(f32[3,16,128]{2,1,0:T(8,128)S(1)} %get-tuple-element.17.w_ref, bf16[2048,128]{1,0:T(8,128)(2,1)S(1)} %bitcast.19, bf16[2048,128]{1,0:T(8,128)(2,1)S(1)} %collective-permute-done.x1, bf16[2048,128]{1,0:T(8,128)(2,1)S(1)} %collective-permute-done.1.x3, ...), custom_call_target="tpu_custom_call" | custom-call | flops 1000000000 | bytes 5000000 | tf_op jit(solution)/shard_map/rows/pallas_call | solution.py:291
  50.2 0.0 collective-permute-done.5.y1
  50.2 0.0 copy-start.1
  50.2 2.1 %hessian.1 = (f32[1024,128]{1,0:T(8,128)S(1)}, bf16[1040,128]{1,0:T(8,128)(2,1)S(1)}) custom-call(s32[5]{0:T(128)S(1)} %stack.23.pos_ref, f32[3,16,128]{2,1,0:T(8,128)S(1)} %get-tuple-element.17.w_ref, bf16[16,128]{1,0:T(8,128)(2,1)S(1)} %get-tuple-element.18.extra_ref, bf16[512,2304]{1,0:T(8,128)(2,1)S(1)} %get-tuple-element.19.right, ...), custom_call_target="tpu_custom_call" | custom-call | flops 1000000000 | bytes 5000000 | tf_op jit(solution)/shard_map/hessian/pallas_call | solution.py:303
  52.3 1.9 %collective-permute-start.6 = (bf16[1040,128]{1,0:T(8,128)(2,1)S(1)}, bf16[1040,128]{1,0:T(8,128)(2,1)S(1)}, u32[]{:S(2)}, u32[]{:S(2)}) collective-permute-start(bf16[1040,128]{1,0:T(8,128)(2,1)S(1)} %get-tuple-element.22), channel_id=1, source_target_pairs={{0,16},{16,0},{1,17},{17,1},{2,18},{18,2},{3,19},{19,3},{4,20},{20... | collective-permute-start | bytes 798728 | tf_op jit(solution)/shard_map/ppermute | solution.py:315
  54.3 1.5 %collective-permute-done.6.got_ref = bf16[1040,128]{1,0:T(8,128)(2,1)S(1)} collective-permute-done((bf16[1040,128]{1,0:T(8,128)(2,1)S(1)}, bf16[1040,128]{1,0:T(8,128)(2,1)S(1)}, u32[]{:S(2)}, u32[]{:S(2)}) %collective-permute-start.6) | collective-permute-done | bytes 266272 | tf_op jit(solution)/shard_map/ppermute | solution.py:315
  55.8 0.1 pair.1
  55.8 18.1 %all_to_all.15.got_ref = bf16[16,80,128]{2,1,0:T(8,128)(2,1)S(1)} all-to-all(bf16[16,80,128]{2,1,0:T(8,128)(2,1)S(1)} %pair.1), channel_id=1, replica_groups=mesh['zh'=4,'zl'=4,'core'=2,'y'=4,'x'=4] {'zl','y'}, dimensions={0} | all-to-all | bytes 655360 | tf_op jit(solution)/shard_map/all_to_all | solution.py:244
  73.9 0.6 plane.1
  74.5 26.5 %all_to_all.16.got_ref = bf16[4,80,128]{2,1,0:T(8,128)(2,1)S(1)} all-to-all(bf16[4,80,128]{2,1,0:T(8,128)(2,1)S(1)} %plane.1), channel_id=1, replica_groups=mesh['zh'=4,'zl'=4,'core'=2,'y'=4,'x'=4] {'zh'}, dimensions={0} | all-to-all | bytes 163840 | tf_op jit(solution)/shard_map/all_to_all | solution.py:244
  101.0 0.0 copy-done.1
  101.0 1.2 %finish.1 = (f32[3]{0:T(128)}, f32[1,128]{1,0:T(1,128)}, f32[64,128]{1,0:T(8,128)}) custom-call(s32[5]{0:T(128)S(1)} %stack.23.pos_ref, bf16[4,80,128]{2,1,0:T(8,128)(2,1)S(1)} %all_to_all.16.got_ref, f32[8,128]{1,0:T(8,128)S(1)} %get-tuple-element.23.sq_ref, f32[1,128]{1,0:T(1,128)S(1)} %bitcast.22), custom_call_target="tpu_custom_call" | custom-call | flops 1000000 | bytes 1000000 | tf_op jit(solution)/shard_map/finish/pallas_call | solution.py:334
Async XLA Ops:
  2.7 19.1 %collective-permute-start.3 = (bf16[2048,128]{1,0:T(8,128)(2,1)}, bf16[2048,128]{1,0:T(8,128)(2,1)S(1)}, u32[]{:S(2)}, u32[]{:S(2)}) collective-permute-start(bf16[2048,128]{1,0:T(8,128)(2,1)} %bitcast.12), channel_id=1, source_target_pairs={{12,0},{0,4},{4,8},{8,12},{13,1},{1,5},{5,9},{9,13},{14,2},{2,6},{... | collective-permute-start | bytes 1572872 | tf_op jit(solution)/shard_map/ppermute | solution.py:240
  6.2 42.6 %collective-permute-start.4 = (bf16[2048,128]{1,0:T(8,128)(2,1)}, bf16[2048,128]{1,0:T(8,128)(2,1)S(1)}, u32[]{:S(2)}, u32[]{:S(2)}) collective-permute-start(bf16[2048,128]{1,0:T(8,128)(2,1)} %bitcast.13), channel_id=1, source_target_pairs={{8,0},{12,4},{0,8},{4,12},{9,1},{13,5},{1,9},{5,13},{10,2},{14,6},... | collective-permute-start | bytes 1572872 | tf_op jit(solution)/shard_map/ppermute | solution.py:240
  11.0 37.8 %collective-permute-start = (bf16[2048,128]{1,0:T(8,128)(2,1)}, bf16[2048,128]{1,0:T(8,128)(2,1)S(1)}, u32[]{:S(2)}, u32[]{:S(2)}) collective-permute-start(bf16[2048,128]{1,0:T(8,128)(2,1)} %bitcast.14), channel_id=1, source_target_pairs={{1,0},{2,1},{3,2},{0,3},{5,4},{6,5},{7,6},{4,7},{9,8},{10,9},{11,1... | collective-permute-start | bytes 1572872 | tf_op jit(solution)/shard_map/ppermute | solution.py:240
  15.7 33.1 %collective-permute-start.1 = (bf16[2048,128]{1,0:T(8,128)(2,1)}, bf16[2048,128]{1,0:T(8,128)(2,1)S(1)}, u32[]{:S(2)}, u32[]{:S(2)}) collective-permute-start(bf16[2048,128]{1,0:T(8,128)(2,1)} %bitcast.15), channel_id=1, source_target_pairs={{3,0},{0,1},{1,2},{2,3},{7,4},{4,5},{5,6},{6,7},{11,8},{8,9},{9,10... | collective-permute-start | bytes 1572872 | tf_op jit(solution)/shard_map/ppermute | solution.py:240
  17.6 31.2 %collective-permute-start.2 = (bf16[2048,128]{1,0:T(8,128)(2,1)}, bf16[2048,128]{1,0:T(8,128)(2,1)S(1)}, u32[]{:S(2)}, u32[]{:S(2)}) collective-permute-start(bf16[2048,128]{1,0:T(8,128)(2,1)} %bitcast.16), channel_id=1, source_target_pairs={{2,0},{3,1},{0,2},{1,3},{6,4},{7,5},{4,6},{5,7},{10,8},{11,9},{8,1... | collective-permute-start | bytes 1572872 | tf_op jit(solution)/shard_map/ppermute | solution.py:240
  21.9 28.3 %collective-permute-start.5 = (bf16[2048,128]{1,0:T(8,128)(2,1)}, bf16[2048,128]{1,0:T(8,128)(2,1)S(1)}, u32[]{:S(2)}, u32[]{:S(2)}) collective-permute-start(bf16[2048,128]{1,0:T(8,128)(2,1)} %bitcast.17), channel_id=1, source_target_pairs={{4,0},{8,4},{12,8},{0,12},{5,1},{9,5},{13,9},{1,13},{6,2},{10,6},{... | collective-permute-start | bytes 1572872 | tf_op jit(solution)/shard_map/ppermute | solution.py:240
  25.1 22.1 %all-to-all-start = ((f32[16,40,128]{2,1,0:T(8,128)}), f32[16,40,128]{2,1,0:T(8,128)S(1)}, u32[]{:S(2)}, u32[]{:S(2)}) async-start(f32[16,40,128]{2,1,0:T(8,128)} %project.1), calls=%async_computation | async-start | bytes 655360 | tf_op jit(solution)/shard_map/all_to_all | solution.py:244
  38.3 0.7 copy-start.2
  39.0 0.7 copy-start.3
  39.7 0.7 copy-start.4
  47.3 1.0 %copy-start = (bf16[256,8,128]{2,1,0:T(8,128)(2,1)S(1)}, bf16[256,8,128]{2,1,0:T(8,128)(2,1)}, u32[]{:S(2)}) copy-start(bf16[256,8,128]{2,1,0:T(8,128)(2,1)} %param.7) | copy-start | bytes 1572868
  50.2 50.9 %copy-start.1 = (f32[128]{0:T(128)S(1)}, f32[128]{0:T(128)}, u32[]{:S(2)}) copy-start(f32[128]{0:T(128)} %param.9) | copy-start | bytes 1540
  52.3 3.4 %collective-permute-start.6 = (bf16[1040,128]{1,0:T(8,128)(2,1)S(1)}, bf16[1040,128]{1,0:T(8,128)(2,1)S(1)}, u32[]{:S(2)}, u32[]{:S(2)}) collective-permute-start(bf16[1040,128]{1,0:T(8,128)(2,1)S(1)} %get-tuple-element.22), channel_id=1, source_target_pairs={{0,16},{16,0},{1,17},{17,1},{2,18},{18,2},{3,19},{19,3},{4,20},{20... | collective-permute-start | bytes 798728 | tf_op jit(solution)/shard_map/ppermute | solution.py:315

commit v5 on v4

--- a/solution.py
+++ b/solution.py
@@ -86,7 +86,8 @@
     return x
 
 
-def layout_kernel(nominal_ref, counts_ref, steps_ref, out_ref):
+def layout_kernel(nominal_ref, counts_ref, steps_ref, own_ref, out_ref, near_ref):
+    near_ref[...] = own_ref[...]
     lane = lax.broadcasted_iota(jnp.int32, (CHUNKS, LANES), 1)
     place = lax.broadcasted_iota(jnp.int32, (CHUNKS, BINS_DEV), 1)
     line = lax.broadcasted_iota(jnp.int32, (CHUNKS, BINS_DEV), 0)
@@ -108,7 +109,7 @@
         out_ref[at : at + 1, :] = jnp.full((1, LANES), steps_ref[j], F32)
 
 
-def weights_kernel(got_ref, local_ref, v_ref, w_ref, bins_ref, sq_ref):
+def weights_kernel(got_ref, local_ref, w_ref, change_ref, sq_ref):
     total = jnp.sum(got_ref[...], axis=0)
     along_start = total[0:CHUNKS]
     along_dir = total[CHUNKS : 2 * CHUNKS]
@@ -132,12 +133,7 @@
     w_ref[0] = base
     w_ref[1] = left
     w_ref[2] = (counts / (base_total * base_total)) * base
-    grad = jnp.zeros((3, LANES), F32)
-    for c in range(CHUNKS):
-        row = jnp.concatenate(thirds(left[c : c + 1]), 0)
-        grad = grad + rows_dot(row, v_ref[c * LANES : (c + 1) * LANES, :])
-    grad = jnp.sum(grad, axis=0, keepdims=True)
-    bins_ref[...] = packed(jnp.concatenate([grad] + part, 0))
+    change_ref[...] = jnp.concatenate(part + [jnp.zeros((5, LANES), F32)], 0)
 
 
 def bin_mask():
@@ -151,8 +147,11 @@
     return (jac[0:16] + jac[16:32] + jac[32:48]).astype(BF16)
 
 
-def rows_kernel(w_ref, own, x1, x3, x2, y3, y2, right, jac_cols, jac_rows):
+def rows_kernel(
+    w_ref, change_ref, own, x1, x3, x2, y3, y2, right, jac_cols, extra_ref, jac_rows, grad
+):
     mine = bin_mask()
+    grad[...] = jnp.zeros((LANES, LANES), F32)
 
     def chunk(c, carry):
         span = pl.ds(pl.multiple_of(c * LANES, LANES), LANES)
@@ -163,11 +162,15 @@
         jac_cols[jac_span, :] = jacobian(base, mine, [ref[span, :] for ref in (own, y2, y3)])
         for step, rows in enumerate(across):
             scaled = rows.T.astype(F32) * left
+            if step == 0:
+                grad[...] += scaled
             right[step * LANES : (step + 1) * LANES, span] = scaled.astype(BF16)
         return carry
 
     lax.fori_loop(0, CHUNKS, chunk, 0, unroll=4)
     right[:, ROWS:] = jac_rows[...].T
+    total = jnp.sum(grad[...].T, axis=0, keepdims=True)
+    extra_ref[...] = packed(jnp.concatenate([total, change_ref[0:3, :]], 0))
 
 
 def hessian_kernel(
@@ -264,42 +267,45 @@
     own, sent = lax.optimization_barrier((own, sent))
     x2, y2, x3, y3, x1, y1 = (from_ahead(own, axis, k) for k in (2, 3, 1) for axis in ("x", "y"))
     got = exchanged(sent, ("y", "x"))
-    local = pl.pallas_call(
+    local, near_own = pl.pallas_call(
         layout_kernel,
-        out_shape=jax.ShapeDtypeStruct((40, LANES), F32),
-        in_specs=[VMEM, VMEM, SMEM],
-        out_specs=VMEM,
+        out_shape=arrays_of(((40, LANES), F32), ((ROWS, LANES), BF16)),
+        in_specs=[VMEM, VMEM, SMEM, VMEM],
+        out_specs=(VMEM, VMEM),
         compiler_params=PARAMS,
         cost_estimate=cost(10_000_000, 1_000_000),
         name="layout",
-    )(log_nominal.T, observed[None, :], step_lengths)
-    weights, extra, squares = pl.pallas_call(
+    )(log_nominal.T, observed[None, :], step_lengths, own)
+    weights, changes, squares = pl.pallas_call(
         weights_kernel,
         out_shape=arrays_of(
-            ((3, CHUNKS, LANES), F32), ((16, LANES), BF16), ((8, LANES), F32)
+            ((3, CHUNKS, LANES), F32), ((8, LANES), F32), ((8, LANES), F32)
         ),
-        in_specs=[VMEM, VMEM, VMEM],
+        in_specs=[VMEM, VMEM],
         out_specs=(VMEM, VMEM, VMEM),
         compiler_params=PARAMS,
         cost_estimate=cost(10_000_000, 1_000_000),
         name="weights",
-    )(got, local, own)
+    )(got, local)
     px, py = lax.axis_index("x"), lax.axis_index("y")
     core = lax.axis_index("core")
     block = lax.axis_index(("zh", "zl", "core"))
     position = jnp.stack([px, py, block, py * SIDE + px, core]).astype(jnp.int32)
-    right, jac_cols = pl.pallas_call(
+    right, jac_cols, extra = pl.pallas_call(
         rows_kernel,
         out_shape=arrays_of(
-            ((SIDE * LANES, DEPTH), BF16), ((BINS_DEV, 3 * LANES), BF16)
+            ((SIDE * LANES, DEPTH), BF16), ((BINS_DEV, 3 * LANES), BF16), ((16, LANES), BF16)
         ),
-        in_specs=[VMEM] * 7,
-        out_specs=(VMEM, VMEM),
-        scratch_shapes=[pltpu.VMEM((BINS_DEV, SIDE * LANES), BF16)],
+        in_specs=[VMEM] * 8,
+        out_specs=(VMEM, VMEM, VMEM),
+        scratch_shapes=[
+            pltpu.VMEM((BINS_DEV, SIDE * LANES), BF16),
+            pltpu.VMEM((LANES, LANES), F32),
+        ],
         compiler_params=PARAMS,
         cost_estimate=cost(1_000_000_000, 5_000_000),
         name="rows",
-    )(weights, own, x1, x3, x2, y3, y2)
+    )(weights, changes, near_own, x1, x3, x2, y3, y2)
     kept, other = pl.pallas_call(
         hessian_kernel,
         out_shape=arrays_of(
@@ -311,7 +317,7 @@
         compiler_params=PARAMS,
         cost_estimate=cost(1_000_000_000, 5_000_000),
         name="hessian",
-    )(position, weights, extra, right, jac_cols, own, y2, y3, y1)
+    )(position, weights, extra, right, jac_cols, near_own, y2, y3, y1)
     swapped = lax.ppermute(other, "core", [(0, 1), (1, 0)])
     pair = pl.pallas_call(
         pair_kernel,

time: 103 us -> 103 us (level)
  waiting for transfers between devices: 7.69 us -> 6.61 us
    all_to_all x1, waiting for transfers between devices: 6.16 us -> 5.09 us  [exchanged(): return lax.all_to_all(array, axes, 0, 0, tiled=True)]
    pallas_call x1, Pallas kernels: 1.31 us -> 2.36 us  [body(): pl.pallas_call(rows_kernel, out_shape=arrays_of(((SIDE * LANES, DEPTH), B...]
  transfers between devices with their start and end apart: 8 -> 8, of which waited for: 2 -> 2; matrix products, arithmetic and copies ran while one was open for 0% -> 0% of each run, Pallas kernels for 2% -> 3%
where the time goes in v5:
time: 103 us; the launch traced here: 102 us
  blocking collectives  44.6 us (43%)
  starting transfers between devices  37.3 us (36%)
  Pallas kernels  9.46 us (9%)
  waiting for transfers between devices  6.61 us (6%)
  local copies, waits for them, and re-layouts  3.16 us (3%)
    all_to_all x2, blocking collectives, exchanged(): return lax.all_to_all(array, axes, 0, 0, tiled=True)  44.6 us
    ppermute x6, starting transfers between devices, from_ahead(): lax.ppermute(array, axis, [((i + step) % SIDE, i) for i in range(SIDE)])  22.3 us
    all_to_all x1, starting transfers between devices, exchanged(): return lax.all_to_all(array, axes, 0, 0, tiled=True)  13.1 us
    all_to_all x1, waiting for transfers between devices, exchanged(): return lax.all_to_all(array, axes, 0, 0, tiled=True)  5.09 us
    unnamed x10, local copies, waits for them, and re-layouts  3.08 us
    pallas_call x1, Pallas kernels, body(): pl.pallas_call(rows_kernel, out_shape=arrays_of(((SIDE * LANES, DEPTH), B...  2.36 us
    pallas_call x1, Pallas kernels, body(): pl.pallas_call(hessian_kernel, out_shape=arrays_of(((PIECES * 64, LANES),...  2.11 us
    pallas_call x1, Pallas kernels, body(): pl.pallas_call(project_kernel, out_shape=jax.ShapeDtypeStruct((16, 40, LA...  2.1 us
  transfers between devices with their start and end apart: 8, of which 2 were waited for; matrix products, arithmetic and copies ran while one was open for 0% of the time, Pallas kernels for 3%

profile of v5, /device:TPU:32, one launch (start us, length us, event | category | flops | bytes accessed | tf_op | source)
XLA Modules:
  0.0 102.0 jit_solution(3736353243622535201)
XLA Ops:
  0.6 2.1 %project.1 = f32[16,40,128]{2,1,0:T(8,128)} custom-call(bf16[2048,128]{1,0:T(8,128)(2,1)} %bitcast.11, f32[1,128]{1,0:T(1,128)} %bitcast.20, f32[1,128]{1,0:T(1,128)} %bitcast.23), custom_call_target="tpu_custom_call" | custom-call | flops 10000000 | bytes 1000000 | tf_op jit(solution)/shard_map/project/pallas_call | solution.py:252
  2.7 3.5 %collective-permute-start.3 = (bf16[2048,128]{1,0:T(8,128)(2,1)}, bf16[2048,128]{1,0:T(8,128)(2,1)S(1)}, u32[]{:S(2)}, u32[]{:S(2)}) collective-permute-start(bf16[2048,128]{1,0:T(8,128)(2,1)} %bitcast.12), channel_id=1, source_target_pairs={{12,0},{0,4},{4,8},{8,12},{13,1},{1,5},{5,9},{9,13},{14,2},{2,6},{... | collective-permute-start | bytes 1572872 | tf_op jit(solution)/shard_map/ppermute | solution.py:243
  6.2 4.8 %collective-permute-start.4 = (bf16[2048,128]{1,0:T(8,128)(2,1)}, bf16[2048,128]{1,0:T(8,128)(2,1)S(1)}, u32[]{:S(2)}, u32[]{:S(2)}) collective-permute-start(bf16[2048,128]{1,0:T(8,128)(2,1)} %bitcast.13), channel_id=1, source_target_pairs={{8,0},{12,4},{0,8},{4,12},{9,1},{13,5},{1,9},{5,13},{10,2},{14,6},... | collective-permute-start | bytes 1572872 | tf_op jit(solution)/shard_map/ppermute | solution.py:243
  11.1 4.7 %collective-permute-start = (bf16[2048,128]{1,0:T(8,128)(2,1)}, bf16[2048,128]{1,0:T(8,128)(2,1)S(1)}, u32[]{:S(2)}, u32[]{:S(2)}) collective-permute-start(bf16[2048,128]{1,0:T(8,128)(2,1)} %bitcast.14), channel_id=1, source_target_pairs={{1,0},{2,1},{3,2},{0,3},{5,4},{6,5},{7,6},{4,7},{9,8},{10,9},{11,1... | collective-permute-start | bytes 1572872 | tf_op jit(solution)/shard_map/ppermute | solution.py:243
  15.7 1.9 %collective-permute-start.1 = (bf16[2048,128]{1,0:T(8,128)(2,1)}, bf16[2048,128]{1,0:T(8,128)(2,1)S(1)}, u32[]{:S(2)}, u32[]{:S(2)}) collective-permute-start(bf16[2048,128]{1,0:T(8,128)(2,1)} %bitcast.15), channel_id=1, source_target_pairs={{3,0},{0,1},{1,2},{2,3},{7,4},{4,5},{5,6},{6,7},{11,8},{8,9},{9,10... | collective-permute-start | bytes 1572872 | tf_op jit(solution)/shard_map/ppermute | solution.py:243
  17.7 4.2 %collective-permute-start.2 = (bf16[2048,128]{1,0:T(8,128)(2,1)}, bf16[2048,128]{1,0:T(8,128)(2,1)}, u32[]{:S(2)}, u32[]{:S(2)}) collective-permute-start(bf16[2048,128]{1,0:T(8,128)(2,1)} %bitcast.16), channel_id=1, source_target_pairs={{2,0},{3,1},{0,2},{1,3},{6,4},{7,5},{4,6},{5,7},{10,8},{11,9},{8,1... | collective-permute-start | bytes 1572872 | tf_op jit(solution)/shard_map/ppermute | solution.py:243
  21.9 0.0 collective-permute-done.3.y3
  21.9 3.3 %collective-permute-start.5 = (bf16[2048,128]{1,0:T(8,128)(2,1)}, bf16[2048,128]{1,0:T(8,128)(2,1)S(1)}, u32[]{:S(2)}, u32[]{:S(2)}) collective-permute-start(bf16[2048,128]{1,0:T(8,128)(2,1)} %bitcast.17), channel_id=1, source_target_pairs={{4,0},{8,4},{12,8},{0,12},{5,1},{9,5},{13,9},{1,13},{6,2},{10,6},{... | collective-permute-start | bytes 1572872 | tf_op jit(solution)/shard_map/ppermute | solution.py:243
  25.1 13.1 %all-to-all-start = ((f32[16,40,128]{2,1,0:T(8,128)}), f32[16,40,128]{2,1,0:T(8,128)S(1)}, u32[]{:S(2)}, u32[]{:S(2)}) async-start(f32[16,40,128]{2,1,0:T(8,128)} %project.1), calls=%async_computation | async-start | bytes 655360 | tf_op jit(solution)/shard_map/all_to_all | solution.py:247
  38.2 0.1 stack.23.pos_ref
  38.3 0.0 copy-start
  38.3 1.0 %copy-done = bf16[256,8,128]{2,1,0:T(8,128)(2,1)S(1)} copy-done((bf16[256,8,128]{2,1,0:T(8,128)(2,1)S(1)}, bf16[256,8,128]{2,1,0:T(8,128)(2,1)}, u32[]{:S(2)}) %copy-start) | copy-done | bytes 524312
  39.4 0.0 copy-start.1
  39.4 0.7 copy-done.1
  40.1 0.0 copy-start.3
  40.1 0.7 copy-done.3
  40.7 0.0 copy-start.4
  40.7 0.7 copy-done.4
  41.4 0.8 layout.1
  42.2 5.1 %all-to-all-done.got_ref = f32[16,40,128]{2,1,0:T(8,128)S(1)} async-done(((f32[16,40,128]{2,1,0:T(8,128)}), f32[16,40,128]{2,1,0:T(8,128)S(1)}, u32[]{:S(2)}, u32[]{:S(2)}) %all-to-all-start) | async-done | bytes 327712 | tf_op jit(solution)/shard_map/all_to_all | solution.py:247
  47.3 0.3 weights.1
  47.5 0.0 collective-permute-done.4.y2
  47.6 0.0 collective-permute-done.x1
  47.6 0.0 collective-permute-done.1.x3
  47.6 0.0 collective-permute-done.2.x2
  47.6 2.4 %rows.1 = (bf16[512,2304]{1,0:T(8,128)(2,1)S(1)}, bf16[256,384]{1,0:T(8,128)(2,1)S(1)}, bf16[16,128]{1,0:T(8,128)(2,1)S(1)}) custom-call(f32[3,16,128]{2,1,0:T(8,128)S(1)} %get-tuple-element.21.w_ref, f32[8,128]{1,0:T(8,128)S(1)} %get-tuple-element.22.change_ref, bf16[2048,128]{1,0:T(8,128)(2,1)S(1)} %get-tuple-element.23.own, ...), custom_call_target="tpu_custom_call" | custom-call | flops 1000000000 | bytes 5000000 | tf_op jit(solution)/shard_map/rows/pallas_call | solution.py:294
  50.0 0.0 collective-permute-done.5.y1
  50.0 0.0 copy-start.2
  50.0 2.1 %hessian.1 = (f32[1024,128]{1,0:T(8,128)S(1)}, bf16[1040,128]{1,0:T(8,128)(2,1)S(1)}) custom-call(s32[5]{0:T(128)S(1)} %stack.23.pos_ref, f32[3,16,128]{2,1,0:T(8,128)S(1)} %get-tuple-element.21.w_ref, bf16[16,128]{1,0:T(8,128)(2,1)S(1)} %get-tuple-element.24.extra_ref, bf16[512,2304]{1,0:T(8,128)(2,1)S(1)} %get-tuple-element.25.right, ...), custom_call_target="tpu_custom_call" | custom-call | flops 1000000000 | bytes 5000000 | tf_op jit(solution)/shard_map/hessian/pallas_call | solution.py:309
  52.1 1.9 %collective-permute-start.6 = (bf16[1040,128]{1,0:T(8,128)(2,1)S(1)}, bf16[1040,128]{1,0:T(8,128)(2,1)S(1)}, u32[]{:S(2)}, u32[]{:S(2)}) collective-permute-start(bf16[1040,128]{1,0:T(8,128)(2,1)S(1)} %get-tuple-element.28), channel_id=1, source_target_pairs={{0,16},{16,0},{1,17},{17,1},{2,18},{18,2},{3,19},{19,3},{4,20},{20... | collective-permute-start | bytes 798728 | tf_op jit(solution)/shard_map/ppermute | solution.py:321
  54.0 1.5 %collective-permute-done.6.got_ref = bf16[1040,128]{1,0:T(8,128)(2,1)S(1)} collective-permute-done((bf16[1040,128]{1,0:T(8,128)(2,1)S(1)}, bf16[1040,128]{1,0:T(8,128)(2,1)S(1)}, u32[]{:S(2)}, u32[]{:S(2)}) %collective-permute-start.6) | collective-permute-done | bytes 266272 | tf_op jit(solution)/shard_map/ppermute | solution.py:321
  55.5 0.1 pair.1
  55.6 18.1 %all_to_all.15.got_ref = bf16[16,80,128]{2,1,0:T(8,128)(2,1)S(1)} all-to-all(bf16[16,80,128]{2,1,0:T(8,128)(2,1)S(1)} %pair.1), channel_id=1, replica_groups=mesh['zh'=4,'zl'=4,'core'=2,'y'=4,'x'=4] {'zl','y'}, dimensions={0} | all-to-all | bytes 655360 | tf_op jit(solution)/shard_map/all_to_all | solution.py:247
  73.7 0.6 plane.1
  74.3 26.5 %all_to_all.16.got_ref = bf16[4,80,128]{2,1,0:T(8,128)(2,1)S(1)} all-to-all(bf16[4,80,128]{2,1,0:T(8,128)(2,1)S(1)} %plane.1), channel_id=1, replica_groups=mesh['zh'=4,'zl'=4,'core'=2,'y'=4,'x'=4] {'zh'}, dimensions={0} | all-to-all | bytes 163840 | tf_op jit(solution)/shard_map/all_to_all | solution.py:247
  100.8 0.0 copy-done.2
  100.8 1.2 %finish.1 = (f32[3]{0:T(128)}, f32[1,128]{1,0:T(1,128)}, f32[64,128]{1,0:T(8,128)}) custom-call(s32[5]{0:T(128)S(1)} %stack.23.pos_ref, bf16[4,80,128]{2,1,0:T(8,128)(2,1)S(1)} %all_to_all.16.got_ref, f32[8,128]{1,0:T(8,128)S(1)} %get-tuple-element.29.sq_ref, f32[1,128]{1,0:T(1,128)S(1)} %bitcast.21), custom_call_target="tpu_custom_call" | custom-call | flops 1000000 | bytes 1000000 | tf_op jit(solution)/shard_map/finish/pallas_call | solution.py:340
Async XLA Ops:
  2.7 19.1 %collective-permute-start.3 = (bf16[2048,128]{1,0:T(8,128)(2,1)}, bf16[2048,128]{1,0:T(8,128)(2,1)S(1)}, u32[]{:S(2)}, u32[]{:S(2)}) collective-permute-start(bf16[2048,128]{1,0:T(8,128)(2,1)} %bitcast.12), channel_id=1, source_target_pairs={{12,0},{0,4},{4,8},{8,12},{13,1},{1,5},{5,9},{9,13},{14,2},{2,6},{... | collective-permute-start | bytes 1572872 | tf_op jit(solution)/shard_map/ppermute | solution.py:243
  6.2 41.3 %collective-permute-start.4 = (bf16[2048,128]{1,0:T(8,128)(2,1)}, bf16[2048,128]{1,0:T(8,128)(2,1)S(1)}, u32[]{:S(2)}, u32[]{:S(2)}) collective-permute-start(bf16[2048,128]{1,0:T(8,128)(2,1)} %bitcast.13), channel_id=1, source_target_pairs={{8,0},{12,4},{0,8},{4,12},{9,1},{13,5},{1,9},{5,13},{10,2},{14,6},... | collective-permute-start | bytes 1572872 | tf_op jit(solution)/shard_map/ppermute | solution.py:243
  11.1 36.5 %collective-permute-start = (bf16[2048,128]{1,0:T(8,128)(2,1)}, bf16[2048,128]{1,0:T(8,128)(2,1)S(1)}, u32[]{:S(2)}, u32[]{:S(2)}) collective-permute-start(bf16[2048,128]{1,0:T(8,128)(2,1)} %bitcast.14), channel_id=1, source_target_pairs={{1,0},{2,1},{3,2},{0,3},{5,4},{6,5},{7,6},{4,7},{9,8},{10,9},{11,1... | collective-permute-start | bytes 1572872 | tf_op jit(solution)/shard_map/ppermute | solution.py:243
  15.7 31.8 %collective-permute-start.1 = (bf16[2048,128]{1,0:T(8,128)(2,1)}, bf16[2048,128]{1,0:T(8,128)(2,1)S(1)}, u32[]{:S(2)}, u32[]{:S(2)}) collective-permute-start(bf16[2048,128]{1,0:T(8,128)(2,1)} %bitcast.15), channel_id=1, source_target_pairs={{3,0},{0,1},{1,2},{2,3},{7,4},{4,5},{5,6},{6,7},{11,8},{8,9},{9,10... | collective-permute-start | bytes 1572872 | tf_op jit(solution)/shard_map/ppermute | solution.py:243
  17.7 29.9 %collective-permute-start.2 = (bf16[2048,128]{1,0:T(8,128)(2,1)}, bf16[2048,128]{1,0:T(8,128)(2,1)}, u32[]{:S(2)}, u32[]{:S(2)}) collective-permute-start(bf16[2048,128]{1,0:T(8,128)(2,1)} %bitcast.16), channel_id=1, source_target_pairs={{2,0},{3,1},{0,2},{1,3},{6,4},{7,5},{4,6},{5,7},{10,8},{11,9},{8,1... | collective-permute-start | bytes 1572872 | tf_op jit(solution)/shard_map/ppermute | solution.py:243
  21.9 28.1 %collective-permute-start.5 = (bf16[2048,128]{1,0:T(8,128)(2,1)}, bf16[2048,128]{1,0:T(8,128)(2,1)S(1)}, u32[]{:S(2)}, u32[]{:S(2)}) collective-permute-start(bf16[2048,128]{1,0:T(8,128)(2,1)} %bitcast.17), channel_id=1, source_target_pairs={{4,0},{8,4},{12,8},{0,12},{5,1},{9,5},{13,9},{1,13},{6,2},{10,6},{... | collective-permute-start | bytes 1572872 | tf_op jit(solution)/shard_map/ppermute | solution.py:243
  25.1 22.1 %all-to-all-start = ((f32[16,40,128]{2,1,0:T(8,128)}), f32[16,40,128]{2,1,0:T(8,128)S(1)}, u32[]{:S(2)}, u32[]{:S(2)}) async-start(f32[16,40,128]{2,1,0:T(8,128)} %project.1), calls=%async_computation | async-start | bytes 655360 | tf_op jit(solution)/shard_map/all_to_all | solution.py:247
  38.3 1.0 %copy-start = (bf16[256,8,128]{2,1,0:T(8,128)(2,1)S(1)}, bf16[256,8,128]{2,1,0:T(8,128)(2,1)}, u32[]{:S(2)}) copy-start(bf16[256,8,128]{2,1,0:T(8,128)(2,1)} %param.7) | copy-start | bytes 1572868
  39.4 0.7 copy-start.1
  40.1 0.7 copy-start.3
  40.7 0.7 copy-start.4
  50.0 50.8 %copy-start.2 = (f32[128]{0:T(128)S(1)}, f32[128]{0:T(128)}, u32[]{:S(2)}) copy-start(f32[128]{0:T(128)} %param.9) | copy-start | bytes 1540
  52.1 3.4 %collective-permute-start.6 = (bf16[1040,128]{1,0:T(8,128)(2,1)S(1)}, bf16[1040,128]{1,0:T(8,128)(2,1)S(1)}, u32[]{:S(2)}, u32[]{:S(2)}) collective-permute-start(bf16[1040,128]{1,0:T(8,128)(2,1)S(1)} %get-tuple-element.28), channel_id=1, source_target_pairs={{0,16},{16,0},{1,17},{17,1},{2,18},{18,2},{3,19},{19,3},{4,20},{20... | collective-permute-start | bytes 798728 | tf_op jit(solution)/shard_map/ppermute | solution.py:321

commit v6 on v5

--- a/solution.py
+++ b/solution.py
@@ -50,7 +50,7 @@
     return wide[..., 0:4, :] + wide[..., 4:8, :] + wide[..., 8:12, :]
 
 
-def project_kernel(v_ref, start_ref, dir_ref, out_ref, flat, rows, ends, sems):
+def project_kernel(v_ref, start_ref, dir_ref, out_ref, rows, flat, ends, sems):
     moves = [
         pltpu.make_async_copy(start_ref, ends.at[0:1], sems.at[0]),
         pltpu.make_async_copy(dir_ref, ends.at[1:2], sems.at[1]),
@@ -86,8 +86,7 @@
     return x
 
 
-def layout_kernel(nominal_ref, counts_ref, steps_ref, own_ref, out_ref, near_ref):
-    near_ref[...] = own_ref[...]
+def layout_kernel(nominal_ref, counts_ref, steps_ref, out_ref):
     lane = lax.broadcasted_iota(jnp.int32, (CHUNKS, LANES), 1)
     place = lax.broadcasted_iota(jnp.int32, (CHUNKS, BINS_DEV), 1)
     line = lax.broadcasted_iota(jnp.int32, (CHUNKS, BINS_DEV), 0)
@@ -148,7 +147,7 @@
 
 
 def rows_kernel(
-    w_ref, change_ref, own, x1, x3, x2, y3, y2, right, jac_cols, extra_ref, jac_rows, grad
+    w_ref, change_ref, own, xa, xb, xr, ya, right, jac_cols, extra_ref, jac_rows, grad
 ):
     mine = bin_mask()
     grad[...] = jnp.zeros((LANES, LANES), F32)
@@ -157,9 +156,9 @@
         span = pl.ds(pl.multiple_of(c * LANES, LANES), LANES)
         jac_span = pl.ds(pl.multiple_of(c * 16, 16), 16)
         base, left, curve = (w_ref[k, pl.ds(c, 1), :] for k in range(3))
-        across = [ref[span, :] for ref in (own, x1, x2, x3)]
+        across = [ref[span, :] for ref in (own, xa, xb, xr)]
         jac_rows[jac_span, :] = jacobian(curve, mine, across)
-        jac_cols[jac_span, :] = jacobian(base, mine, [ref[span, :] for ref in (own, y2, y3)])
+        jac_cols[jac_span, :] = jacobian(base, mine, [ref[span, :] for ref in (own, ya)])
         for step, rows in enumerate(across):
             scaled = rows.T.astype(F32) * left
             if step == 0:
@@ -174,26 +173,27 @@
 
 
 def hessian_kernel(
-    pos_ref, w_ref, extra_ref, right, jac_ref, own, y2, y3, y1, kept_ref, sent_ref, jac_last
+    pos_ref, w_ref, extra_ref, right, jac_ref, own, ya, yb, yr, kept_ref, sent_ref, jac_last
 ):
     px, py, core = pos_ref[0], pos_ref[1], pos_ref[4]
     mine = bin_mask()
     for c in range(CHUNKS):
-        rows = y1[c * LANES : (c + 1) * LANES, :]
-        jac_last[c * 16 : (c + 1) * 16, :] = jacobian(w_ref[0, c : c + 1, :], mine, [rows])
-    jacs = [jac_ref[:, k * LANES : (k + 1) * LANES] for k in range(3)] + [jac_last[...]]
-    steps = ((own, 0), (y2, 2), (y3, 3), (y1, 1))
+        rows = [ref[c * LANES : (c + 1) * LANES, :] for ref in (yb, yr)]
+        jac_last[c * 16 : (c + 1) * 16, :] = jacobian(w_ref[0, c : c + 1, :], mine, rows)
+    jacs = [ref[:, k * LANES : (k + 1) * LANES] for ref in (jac_ref, jac_last) for k in range(2)]
+    steps = (0, 1 + 2 * core, 3 - 2 * core, 2)
+    cols_in = (own, ya, yb, yr)
     for n in range(2):
         cols = [
-            jnp.concatenate([steps[k][0][...], jacs[k]], 0) for k in (2 * n, 2 * n + 1)
+            jnp.concatenate([cols_in[k][...], jacs[k]], 0) for k in (2 * n, 2 * n + 1)
         ]
         term = rows_dot(right[...], jnp.concatenate(cols, 1))
         for i in range(SIDE):
-            row_at = lax.rem(px + i, SIDE)
+            row_at = lax.rem(px + steps[i], SIDE)
             for half in range(2):
                 part = term[i * LANES : (i + 1) * LANES, half * LANES : (half + 1) * LANES]
                 first, second = part[0:64], part[64:]
-                col_at = lax.rem(py + steps[2 * n + half][1], SIDE)
+                col_at = lax.rem(py + steps[2 * n + half], SIDE)
                 at = pl.ds(pl.multiple_of((row_at * SIDE + col_at) * 64, 64), 64)
                 kept_ref[at, :] = jnp.where(core == 0, first, second)
                 sent_ref[at, :] = jnp.where(core == 0, second, first).astype(BF16)
@@ -235,12 +235,20 @@
         line_ref[j] = jnp.sum(extra[1 + j : 2 + j, :] + 0.5 * sq_ref[j : j + 1, :]) * scale
 
 
+def in_hbm(array):
+    return pltpu.with_memory_space_constraint(array, pltpu.HBM)
+
+
 def arrays_of(*shapes):
     return tuple(jax.ShapeDtypeStruct(s, d) for s, d in shapes)
 
 
-def from_ahead(array, axis, step):
-    return lax.ppermute(array, axis, [((i + step) % SIDE, i) for i in range(SIDE)])
+def around(array, axis, way):
+    pairs = []
+    for core in range(2):
+        step = way if core == 0 else -way
+        pairs += [(core * SIDE + (i + step) % SIDE, core * SIDE + i) for i in range(SIDE)]
+    return lax.ppermute(array, ("core", axis), pairs)
 
 
 def exchanged(array, axes):
@@ -249,33 +257,33 @@
 
 def body(log_nominal, variations, observed, start, direction, step_lengths):
     own = variations.reshape(ROWS, LANES)
-    sent = pl.pallas_call(
+    sent, own = pl.pallas_call(
         project_kernel,
-        out_shape=jax.ShapeDtypeStruct((16, 40, LANES), F32),
+        out_shape=arrays_of(((16, 40, LANES), F32), ((ROWS, LANES), BF16)),
         in_specs=[HBM, HBM, HBM],
-        out_specs=VMEM,
+        out_specs=(VMEM, VMEM),
         scratch_shapes=[
             pltpu.VMEM((40, LANES), F32),
-            pltpu.VMEM((ROWS, LANES), BF16),
             pltpu.VMEM((8, LANES), F32),
             pltpu.SemaphoreType.DMA((3,)),
         ],
-        compiler_params=pltpu.CompilerParams(vmem_limit_bytes=62 * 1024 * 1024),
+        compiler_params=PARAMS,
         cost_estimate=cost(10_000_000, 1_000_000),
         name="project",
-    )(own, start[None, :], direction[None, :])
-    own, sent = lax.optimization_barrier((own, sent))
-    x2, y2, x3, y3, x1, y1 = (from_ahead(own, axis, k) for k in (2, 3, 1) for axis in ("x", "y"))
+    )(in_hbm(own), in_hbm(start[None, :]), in_hbm(direction[None, :]))
+    xa, ya = (around(own, axis, 1) for axis in ("x", "y"))
+    xb, yb = (around(own, axis, -1) for axis in ("x", "y"))
+    xr, yr = (around(got, axis, 1) for got, axis in ((xa, "x"), (ya, "y")))
     got = exchanged(sent, ("y", "x"))
-    local, near_own = pl.pallas_call(
+    local = pl.pallas_call(
         layout_kernel,
-        out_shape=arrays_of(((40, LANES), F32), ((ROWS, LANES), BF16)),
-        in_specs=[VMEM, VMEM, SMEM, VMEM],
-        out_specs=(VMEM, VMEM),
+        out_shape=jax.ShapeDtypeStruct((40, LANES), F32),
+        in_specs=[VMEM, VMEM, SMEM],
+        out_specs=VMEM,
         compiler_params=PARAMS,
         cost_estimate=cost(10_000_000, 1_000_000),
         name="layout",
-    )(log_nominal.T, observed[None, :], step_lengths, own)
+    )(*map(in_hbm, (log_nominal.T, observed[None, :], step_lengths)))
     weights, changes, squares = pl.pallas_call(
         weights_kernel,
         out_shape=arrays_of(
@@ -294,9 +302,9 @@
     right, jac_cols, extra = pl.pallas_call(
         rows_kernel,
         out_shape=arrays_of(
-            ((SIDE * LANES, DEPTH), BF16), ((BINS_DEV, 3 * LANES), BF16), ((16, LANES), BF16)
+            ((SIDE * LANES, DEPTH), BF16), ((BINS_DEV, 2 * LANES), BF16), ((16, LANES), BF16)
         ),
-        in_specs=[VMEM] * 8,
+        in_specs=[VMEM] * 7,
         out_specs=(VMEM, VMEM, VMEM),
         scratch_shapes=[
             pltpu.VMEM((BINS_DEV, SIDE * LANES), BF16),
@@ -305,7 +313,7 @@
         compiler_params=PARAMS,
         cost_estimate=cost(1_000_000_000, 5_000_000),
         name="rows",
-    )(weights, changes, near_own, x1, x3, x2, y3, y2)
+    )(weights, changes, own, xa, xb, xr, ya)
     kept, other = pl.pallas_call(
         hessian_kernel,
         out_shape=arrays_of(
@@ -313,11 +321,11 @@
         ),
         in_specs=[SMEM] + [VMEM] * 8,
         out_specs=(VMEM, VMEM),
-        scratch_shapes=[pltpu.VMEM((BINS_DEV, LANES), BF16)],
+        scratch_shapes=[pltpu.VMEM((BINS_DEV, 2 * LANES), BF16)],
         compiler_params=PARAMS,
         cost_estimate=cost(1_000_000_000, 5_000_000),
         name="hessian",
-    )(position, weights, extra, right, jac_cols, near_own, y2, y3, y1)
+    )(position, weights, extra, right, jac_cols, own, ya, yb, yr)
     swapped = lax.ppermute(other, "core", [(0, 1), (1, 0)])
     pair = pl.pallas_call(
         pair_kernel,

time: 103 us -> 96.5 us (0.937)
  starting transfers between devices: 37.3 us -> 30.7 us
  waiting for transfers between devices: 6.61 us -> 10.7 us
  local copies, waits for them, and re-layouts: 3.16 us -> 0.09 us
    all_to_all x1, starting transfers between devices: 13.1 us -> 3.55 us  [exchanged(): return lax.all_to_all(array, axes, 0, 0, tiled=True)]
    unnamed x10 -> x2, local copies, waits for them, and re-layouts: 3.08 us -> 0.01 us
    ppermute x6, starting transfers between devices: 22.3 us -> 25.2 us  [around(): return lax.ppermute(array, ('core', axis), pairs)]
    all_to_all x1, waiting for transfers between devices: 5.09 us -> 7.89 us  [exchanged(): return lax.all_to_all(array, axes, 0, 0, tiled=True)]
    ppermute x6, waiting for transfers between devices: 0.02 us -> 1.25 us  [around(): return lax.ppermute(array, ('core', axis), pairs)]
  transfers between devices with their start and end apart: 8 -> 8, of which waited for: 2 -> 3; matrix products, arithmetic and copies ran while one was open for 0% -> 0% of each run, Pallas kernels for 3% -> 4%
where the time goes in v6:
time: 96.5 us; the launch traced here: 96 us
  blocking collectives  44.1 us (46%)
  starting transfers between devices  30.7 us (32%)
  waiting for transfers between devices  10.7 us (11%)
  Pallas kernels  9.56 us (10%)
    all_to_all x2, blocking collectives, exchanged(): return lax.all_to_all(array, axes, 0, 0, tiled=True)  44.1 us
    ppermute x6, starting transfers between devices, around(): return lax.ppermute(array, ('core', axis), pairs)  25.2 us
    all_to_all x1, waiting for transfers between devices, exchanged(): return lax.all_to_all(array, axes, 0, 0, tiled=True)  7.89 us
    all_to_all x1, starting transfers between devices, exchanged(): return lax.all_to_all(array, axes, 0, 0, tiled=True)  3.55 us
    pallas_call x1, Pallas kernels, body(): pl.pallas_call(rows_kernel, out_shape=arrays_of(((SIDE * LANES, DEPTH), B...  2.23 us
    pallas_call x1, Pallas kernels, body(): pl.pallas_call(hessian_kernel, out_shape=arrays_of(((PIECES * 64, LANES),...  2.13 us
    pallas_call x1, Pallas kernels, body(): pl.pallas_call(project_kernel, out_shape=arrays_of(((16, 40, LANES), F32)...  2.09 us
  transfers between devices with their start and end apart: 8, of which 3 were waited for; matrix products, arithmetic and copies ran while one was open for 0% of the time, Pallas kernels for 4%

profile of v6, /device:TPU:32, one launch (start us, length us, event | category | flops | bytes accessed | tf_op | source)
XLA Modules:
  0.0 96.0 jit_solution(8326317191337093085)
XLA Ops:
  0.6 2.1 %project.1 = (f32[16,40,128]{2,1,0:T(8,128)}, bf16[2048,128]{1,0:T(8,128)(2,1)S(1)}) custom-call(bf16[2048,128]{1,0:T(8,128)(2,1)} %bitcast.13, f32[1,128]{1,0:T(1,128)} %bitcast.11, f32[1,128]{1,0:T(1,128)} %bitcast.14), custom_call_target="tpu_custom_call" | custom-call | flops 10000000 | bytes 1000000 | tf_op jit(solution)/shard_map/project/pallas_call | solution.py:260
  2.7 4.7 %collective-permute-start = (bf16[2048,128]{1,0:T(8,128)(2,1)S(1)}, bf16[2048,128]{1,0:T(8,128)(2,1)S(1)}, u32[]{:S(2)}, u32[]{:S(2)}) collective-permute-start(bf16[2048,128]{1,0:T(8,128)(2,1)S(1)} %get-tuple-element.19.own), channel_id=1, source_target_pairs={{1,0},{2,1},{3,2},{0,3},{19,16},{16,17},{17,18},{18,19},{5,4},{6,5... | collective-permute-start | bytes 1572872 | tf_op jit(solution)/shard_map/ppermute | solution.py:251
  7.4 4.9 %collective-permute-start.3 = (bf16[2048,128]{1,0:T(8,128)(2,1)S(1)}, bf16[2048,128]{1,0:T(8,128)(2,1)S(1)}, u32[]{:S(2)}, u32[]{:S(2)}) collective-permute-start(bf16[2048,128]{1,0:T(8,128)(2,1)S(1)} %get-tuple-element.19.own), channel_id=1, source_target_pairs={{4,0},{8,4},{12,8},{0,12},{28,16},{16,20},{20,24},{24,28},{5,1},{9... | collective-permute-start | bytes 1572872 | tf_op jit(solution)/shard_map/ppermute | solution.py:251
  12.3 1.9 %collective-permute-start.1 = (bf16[2048,128]{1,0:T(8,128)(2,1)S(1)}, bf16[2048,128]{1,0:T(8,128)(2,1)S(1)}, u32[]{:S(2)}, u32[]{:S(2)}) collective-permute-start(bf16[2048,128]{1,0:T(8,128)(2,1)S(1)} %get-tuple-element.19.own), channel_id=1, source_target_pairs={{3,0},{0,1},{1,2},{2,3},{17,16},{18,17},{19,18},{16,19},{7,4},{4,5... | collective-permute-start | bytes 1572872 | tf_op jit(solution)/shard_map/ppermute | solution.py:251
  14.3 1.2 %collective-permute-done.xa = bf16[2048,128]{1,0:T(8,128)(2,1)S(1)} collective-permute-done((bf16[2048,128]{1,0:T(8,128)(2,1)S(1)}, bf16[2048,128]{1,0:T(8,128)(2,1)S(1)}, u32[]{:S(2)}, u32[]{:S(2)}) %collective-permute-start) | collective-permute-done | bytes 524320 | tf_op jit(solution)/shard_map/ppermute | solution.py:251
  15.5 5.6 %collective-permute-start.2 = (bf16[2048,128]{1,0:T(8,128)(2,1)S(1)}, bf16[2048,128]{1,0:T(8,128)(2,1)}, u32[]{:S(2)}, u32[]{:S(2)}) collective-permute-start(bf16[2048,128]{1,0:T(8,128)(2,1)S(1)} %collective-permute-done.xa), channel_id=1, source_target_pairs={{1,0},{2,1},{3,2},{0,3},{19,16},{16,17},{17,18},{18,19},{5,4},{6,5... | collective-permute-start | bytes 1572872 | tf_op jit(solution)/shard_map/ppermute | solution.py:251
  21.1 3.5 %collective-permute-start.4 = (bf16[2048,128]{1,0:T(8,128)(2,1)S(1)}, bf16[2048,128]{1,0:T(8,128)(2,1)S(1)}, u32[]{:S(2)}, u32[]{:S(2)}) collective-permute-start(bf16[2048,128]{1,0:T(8,128)(2,1)S(1)} %get-tuple-element.19.own), channel_id=1, source_target_pairs={{12,0},{0,4},{4,8},{8,12},{20,16},{24,20},{28,24},{16,28},{13,1},{... | collective-permute-start | bytes 1572872 | tf_op jit(solution)/shard_map/ppermute | solution.py:251
  24.6 0.0 collective-permute-done.3.ya
  24.6 4.6 %collective-permute-start.5 = (bf16[2048,128]{1,0:T(8,128)(2,1)S(1)}, bf16[2048,128]{1,0:T(8,128)(2,1)S(1)}, u32[]{:S(2)}, u32[]{:S(2)}) collective-permute-start(bf16[2048,128]{1,0:T(8,128)(2,1)S(1)} %collective-permute-done.3.ya), channel_id=1, source_target_pairs={{4,0},{8,4},{12,8},{0,12},{28,16},{16,20},{20,24},{24,28},{5,1},{9... | collective-permute-start | bytes 1572872 | tf_op jit(solution)/shard_map/ppermute | solution.py:251
  29.3 3.6 %all-to-all-start = ((f32[16,40,128]{2,1,0:T(8,128)}), f32[16,40,128]{2,1,0:T(8,128)S(1)}, u32[]{:S(2)}, u32[]{:S(2)}) async-start(f32[16,40,128]{2,1,0:T(8,128)} %get-tuple-element.16), calls=%async_computation | async-start | bytes 655360 | tf_op jit(solution)/shard_map/all_to_all | solution.py:255
  32.8 0.1 stack.23.pos_ref
  32.9 1.0 %layout.1.local_ref = f32[40,128]{1,0:T(8,128)S(1)} custom-call(f32[8,256]{1,0:T(8,128)} %bitcast.15, s32[1,256]{1,0:T(1,128)} %bitcast.16, f32[3]{0:T(128)} %steps_ref.1), custom_call_target="tpu_custom_call" | custom-call | flops 10000000 | bytes 1000000 | tf_op jit(solution)/shard_map/layout/pallas_call | solution.py:278
  33.9 7.9 %all-to-all-done.got_ref = f32[16,40,128]{2,1,0:T(8,128)S(1)} async-done(((f32[16,40,128]{2,1,0:T(8,128)}), f32[16,40,128]{2,1,0:T(8,128)S(1)}, u32[]{:S(2)}, u32[]{:S(2)}) %all-to-all-start) | async-done | bytes 327712 | tf_op jit(solution)/shard_map/all_to_all | solution.py:255
  41.8 0.3 weights.1
  42.1 0.0 collective-permute-done.1.xb
  42.1 0.0 collective-permute-done.2.xr
  42.1 2.2 %rows.1 = (bf16[512,2304]{1,0:T(8,128)(2,1)S(1)}, bf16[256,256]{1,0:T(8,128)(2,1)S(1)}, bf16[16,128]{1,0:T(8,128)(2,1)S(1)}) custom-call(f32[3,16,128]{2,1,0:T(8,128)S(1)} %get-tuple-element.17.w_ref, f32[8,128]{1,0:T(8,128)S(1)} %get-tuple-element.18.change_ref, bf16[2048,128]{1,0:T(8,128)(2,1)S(1)} %get-tuple-element.19.own, ...), custom_call_target="tpu_custom_call" | custom-call | flops 1000000000 | bytes 5000000 | tf_op jit(solution)/shard_map/rows/pallas_call | solution.py:302
  44.4 0.0 collective-permute-done.4.yb
  44.4 0.0 collective-permute-done.5.yr
  44.4 0.0 copy-start
  44.4 2.1 %hessian.1 = (f32[1024,128]{1,0:T(8,128)S(1)}, bf16[1040,128]{1,0:T(8,128)(2,1)S(1)}) custom-call(s32[5]{0:T(128)S(1)} %stack.23.pos_ref, f32[3,16,128]{2,1,0:T(8,128)S(1)} %get-tuple-element.17.w_ref, bf16[16,128]{1,0:T(8,128)(2,1)S(1)} %get-tuple-element.20.extra_ref, bf16[512,2304]{1,0:T(8,128)(2,1)S(1)} %get-tuple-element.21.right, ...), custom_call_target="tpu_custom_call" | custom-call | flops 1000000000 | bytes 5000000 | tf_op jit(solution)/shard_map/hessian/pallas_call | solution.py:317
  46.5 1.9 %collective-permute-start.6 = (bf16[1040,128]{1,0:T(8,128)(2,1)S(1)}, bf16[1040,128]{1,0:T(8,128)(2,1)S(1)}, u32[]{:S(2)}, u32[]{:S(2)}) collective-permute-start(bf16[1040,128]{1,0:T(8,128)(2,1)S(1)} %get-tuple-element.24), channel_id=1, source_target_pairs={{0,16},{16,0},{1,17},{17,1},{2,18},{18,2},{3,19},{19,3},{4,20},{20... | collective-permute-start | bytes 798728 | tf_op jit(solution)/shard_map/ppermute | solution.py:329
  48.5 1.5 %collective-permute-done.6.got_ref = bf16[1040,128]{1,0:T(8,128)(2,1)S(1)} collective-permute-done((bf16[1040,128]{1,0:T(8,128)(2,1)S(1)}, bf16[1040,128]{1,0:T(8,128)(2,1)S(1)}, u32[]{:S(2)}, u32[]{:S(2)}) %collective-permute-start.6) | collective-permute-done | bytes 266272 | tf_op jit(solution)/shard_map/ppermute | solution.py:329
  50.0 0.1 pair.1
  50.0 18.2 %all_to_all.15.got_ref = bf16[16,80,128]{2,1,0:T(8,128)(2,1)S(1)} all-to-all(bf16[16,80,128]{2,1,0:T(8,128)(2,1)S(1)} %pair.1), channel_id=1, replica_groups=mesh['zh'=4,'zl'=4,'core'=2,'y'=4,'x'=4] {'zl','y'}, dimensions={0} | all-to-all | bytes 655360 | tf_op jit(solution)/shard_map/all_to_all | solution.py:255
  68.3 0.6 plane.1
  68.9 25.9 %all_to_all.16.got_ref = bf16[4,80,128]{2,1,0:T(8,128)(2,1)S(1)} all-to-all(bf16[4,80,128]{2,1,0:T(8,128)(2,1)S(1)} %plane.1), channel_id=1, replica_groups=mesh['zh'=4,'zl'=4,'core'=2,'y'=4,'x'=4] {'zh'}, dimensions={0} | all-to-all | bytes 163840 | tf_op jit(solution)/shard_map/all_to_all | solution.py:255
  94.8 0.0 copy-done
  94.8 1.2 %finish.1 = (f32[3]{0:T(128)}, f32[1,128]{1,0:T(1,128)}, f32[64,128]{1,0:T(8,128)}) custom-call(s32[5]{0:T(128)S(1)} %stack.23.pos_ref, bf16[4,80,128]{2,1,0:T(8,128)(2,1)S(1)} %all_to_all.16.got_ref, f32[8,128]{1,0:T(8,128)S(1)} %get-tuple-element.25.sq_ref, f32[1,128]{1,0:T(1,128)S(1)} %bitcast.12), custom_call_target="tpu_custom_call" | custom-call | flops 1000000 | bytes 1000000 | tf_op jit(solution)/shard_map/finish/pallas_call | solution.py:348
Async XLA Ops:
  2.7 12.8 %collective-permute-start = (bf16[2048,128]{1,0:T(8,128)(2,1)S(1)}, bf16[2048,128]{1,0:T(8,128)(2,1)S(1)}, u32[]{:S(2)}, u32[]{:S(2)}) collective-permute-start(bf16[2048,128]{1,0:T(8,128)(2,1)S(1)} %get-tuple-element.19.own), channel_id=1, source_target_pairs={{1,0},{2,1},{3,2},{0,3},{19,16},{16,17},{17,18},{18,19},{5,4},{6,5... | collective-permute-start | bytes 1572872 | tf_op jit(solution)/shard_map/ppermute | solution.py:251
  7.4 17.2 %collective-permute-start.3 = (bf16[2048,128]{1,0:T(8,128)(2,1)S(1)}, bf16[2048,128]{1,0:T(8,128)(2,1)S(1)}, u32[]{:S(2)}, u32[]{:S(2)}) collective-permute-start(bf16[2048,128]{1,0:T(8,128)(2,1)S(1)} %get-tuple-element.19.own), channel_id=1, source_target_pairs={{4,0},{8,4},{12,8},{0,12},{28,16},{16,20},{20,24},{24,28},{5,1},{9... | collective-permute-start | bytes 1572872 | tf_op jit(solution)/shard_map/ppermute | solution.py:251
  12.3 29.8 %collective-permute-start.1 = (bf16[2048,128]{1,0:T(8,128)(2,1)S(1)}, bf16[2048,128]{1,0:T(8,128)(2,1)S(1)}, u32[]{:S(2)}, u32[]{:S(2)}) collective-permute-start(bf16[2048,128]{1,0:T(8,128)(2,1)S(1)} %get-tuple-element.19.own), channel_id=1, source_target_pairs={{3,0},{0,1},{1,2},{2,3},{17,16},{18,17},{19,18},{16,19},{7,4},{4,5... | collective-permute-start | bytes 1572872 | tf_op jit(solution)/shard_map/ppermute | solution.py:251
  15.5 26.6 %collective-permute-start.2 = (bf16[2048,128]{1,0:T(8,128)(2,1)S(1)}, bf16[2048,128]{1,0:T(8,128)(2,1)}, u32[]{:S(2)}, u32[]{:S(2)}) collective-permute-start(bf16[2048,128]{1,0:T(8,128)(2,1)S(1)} %collective-permute-done.xa), channel_id=1, source_target_pairs={{1,0},{2,1},{3,2},{0,3},{19,16},{16,17},{17,18},{18,19},{5,4},{6,5... | collective-permute-start | bytes 1572872 | tf_op jit(solution)/shard_map/ppermute | solution.py:251
  21.1 23.3 %collective-permute-start.4 = (bf16[2048,128]{1,0:T(8,128)(2,1)S(1)}, bf16[2048,128]{1,0:T(8,128)(2,1)S(1)}, u32[]{:S(2)}, u32[]{:S(2)}) collective-permute-start(bf16[2048,128]{1,0:T(8,128)(2,1)S(1)} %get-tuple-element.19.own), channel_id=1, source_target_pairs={{12,0},{0,4},{4,8},{8,12},{20,16},{24,20},{28,24},{16,28},{13,1},{... | collective-permute-start | bytes 1572872 | tf_op jit(solution)/shard_map/ppermute | solution.py:251
  24.6 19.8 %collective-permute-start.5 = (bf16[2048,128]{1,0:T(8,128)(2,1)S(1)}, bf16[2048,128]{1,0:T(8,128)(2,1)S(1)}, u32[]{:S(2)}, u32[]{:S(2)}) collective-permute-start(bf16[2048,128]{1,0:T(8,128)(2,1)S(1)} %collective-permute-done.3.ya), channel_id=1, source_target_pairs={{4,0},{8,4},{12,8},{0,12},{28,16},{16,20},{20,24},{24,28},{5,1},{9... | collective-permute-start | bytes 1572872 | tf_op jit(solution)/shard_map/ppermute | solution.py:251
  29.3 12.6 %all-to-all-start = ((f32[16,40,128]{2,1,0:T(8,128)}), f32[16,40,128]{2,1,0:T(8,128)S(1)}, u32[]{:S(2)}, u32[]{:S(2)}) async-start(f32[16,40,128]{2,1,0:T(8,128)} %get-tuple-element.16), calls=%async_computation | async-start | bytes 655360 | tf_op jit(solution)/shard_map/all_to_all | solution.py:255
  44.4 50.4 %copy-start = (f32[128]{0:T(128)S(1)}, f32[128]{0:T(128)}, u32[]{:S(2)}) copy-start(f32[128]{0:T(128)} %param.9) | copy-start | bytes 1540
  46.5 3.4 %collective-permute-start.6 = (bf16[1040,128]{1,0:T(8,128)(2,1)S(1)}, bf16[1040,128]{1,0:T(8,128)(2,1)S(1)}, u32[]{:S(2)}, u32[]{:S(2)}) collective-permute-start(bf16[1040,128]{1,0:T(8,128)(2,1)S(1)} %get-tuple-element.24), channel_id=1, source_target_pairs={{0,16},{16,0},{1,17},{17,1},{2,18},{18,2},{3,19},{19,3},{4,20},{20... | collective-permute-start | bytes 798728 | tf_op jit(solution)/shard_map/ppermute | solution.py:329

commit v7 on v6

--- a/solution.py
+++ b/solution.py
@@ -146,8 +146,25 @@
     return (jac[0:16] + jac[16:32] + jac[32:48]).astype(BF16)
 
 
+def product(pos_ref, right, blocks, jacs, first, kept_ref, sent_ref):
+    px, py, core = pos_ref[0], pos_ref[1], pos_ref[4]
+    steps = (0, 1 + 2 * core, 3 - 2 * core, 2)
+    cols = [jnp.concatenate([b[...], jacs[:, k * LANES : (k + 1) * LANES]], 0) for k, b in enumerate(blocks)]
+    term = rows_dot(right[...], jnp.concatenate(cols, 1))
+    for i in range(SIDE):
+        row_at = lax.rem(px + steps[i], SIDE)
+        for half in range(2):
+            part = term[i * LANES : (i + 1) * LANES, half * LANES : (half + 1) * LANES]
+            upper, lower = part[0:64], part[64:]
+            col_at = lax.rem(py + steps[first + half], SIDE)
+            at = pl.ds(pl.multiple_of((row_at * SIDE + col_at) * 64, 64), 64)
+            kept_ref[at, :] = jnp.where(core == 0, upper, lower)
+            sent_ref[at, :] = jnp.where(core == 0, lower, upper).astype(BF16)
+
+
 def rows_kernel(
-    w_ref, change_ref, own, xa, xb, xr, ya, right, jac_cols, extra_ref, jac_rows, grad
+    pos_ref, w_ref, change_ref, own, xa, xb, xr, ya, right, extra_ref, kept_ref, sent_ref,
+    jac_rows, jac_cols, grad,
 ):
     mine = bin_mask()
     grad[...] = jnp.zeros((LANES, LANES), F32)
@@ -169,35 +186,20 @@
     lax.fori_loop(0, CHUNKS, chunk, 0, unroll=4)
     right[:, ROWS:] = jac_rows[...].T
     total = jnp.sum(grad[...].T, axis=0, keepdims=True)
-    extra_ref[...] = packed(jnp.concatenate([total, change_ref[0:3, :]], 0))
+    extra = packed(jnp.concatenate([total, change_ref[0:3, :]], 0))
+    extra_ref[...] = extra
+    product(pos_ref, right, (own, ya), jac_cols, 0, kept_ref, sent_ref)
+    sent_ref[PIECES * 64 :, :] = extra
 
 
 def hessian_kernel(
-    pos_ref, w_ref, extra_ref, right, jac_ref, own, ya, yb, yr, kept_ref, sent_ref, jac_last
+    pos_ref, w_ref, right, yb, yr, kept_in, sent_in, kept_ref, sent_ref, jac_cols
 ):
-    px, py, core = pos_ref[0], pos_ref[1], pos_ref[4]
     mine = bin_mask()
     for c in range(CHUNKS):
         rows = [ref[c * LANES : (c + 1) * LANES, :] for ref in (yb, yr)]
-        jac_last[c * 16 : (c + 1) * 16, :] = jacobian(w_ref[0, c : c + 1, :], mine, rows)
-    jacs = [ref[:, k * LANES : (k + 1) * LANES] for ref in (jac_ref, jac_last) for k in range(2)]
-    steps = (0, 1 + 2 * core, 3 - 2 * core, 2)
-    cols_in = (own, ya, yb, yr)
-    for n in range(2):
-        cols = [
-            jnp.concatenate([cols_in[k][...], jacs[k]], 0) for k in (2 * n, 2 * n + 1)
-        ]
-        term = rows_dot(right[...], jnp.concatenate(cols, 1))
-        for i in range(SIDE):
-            row_at = lax.rem(px + steps[i], SIDE)
-            for half in range(2):
-                part = term[i * LANES : (i + 1) * LANES, half * LANES : (half + 1) * LANES]
-                first, second = part[0:64], part[64:]
-                col_at = lax.rem(py + steps[2 * n + half], SIDE)
-                at = pl.ds(pl.multiple_of((row_at * SIDE + col_at) * 64, 64), 64)
-                kept_ref[at, :] = jnp.where(core == 0, first, second)
-                sent_ref[at, :] = jnp.where(core == 0, second, first).astype(BF16)
-    sent_ref[PIECES * 64 :, :] = extra_ref[...]
+        jac_cols[c * 16 : (c + 1) * 16, :] = jacobian(w_ref[0, c : c + 1, :], mine, rows)
+    product(pos_ref, right, (yb, yr), jac_cols, 2, kept_ref, sent_ref)
 
 
 def pair_kernel(kept_ref, extra_ref, got_ref, out_ref):
@@ -299,33 +301,32 @@
     core = lax.axis_index("core")
     block = lax.axis_index(("zh", "zl", "core"))
     position = jnp.stack([px, py, block, py * SIDE + px, core]).astype(jnp.int32)
-    right, jac_cols, extra = pl.pallas_call(
+    tiles = arrays_of(((PIECES * 64, LANES), F32), ((PIECES * 64 + 16, LANES), BF16))
+    right, extra, kept, other = pl.pallas_call(
         rows_kernel,
-        out_shape=arrays_of(
-            ((SIDE * LANES, DEPTH), BF16), ((BINS_DEV, 2 * LANES), BF16), ((16, LANES), BF16)
-        ),
-        in_specs=[VMEM] * 7,
-        out_specs=(VMEM, VMEM, VMEM),
+        out_shape=arrays_of(((SIDE * LANES, DEPTH), BF16), ((16, LANES), BF16)) + tiles,
+        in_specs=[SMEM] + [VMEM] * 7,
+        out_specs=(VMEM, VMEM, VMEM, VMEM),
         scratch_shapes=[
             pltpu.VMEM((BINS_DEV, SIDE * LANES), BF16),
+            pltpu.VMEM((BINS_DEV, 2 * LANES), BF16),
             pltpu.VMEM((LANES, LANES), F32),
         ],
         compiler_params=PARAMS,
-        cost_estimate=cost(1_000_000_000, 5_000_000),
+        cost_estimate=cost(1_500_000_000, 5_000_000),
         name="rows",
-    )(weights, changes, own, xa, xb, xr, ya)
+    )(position, weights, changes, own, xa, xb, xr, ya)
     kept, other = pl.pallas_call(
         hessian_kernel,
-        out_shape=arrays_of(
-            ((PIECES * 64, LANES), F32), ((PIECES * 64 + 16, LANES), BF16)
-        ),
-        in_specs=[SMEM] + [VMEM] * 8,
+        out_shape=tiles,
+        in_specs=[SMEM] + [VMEM] * 6,
         out_specs=(VMEM, VMEM),
         scratch_shapes=[pltpu.VMEM((BINS_DEV, 2 * LANES), BF16)],
+        input_output_aliases={5: 0, 6: 1},
         compiler_params=PARAMS,
         cost_estimate=cost(1_000_000_000, 5_000_000),
         name="hessian",
-    )(position, weights, extra, right, jac_cols, own, ya, yb, yr)
+    )(position, weights, right, yb, yr, kept, other)
     swapped = lax.ppermute(other, "core", [(0, 1), (1, 0)])
     pair = pl.pallas_call(
         pair_kernel,

time: 96.5 us -> 96.5 us (level)
  no operation moved by 1% of the time
where the time goes in v7:
time: 96.5 us; the launch traced here: 95.9 us
  blocking collectives  44.1 us (46%)
  starting transfers between devices  30.7 us (32%)
  waiting for transfers between devices  10.7 us (11%)
  Pallas kernels  9.52 us (10%)
    all_to_all x2, blocking collectives, exchanged(): return lax.all_to_all(array, axes, 0, 0, tiled=True)  44.1 us
    ppermute x6, starting transfers between devices, around(): return lax.ppermute(array, ('core', axis), pairs)  25.2 us
    all_to_all x1, waiting for transfers between devices, exchanged(): return lax.all_to_all(array, axes, 0, 0, tiled=True)  7.89 us
    all_to_all x1, starting transfers between devices, exchanged(): return lax.all_to_all(array, axes, 0, 0, tiled=True)  3.55 us
    pallas_call x1, Pallas kernels, body(): pl.pallas_call(rows_kernel, out_shape=arrays_of(((SIDE * LANES, DEPTH), B...  2.83 us
    pallas_call x1, Pallas kernels, body(): pl.pallas_call(project_kernel, out_shape=arrays_of(((16, 40, LANES), F32)...  2.09 us
  transfers between devices with their start and end apart: 8, of which 3 were waited for; matrix products, arithmetic and copies ran while one was open for 0% of the time, Pallas kernels for 4%

profile of v7, /device:TPU:32, one launch (start us, length us, event | category | flops | bytes accessed | tf_op | source)
XLA Modules:
  0.0 95.9 jit_solution(7049712072993210897)
XLA Ops:
  0.6 2.1 %project.1 = (f32[16,40,128]{2,1,0:T(8,128)}, bf16[2048,128]{1,0:T(8,128)(2,1)S(1)}) custom-call(bf16[2048,128]{1,0:T(8,128)(2,1)} %bitcast.13, f32[1,128]{1,0:T(1,128)} %bitcast.11, f32[1,128]{1,0:T(1,128)} %bitcast.14), custom_call_target="tpu_custom_call" | custom-call | flops 10000000 | bytes 1000000 | tf_op jit(solution)/shard_map/project/pallas_call | solution.py:262
  2.7 4.7 %collective-permute-start = (bf16[2048,128]{1,0:T(8,128)(2,1)S(1)}, bf16[2048,128]{1,0:T(8,128)(2,1)S(1)}, u32[]{:S(2)}, u32[]{:S(2)}) collective-permute-start(bf16[2048,128]{1,0:T(8,128)(2,1)S(1)} %get-tuple-element.20.own), channel_id=1, source_target_pairs={{1,0},{2,1},{3,2},{0,3},{19,16},{16,17},{17,18},{18,19},{5,4},{6,5... | collective-permute-start | bytes 1572872 | tf_op jit(solution)/shard_map/ppermute | solution.py:253
  7.4 4.9 %collective-permute-start.3 = (bf16[2048,128]{1,0:T(8,128)(2,1)S(1)}, bf16[2048,128]{1,0:T(8,128)(2,1)S(1)}, u32[]{:S(2)}, u32[]{:S(2)}) collective-permute-start(bf16[2048,128]{1,0:T(8,128)(2,1)S(1)} %get-tuple-element.20.own), channel_id=1, source_target_pairs={{4,0},{8,4},{12,8},{0,12},{28,16},{16,20},{20,24},{24,28},{5,1},{9... | collective-permute-start | bytes 1572872 | tf_op jit(solution)/shard_map/ppermute | solution.py:253
  12.3 1.9 %collective-permute-start.1 = (bf16[2048,128]{1,0:T(8,128)(2,1)S(1)}, bf16[2048,128]{1,0:T(8,128)(2,1)S(1)}, u32[]{:S(2)}, u32[]{:S(2)}) collective-permute-start(bf16[2048,128]{1,0:T(8,128)(2,1)S(1)} %get-tuple-element.20.own), channel_id=1, source_target_pairs={{3,0},{0,1},{1,2},{2,3},{17,16},{18,17},{19,18},{16,19},{7,4},{4,5... | collective-permute-start | bytes 1572872 | tf_op jit(solution)/shard_map/ppermute | solution.py:253
  14.3 1.2 %collective-permute-done.xa = bf16[2048,128]{1,0:T(8,128)(2,1)S(1)} collective-permute-done((bf16[2048,128]{1,0:T(8,128)(2,1)S(1)}, bf16[2048,128]{1,0:T(8,128)(2,1)S(1)}, u32[]{:S(2)}, u32[]{:S(2)}) %collective-permute-start) | collective-permute-done | bytes 524320 | tf_op jit(solution)/shard_map/ppermute | solution.py:253
  15.5 5.6 %collective-permute-start.2 = (bf16[2048,128]{1,0:T(8,128)(2,1)S(1)}, bf16[2048,128]{1,0:T(8,128)(2,1)}, u32[]{:S(2)}, u32[]{:S(2)}) collective-permute-start(bf16[2048,128]{1,0:T(8,128)(2,1)S(1)} %collective-permute-done.xa), channel_id=1, source_target_pairs={{1,0},{2,1},{3,2},{0,3},{19,16},{16,17},{17,18},{18,19},{5,4},{6,5... | collective-permute-start | bytes 1572872 | tf_op jit(solution)/shard_map/ppermute | solution.py:253
  21.1 3.5 %collective-permute-start.4 = (bf16[2048,128]{1,0:T(8,128)(2,1)S(1)}, bf16[2048,128]{1,0:T(8,128)(2,1)S(1)}, u32[]{:S(2)}, u32[]{:S(2)}) collective-permute-start(bf16[2048,128]{1,0:T(8,128)(2,1)S(1)} %get-tuple-element.20.own), channel_id=1, source_target_pairs={{12,0},{0,4},{4,8},{8,12},{20,16},{24,20},{28,24},{16,28},{13,1},{... | collective-permute-start | bytes 1572872 | tf_op jit(solution)/shard_map/ppermute | solution.py:253
  24.6 0.0 collective-permute-done.3.ya
  24.6 4.6 %collective-permute-start.5 = (bf16[2048,128]{1,0:T(8,128)(2,1)S(1)}, bf16[2048,128]{1,0:T(8,128)(2,1)S(1)}, u32[]{:S(2)}, u32[]{:S(2)}) collective-permute-start(bf16[2048,128]{1,0:T(8,128)(2,1)S(1)} %collective-permute-done.3.ya), channel_id=1, source_target_pairs={{4,0},{8,4},{12,8},{0,12},{28,16},{16,20},{20,24},{24,28},{5,1},{9... | collective-permute-start | bytes 1572872 | tf_op jit(solution)/shard_map/ppermute | solution.py:253
  29.3 3.6 %all-to-all-start = ((f32[16,40,128]{2,1,0:T(8,128)}), f32[16,40,128]{2,1,0:T(8,128)S(1)}, u32[]{:S(2)}, u32[]{:S(2)}) async-start(f32[16,40,128]{2,1,0:T(8,128)} %get-tuple-element.17), calls=%async_computation | async-start | bytes 655360 | tf_op jit(solution)/shard_map/all_to_all | solution.py:257
  32.8 0.1 stack.23.pos_ref
  32.9 1.0 %layout.1.local_ref = f32[40,128]{1,0:T(8,128)S(1)} custom-call(f32[8,256]{1,0:T(8,128)} %bitcast.15, s32[1,256]{1,0:T(1,128)} %bitcast.16, f32[3]{0:T(128)} %steps_ref.1), custom_call_target="tpu_custom_call" | custom-call | flops 10000000 | bytes 1000000 | tf_op jit(solution)/shard_map/layout/pallas_call | solution.py:280
  33.9 7.9 %all-to-all-done.got_ref = f32[16,40,128]{2,1,0:T(8,128)S(1)} async-done(((f32[16,40,128]{2,1,0:T(8,128)}), f32[16,40,128]{2,1,0:T(8,128)S(1)}, u32[]{:S(2)}, u32[]{:S(2)}) %all-to-all-start) | async-done | bytes 327712 | tf_op jit(solution)/shard_map/all_to_all | solution.py:257
  41.8 0.3 weights.1
  42.1 0.0 collective-permute-done.1.xb
  42.1 0.0 collective-permute-done.2.xr
  42.1 2.8 %rows.1 = (bf16[512,2304]{1,0:T(8,128)(2,1)S(1)}, bf16[16,128]{1,0:T(8,128)(2,1)S(1)}, f32[1024,128]{1,0:T(8,128)S(1)}, bf16[1040,128]{1,0:T(8,128)(2,1)S(1)}) custom-call(s32[5]{0:T(128)S(1)} %stack.23.pos_ref, f32[3,16,128]{2,1,0:T(8,128)S(1)} %get-tuple-element.18.w_ref, f32[8,128]{1,0:T(8,128)S(1)} %get-tuple-element.19.change_ref, ...), custom_call_target="tpu_custom_call" | custom-call | flops 1500000000 | bytes 5000000 | tf_op jit(solution)/shard_map/rows/pallas_call | solution.py:305
  45.0 0.0 collective-permute-done.4.yb
  45.0 0.0 collective-permute-done.5.yr
  45.0 0.0 copy-start
  45.0 1.5 %hessian.1 = (f32[1024,128]{1,0:T(8,128)S(1)}, bf16[1040,128]{1,0:T(8,128)(2,1)S(1)}) custom-call(s32[5]{0:T(128)S(1)} %stack.23.pos_ref, f32[3,16,128]{2,1,0:T(8,128)S(1)} %get-tuple-element.18.w_ref, bf16[512,2304]{1,0:T(8,128)(2,1)S(1)} %get-tuple-element.21.right, ...), custom_call_target="tpu_custom_call", output_to_operand_aliasing={{0}: (5, {}), {1}: (6, {})} | custom-call | flops 1000000000 | bytes 5000000 | tf_op jit(solution)/shard_map/hessian/pallas_call | solution.py:319
  46.5 1.9 %collective-permute-start.6 = (bf16[1040,128]{1,0:T(8,128)(2,1)S(1)}, bf16[1040,128]{1,0:T(8,128)(2,1)S(1)}, u32[]{:S(2)}, u32[]{:S(2)}) collective-permute-start(bf16[1040,128]{1,0:T(8,128)(2,1)S(1)} %get-tuple-element.26), channel_id=1, source_target_pairs={{0,16},{16,0},{1,17},{17,1},{2,18},{18,2},{3,19},{19,3},{4,20},{20... | collective-permute-start | bytes 798728 | tf_op jit(solution)/shard_map/ppermute | solution.py:330
  48.4 1.5 %collective-permute-done.6.got_ref = bf16[1040,128]{1,0:T(8,128)(2,1)S(1)} collective-permute-done((bf16[1040,128]{1,0:T(8,128)(2,1)S(1)}, bf16[1040,128]{1,0:T(8,128)(2,1)S(1)}, u32[]{:S(2)}, u32[]{:S(2)}) %collective-permute-start.6) | collective-permute-done | bytes 266272 | tf_op jit(solution)/shard_map/ppermute | solution.py:330
  49.9 0.1 pair.1
  50.0 18.2 %all_to_all.15.got_ref = bf16[16,80,128]{2,1,0:T(8,128)(2,1)S(1)} all-to-all(bf16[16,80,128]{2,1,0:T(8,128)(2,1)S(1)} %pair.1), channel_id=1, replica_groups=mesh['zh'=4,'zl'=4,'core'=2,'y'=4,'x'=4] {'zl','y'}, dimensions={0} | all-to-all | bytes 655360 | tf_op jit(solution)/shard_map/all_to_all | solution.py:257
  68.2 0.6 plane.1
  68.8 25.9 %all_to_all.16.got_ref = bf16[4,80,128]{2,1,0:T(8,128)(2,1)S(1)} all-to-all(bf16[4,80,128]{2,1,0:T(8,128)(2,1)S(1)} %plane.1), channel_id=1, replica_groups=mesh['zh'=4,'zl'=4,'core'=2,'y'=4,'x'=4] {'zh'}, dimensions={0} | all-to-all | bytes 163840 | tf_op jit(solution)/shard_map/all_to_all | solution.py:257
  94.7 0.0 copy-done
  94.7 1.2 %finish.1 = (f32[3]{0:T(128)}, f32[1,128]{1,0:T(1,128)}, f32[64,128]{1,0:T(8,128)}) custom-call(s32[5]{0:T(128)S(1)} %stack.23.pos_ref, bf16[4,80,128]{2,1,0:T(8,128)(2,1)S(1)} %all_to_all.16.got_ref, f32[8,128]{1,0:T(8,128)S(1)} %get-tuple-element.27.sq_ref, f32[1,128]{1,0:T(1,128)S(1)} %bitcast.12), custom_call_target="tpu_custom_call" | custom-call | flops 1000000 | bytes 1000000 | tf_op jit(solution)/shard_map/finish/pallas_call | solution.py:349
Async XLA Ops:
  2.7 12.8 %collective-permute-start = (bf16[2048,128]{1,0:T(8,128)(2,1)S(1)}, bf16[2048,128]{1,0:T(8,128)(2,1)S(1)}, u32[]{:S(2)}, u32[]{:S(2)}) collective-permute-start(bf16[2048,128]{1,0:T(8,128)(2,1)S(1)} %get-tuple-element.20.own), channel_id=1, source_target_pairs={{1,0},{2,1},{3,2},{0,3},{19,16},{16,17},{17,18},{18,19},{5,4},{6,5... | collective-permute-start | bytes 1572872 | tf_op jit(solution)/shard_map/ppermute | solution.py:253
  7.4 17.2 %collective-permute-start.3 = (bf16[2048,128]{1,0:T(8,128)(2,1)S(1)}, bf16[2048,128]{1,0:T(8,128)(2,1)S(1)}, u32[]{:S(2)}, u32[]{:S(2)}) collective-permute-start(bf16[2048,128]{1,0:T(8,128)(2,1)S(1)} %get-tuple-element.20.own), channel_id=1, source_target_pairs={{4,0},{8,4},{12,8},{0,12},{28,16},{16,20},{20,24},{24,28},{5,1},{9... | collective-permute-start | bytes 1572872 | tf_op jit(solution)/shard_map/ppermute | solution.py:253
  12.3 29.8 %collective-permute-start.1 = (bf16[2048,128]{1,0:T(8,128)(2,1)S(1)}, bf16[2048,128]{1,0:T(8,128)(2,1)S(1)}, u32[]{:S(2)}, u32[]{:S(2)}) collective-permute-start(bf16[2048,128]{1,0:T(8,128)(2,1)S(1)} %get-tuple-element.20.own), channel_id=1, source_target_pairs={{3,0},{0,1},{1,2},{2,3},{17,16},{18,17},{19,18},{16,19},{7,4},{4,5... | collective-permute-start | bytes 1572872 | tf_op jit(solution)/shard_map/ppermute | solution.py:253
  15.5 26.6 %collective-permute-start.2 = (bf16[2048,128]{1,0:T(8,128)(2,1)S(1)}, bf16[2048,128]{1,0:T(8,128)(2,1)}, u32[]{:S(2)}, u32[]{:S(2)}) collective-permute-start(bf16[2048,128]{1,0:T(8,128)(2,1)S(1)} %collective-permute-done.xa), channel_id=1, source_target_pairs={{1,0},{2,1},{3,2},{0,3},{19,16},{16,17},{17,18},{18,19},{5,4},{6,5... | collective-permute-start | bytes 1572872 | tf_op jit(solution)/shard_map/ppermute | solution.py:253
  21.1 23.9 %collective-permute-start.4 = (bf16[2048,128]{1,0:T(8,128)(2,1)S(1)}, bf16[2048,128]{1,0:T(8,128)(2,1)S(1)}, u32[]{:S(2)}, u32[]{:S(2)}) collective-permute-start(bf16[2048,128]{1,0:T(8,128)(2,1)S(1)} %get-tuple-element.20.own), channel_id=1, source_target_pairs={{12,0},{0,4},{4,8},{8,12},{20,16},{24,20},{28,24},{16,28},{13,1},{... | collective-permute-start | bytes 1572872 | tf_op jit(solution)/shard_map/ppermute | solution.py:253
  24.6 20.4 %collective-permute-start.5 = (bf16[2048,128]{1,0:T(8,128)(2,1)S(1)}, bf16[2048,128]{1,0:T(8,128)(2,1)S(1)}, u32[]{:S(2)}, u32[]{:S(2)}) collective-permute-start(bf16[2048,128]{1,0:T(8,128)(2,1)S(1)} %collective-permute-done.3.ya), channel_id=1, source_target_pairs={{4,0},{8,4},{12,8},{0,12},{28,16},{16,20},{20,24},{24,28},{5,1},{9... | collective-permute-start | bytes 1572872 | tf_op jit(solution)/shard_map/ppermute | solution.py:253
  29.3 12.6 %all-to-all-start = ((f32[16,40,128]{2,1,0:T(8,128)}), f32[16,40,128]{2,1,0:T(8,128)S(1)}, u32[]{:S(2)}, u32[]{:S(2)}) async-start(f32[16,40,128]{2,1,0:T(8,128)} %get-tuple-element.17), calls=%async_computation | async-start | bytes 655360 | tf_op jit(solution)/shard_map/all_to_all | solution.py:257
  45.0 49.7 %copy-start = (f32[128]{0:T(128)S(1)}, f32[128]{0:T(128)}, u32[]{:S(2)}) copy-start(f32[128]{0:T(128)} %param.9) | copy-start | bytes 1540
  46.5 3.4 %collective-permute-start.6 = (bf16[1040,128]{1,0:T(8,128)(2,1)S(1)}, bf16[1040,128]{1,0:T(8,128)(2,1)S(1)}, u32[]{:S(2)}, u32[]{:S(2)}) collective-permute-start(bf16[1040,128]{1,0:T(8,128)(2,1)S(1)} %get-tuple-element.26), channel_id=1, source_target_pairs={{0,16},{16,0},{1,17},{17,1},{2,18},{18,2},{3,19},{19,3},{4,20},{20... | collective-permute-start | bytes 798728 | tf_op jit(solution)/shard_map/ppermute | solution.py:330

commit v8 on v7

--- a/solution.py
+++ b/solution.py
@@ -41,13 +41,21 @@
     return lax.dot_general(a, b, (((1,), (0,)), ((), ())), preferred_element_type=F32)
 
 
-def packed(four):
-    return jnp.concatenate(thirds(four) + [jnp.zeros((4, LANES), BF16)], 0)
+def packed(two):
+    return jnp.concatenate(thirds(two) + [jnp.zeros((2, LANES), BF16)], 0)
 
 
 def unpacked(rows):
     wide = rows.astype(F32)
-    return wide[..., 0:4, :] + wide[..., 4:8, :] + wide[..., 8:12, :]
+    return wide[..., 0:2, :] + wide[..., 2:4, :] + wide[..., 4:6, :]
+
+
+def in_lanes(parts):
+    lane = lax.broadcasted_iota(jnp.int32, (1, LANES), 1)
+    row = jnp.zeros((1, LANES), F32)
+    for j, part in enumerate(parts):
+        row = jnp.where(lane == j, jnp.sum(part, axis=1, keepdims=True), row)
+    return jnp.concatenate([row, jnp.zeros((7, LANES), F32)], 0)
 
 
 def project_kernel(v_ref, start_ref, dir_ref, out_ref, rows, flat, ends, sems):
@@ -126,13 +134,13 @@
         change = (expected - base_total) - counts * (jnp.log(expected) - base_log)
         part.append(jnp.sum(change, axis=0, keepdims=True) * (1.0 / PROC))
         norms.append(step * (2.0 * cross + step * square))
-    sq_ref[...] = jnp.concatenate(norms + [jnp.zeros((5, LANES), F32)], 0)
+    sq_ref[...] = in_lanes(norms)
     residual = 1.0 - counts / base_total
     left = residual * base
     w_ref[0] = base
     w_ref[1] = left
     w_ref[2] = (counts / (base_total * base_total)) * base
-    change_ref[...] = jnp.concatenate(part + [jnp.zeros((5, LANES), F32)], 0)
+    change_ref[...] = in_lanes(part)
 
 
 def bin_mask():
@@ -186,7 +194,7 @@
     lax.fori_loop(0, CHUNKS, chunk, 0, unroll=4)
     right[:, ROWS:] = jac_rows[...].T
     total = jnp.sum(grad[...].T, axis=0, keepdims=True)
-    extra = packed(jnp.concatenate([total, change_ref[0:3, :]], 0))
+    extra = packed(jnp.concatenate([total, change_ref[0:1, :]], 0))
     extra_ref[...] = extra
     product(pos_ref, right, (own, ya), jac_cols, 0, kept_ref, sent_ref)
     sent_ref[PIECES * 64 :, :] = extra
@@ -233,8 +241,9 @@
     col = lax.broadcasted_iota(jnp.int32, (64, LANES), 1) + pos_ref[3] * LANES
     hess_ref[...] = (tile + (row == col).astype(F32)) * scale
     grad_ref[...] = (extra[0:1] + start_ref[...]) * scale
+    line = (extra[1:2] + 0.5 * sq_ref[0:1, :]) * scale
     for j in range(3):
-        line_ref[j] = jnp.sum(extra[1 + j : 2 + j, :] + 0.5 * sq_ref[j : j + 1, :]) * scale
+        line_ref[j] = line[0, j]
 
 
 def in_hbm(array):
@@ -301,10 +310,10 @@
     core = lax.axis_index("core")
     block = lax.axis_index(("zh", "zl", "core"))
     position = jnp.stack([px, py, block, py * SIDE + px, core]).astype(jnp.int32)
-    tiles = arrays_of(((PIECES * 64, LANES), F32), ((PIECES * 64 + 16, LANES), BF16))
+    tiles = arrays_of(((PIECES * 64, LANES), F32), ((PIECES * 64 + 8, LANES), BF16))
     right, extra, kept, other = pl.pallas_call(
         rows_kernel,
-        out_shape=arrays_of(((SIDE * LANES, DEPTH), BF16), ((16, LANES), BF16)) + tiles,
+        out_shape=arrays_of(((SIDE * LANES, DEPTH), BF16), ((8, LANES), BF16)) + tiles,
         in_specs=[SMEM] + [VMEM] * 7,
         out_specs=(VMEM, VMEM, VMEM, VMEM),
         scratch_shapes=[
@@ -330,7 +339,7 @@
     swapped = lax.ppermute(other, "core", [(0, 1), (1, 0)])
     pair = pl.pallas_call(
         pair_kernel,
-        out_shape=jax.ShapeDtypeStruct((PIECES, 80, LANES), BF16),
+        out_shape=jax.ShapeDtypeStruct((PIECES, 72, LANES), BF16),
         in_specs=[VMEM] * 3,
         out_specs=VMEM,
         compiler_params=PARAMS,
@@ -339,7 +348,7 @@
     )(kept, extra, swapped)
     near = pl.pallas_call(
         plane_kernel,
-        out_shape=jax.ShapeDtypeStruct((SIDE, 80, LANES), BF16),
+        out_shape=jax.ShapeDtypeStruct((SIDE, 72, LANES), BF16),
         in_specs=[SMEM, VMEM],
         out_specs=VMEM,
         compiler_params=PARAMS,

time: 96.5 us -> 95.2 us (0.987)
  the two profiles are of different devices: /device:TPU:32 before, /device:TPU:1 now
where the time goes in v8:
time: 95.2 us; the launch traced here: 93.4 us
  starting transfers between devices  37.7 us (40%)
  blocking collectives  36.1 us (38%)
  Pallas kernels  9.58 us (10%)
  waiting for transfers between devices  9.17 us (10%)
    all_to_all x2, blocking collectives, exchanged(): return lax.all_to_all(array, axes, 0, 0, tiled=True)  36.1 us
    ppermute x6, starting transfers between devices, around(): return lax.ppermute(array, ('core', axis), pairs)  19.5 us
    ppermute x1, starting transfers between devices, body(): swapped = lax.ppermute(other, 'core', [(0, 1), (1, 0)])  12 us
    all_to_all x1, waiting for transfers between devices, exchanged(): return lax.all_to_all(array, axes, 0, 0, tiled=True)  6.79 us
    all_to_all x1, starting transfers between devices, exchanged(): return lax.all_to_all(array, axes, 0, 0, tiled=True)  6.22 us
    pallas_call x1, Pallas kernels, body(): pl.pallas_call(rows_kernel, out_shape=arrays_of(((SIDE * LANES, DEPTH), B...  2.83 us
    pallas_call x1, Pallas kernels, body(): pl.pallas_call(project_kernel, out_shape=arrays_of(((16, 40, LANES), F32)...  2.09 us
  transfers between devices with their start and end apart: 8, of which 3 were waited for; matrix products, arithmetic and copies ran while one was open for 0% of the time, Pallas kernels for 4%

profile of v8, /device:TPU:1, one launch (start us, length us, event | category | flops | bytes accessed | tf_op | source)
XLA Modules:
  0.0 93.4 jit_solution(15779510455702137872)
XLA Ops:
  0.6 2.1 %project.1 = (f32[16,40,128]{2,1,0:T(8,128)}, bf16[2048,128]{1,0:T(8,128)(2,1)S(1)}) custom-call(bf16[2048,128]{1,0:T(8,128)(2,1)} %bitcast.13, f32[1,128]{1,0:T(1,128)} %bitcast.11, f32[1,128]{1,0:T(1,128)} %bitcast.14), custom_call_target="tpu_custom_call" | custom-call | flops 10000000 | bytes 1000000 | tf_op jit(solution)/shard_map/project/pallas_call | solution.py:271
  2.7 3.9 %collective-permute-start = (bf16[2048,128]{1,0:T(8,128)(2,1)S(1)}, bf16[2048,128]{1,0:T(8,128)(2,1)S(1)}, u32[]{:S(2)}, u32[]{:S(2)}) collective-permute-start(bf16[2048,128]{1,0:T(8,128)(2,1)S(1)} %get-tuple-element.20.own), channel_id=1, source_target_pairs={{1,0},{2,1},{3,2},{0,3},{19,16},{16,17},{17,18},{18,19},{5,4},{6,5... | collective-permute-start | bytes 1572872 | tf_op jit(solution)/shard_map/ppermute | solution.py:262
  6.7 3.2 %collective-permute-start.3 = (bf16[2048,128]{1,0:T(8,128)(2,1)S(1)}, bf16[2048,128]{1,0:T(8,128)(2,1)S(1)}, u32[]{:S(2)}, u32[]{:S(2)}) collective-permute-start(bf16[2048,128]{1,0:T(8,128)(2,1)S(1)} %get-tuple-element.20.own), channel_id=1, source_target_pairs={{4,0},{8,4},{12,8},{0,12},{28,16},{16,20},{20,24},{24,28},{5,1},{9... | collective-permute-start | bytes 1572872 | tf_op jit(solution)/shard_map/ppermute | solution.py:262
  9.9 3.4 %collective-permute-start.1 = (bf16[2048,128]{1,0:T(8,128)(2,1)S(1)}, bf16[2048,128]{1,0:T(8,128)(2,1)S(1)}, u32[]{:S(2)}, u32[]{:S(2)}) collective-permute-start(bf16[2048,128]{1,0:T(8,128)(2,1)S(1)} %get-tuple-element.20.own), channel_id=1, source_target_pairs={{3,0},{0,1},{1,2},{2,3},{17,16},{18,17},{19,18},{16,19},{7,4},{4,5... | collective-permute-start | bytes 1572872 | tf_op jit(solution)/shard_map/ppermute | solution.py:262
  13.3 1.2 %collective-permute-done.xa = bf16[2048,128]{1,0:T(8,128)(2,1)S(1)} collective-permute-done((bf16[2048,128]{1,0:T(8,128)(2,1)S(1)}, bf16[2048,128]{1,0:T(8,128)(2,1)S(1)}, u32[]{:S(2)}, u32[]{:S(2)}) %collective-permute-start) | collective-permute-done | bytes 524320 | tf_op jit(solution)/shard_map/ppermute | solution.py:262
  14.5 2.4 %collective-permute-start.2 = (bf16[2048,128]{1,0:T(8,128)(2,1)S(1)}, bf16[2048,128]{1,0:T(8,128)(2,1)}, u32[]{:S(2)}, u32[]{:S(2)}) collective-permute-start(bf16[2048,128]{1,0:T(8,128)(2,1)S(1)} %collective-permute-done.xa), channel_id=1, source_target_pairs={{1,0},{2,1},{3,2},{0,3},{19,16},{16,17},{17,18},{18,19},{5,4},{6,5... | collective-permute-start | bytes 1572872 | tf_op jit(solution)/shard_map/ppermute | solution.py:262
  16.9 4.6 %collective-permute-start.4 = (bf16[2048,128]{1,0:T(8,128)(2,1)S(1)}, bf16[2048,128]{1,0:T(8,128)(2,1)S(1)}, u32[]{:S(2)}, u32[]{:S(2)}) collective-permute-start(bf16[2048,128]{1,0:T(8,128)(2,1)S(1)} %get-tuple-element.20.own), channel_id=1, source_target_pairs={{12,0},{0,4},{4,8},{8,12},{20,16},{24,20},{28,24},{16,28},{13,1},{... | collective-permute-start | bytes 1572872 | tf_op jit(solution)/shard_map/ppermute | solution.py:262
  21.5 0.0 collective-permute-done.3.ya
  21.5 1.9 %collective-permute-start.5 = (bf16[2048,128]{1,0:T(8,128)(2,1)S(1)}, bf16[2048,128]{1,0:T(8,128)(2,1)S(1)}, u32[]{:S(2)}, u32[]{:S(2)}) collective-permute-start(bf16[2048,128]{1,0:T(8,128)(2,1)S(1)} %collective-permute-done.3.ya), channel_id=1, source_target_pairs={{4,0},{8,4},{12,8},{0,12},{28,16},{16,20},{20,24},{24,28},{5,1},{9... | collective-permute-start | bytes 1572872 | tf_op jit(solution)/shard_map/ppermute | solution.py:262
  23.5 6.2 %all-to-all-start = ((f32[16,40,128]{2,1,0:T(8,128)}), f32[16,40,128]{2,1,0:T(8,128)S(1)}, u32[]{:S(2)}, u32[]{:S(2)}) async-start(f32[16,40,128]{2,1,0:T(8,128)} %get-tuple-element.17), calls=%async_computation | async-start | bytes 655360 | tf_op jit(solution)/shard_map/all_to_all | solution.py:266
  29.7 0.1 stack.23.pos_ref
  29.8 1.0 %layout.1.local_ref = f32[40,128]{1,0:T(8,128)S(1)} custom-call(f32[8,256]{1,0:T(8,128)} %bitcast.15, s32[1,256]{1,0:T(1,128)} %bitcast.16, f32[3]{0:T(128)} %steps_ref.1), custom_call_target="tpu_custom_call" | custom-call | flops 10000000 | bytes 1000000 | tf_op jit(solution)/shard_map/layout/pallas_call | solution.py:289
  30.8 6.8 %all-to-all-done.got_ref = f32[16,40,128]{2,1,0:T(8,128)S(1)} async-done(((f32[16,40,128]{2,1,0:T(8,128)}), f32[16,40,128]{2,1,0:T(8,128)S(1)}, u32[]{:S(2)}, u32[]{:S(2)}) %all-to-all-start) | async-done | bytes 327712 | tf_op jit(solution)/shard_map/all_to_all | solution.py:266
  37.6 0.3 weights.1
  37.9 0.0 collective-permute-done.1.xb
  37.9 0.0 collective-permute-done.2.xr
  38.0 2.8 %rows.1 = (bf16[512,2304]{1,0:T(8,128)(2,1)S(1)}, bf16[8,128]{1,0:T(8,128)(2,1)S(1)}, f32[1024,128]{1,0:T(8,128)S(1)}, bf16[1032,128]{1,0:T(8,128)(2,1)S(1)}) custom-call(s32[5]{0:T(128)S(1)} %stack.23.pos_ref, f32[3,16,128]{2,1,0:T(8,128)S(1)} %get-tuple-element.18.w_ref, f32[8,128]{1,0:T(8,128)S(1)} %get-tuple-element.19.change_ref, ...), custom_call_target="tpu_custom_call" | custom-call | flops 1500000000 | bytes 5000000 | tf_op jit(solution)/shard_map/rows/pallas_call | solution.py:314
  40.8 0.0 collective-permute-done.4.yb
  40.8 0.0 collective-permute-done.5.yr
  40.8 0.0 copy-start
  40.8 1.5 %hessian.1 = (f32[1024,128]{1,0:T(8,128)S(1)}, bf16[1032,128]{1,0:T(8,128)(2,1)S(1)}) custom-call(s32[5]{0:T(128)S(1)} %stack.23.pos_ref, f32[3,16,128]{2,1,0:T(8,128)S(1)} %get-tuple-element.18.w_ref, bf16[512,2304]{1,0:T(8,128)(2,1)S(1)} %get-tuple-element.21.right, ...), custom_call_target="tpu_custom_call", output_to_operand_aliasing={{0}: (5, {}), {1}: (6, {})} | custom-call | flops 1000000000 | bytes 5000000 | tf_op jit(solution)/shard_map/hessian/pallas_call | solution.py:328
  42.3 12.0 %collective-permute-start.6 = (bf16[1032,128]{1,0:T(8,128)(2,1)S(1)}, bf16[1032,128]{1,0:T(8,128)(2,1)S(1)}, u32[]{:S(2)}, u32[]{:S(2)}) collective-permute-start(bf16[1032,128]{1,0:T(8,128)(2,1)S(1)} %get-tuple-element.26), channel_id=1, source_target_pairs={{0,16},{16,0},{1,17},{17,1},{2,18},{18,2},{3,19},{19,3},{4,20},{20... | collective-permute-start | bytes 792584 | tf_op jit(solution)/shard_map/ppermute | solution.py:339
  54.3 1.1 %collective-permute-done.6.got_ref = bf16[1032,128]{1,0:T(8,128)(2,1)S(1)} collective-permute-done((bf16[1032,128]{1,0:T(8,128)(2,1)S(1)}, bf16[1032,128]{1,0:T(8,128)(2,1)S(1)}, u32[]{:S(2)}, u32[]{:S(2)}) %collective-permute-start.6) | collective-permute-done | bytes 264224 | tf_op jit(solution)/shard_map/ppermute | solution.py:339
  55.5 0.1 pair.1
  55.5 13.2 %all_to_all.15.got_ref = bf16[16,72,128]{2,1,0:T(8,128)(2,1)S(1)} all-to-all(bf16[16,72,128]{2,1,0:T(8,128)(2,1)S(1)} %pair.1), channel_id=1, replica_groups=mesh['zh'=4,'zl'=4,'core'=2,'y'=4,'x'=4] {'zl','y'}, dimensions={0} | all-to-all | bytes 589824 | tf_op jit(solution)/shard_map/all_to_all | solution.py:266
  68.8 0.6 plane.1
  69.4 22.9 %all_to_all.16.got_ref = bf16[4,72,128]{2,1,0:T(8,128)(2,1)S(1)} all-to-all(bf16[4,72,128]{2,1,0:T(8,128)(2,1)S(1)} %plane.1), channel_id=1, replica_groups=mesh['zh'=4,'zl'=4,'core'=2,'y'=4,'x'=4] {'zh'}, dimensions={0} | all-to-all | bytes 147456 | tf_op jit(solution)/shard_map/all_to_all | solution.py:266
  92.2 0.0 copy-done
  92.2 1.2 %finish.1 = (f32[3]{0:T(128)}, f32[1,128]{1,0:T(1,128)}, f32[64,128]{1,0:T(8,128)}) custom-call(s32[5]{0:T(128)S(1)} %stack.23.pos_ref, bf16[4,72,128]{2,1,0:T(8,128)(2,1)S(1)} %all_to_all.16.got_ref, f32[8,128]{1,0:T(8,128)S(1)} %get-tuple-element.27.sq_ref, f32[1,128]{1,0:T(1,128)S(1)} %bitcast.12), custom_call_target="tpu_custom_call" | custom-call | flops 1000000 | bytes 1000000 | tf_op jit(solution)/shard_map/finish/pallas_call | solution.py:358
Async XLA Ops:
  2.7 11.8 %collective-permute-start = (bf16[2048,128]{1,0:T(8,128)(2,1)S(1)}, bf16[2048,128]{1,0:T(8,128)(2,1)S(1)}, u32[]{:S(2)}, u32[]{:S(2)}) collective-permute-start(bf16[2048,128]{1,0:T(8,128)(2,1)S(1)} %get-tuple-element.20.own), channel_id=1, source_target_pairs={{1,0},{2,1},{3,2},{0,3},{19,16},{16,17},{17,18},{18,19},{5,4},{6,5... | collective-permute-start | bytes 1572872 | tf_op jit(solution)/shard_map/ppermute | solution.py:262
  6.7 14.9 %collective-permute-start.3 = (bf16[2048,128]{1,0:T(8,128)(2,1)S(1)}, bf16[2048,128]{1,0:T(8,128)(2,1)S(1)}, u32[]{:S(2)}, u32[]{:S(2)}) collective-permute-start(bf16[2048,128]{1,0:T(8,128)(2,1)S(1)} %get-tuple-element.20.own), channel_id=1, source_target_pairs={{4,0},{8,4},{12,8},{0,12},{28,16},{16,20},{20,24},{24,28},{5,1},{9... | collective-permute-start | bytes 1572872 | tf_op jit(solution)/shard_map/ppermute | solution.py:262
  9.9 28.1 %collective-permute-start.1 = (bf16[2048,128]{1,0:T(8,128)(2,1)S(1)}, bf16[2048,128]{1,0:T(8,128)(2,1)S(1)}, u32[]{:S(2)}, u32[]{:S(2)}) collective-permute-start(bf16[2048,128]{1,0:T(8,128)(2,1)S(1)} %get-tuple-element.20.own), channel_id=1, source_target_pairs={{3,0},{0,1},{1,2},{2,3},{17,16},{18,17},{19,18},{16,19},{7,4},{4,5... | collective-permute-start | bytes 1572872 | tf_op jit(solution)/shard_map/ppermute | solution.py:262
  14.5 23.5 %collective-permute-start.2 = (bf16[2048,128]{1,0:T(8,128)(2,1)S(1)}, bf16[2048,128]{1,0:T(8,128)(2,1)}, u32[]{:S(2)}, u32[]{:S(2)}) collective-permute-start(bf16[2048,128]{1,0:T(8,128)(2,1)S(1)} %collective-permute-done.xa), channel_id=1, source_target_pairs={{1,0},{2,1},{3,2},{0,3},{19,16},{16,17},{17,18},{18,19},{5,4},{6,5... | collective-permute-start | bytes 1572872 | tf_op jit(solution)/shard_map/ppermute | solution.py:262
  16.9 23.9 %collective-permute-start.4 = (bf16[2048,128]{1,0:T(8,128)(2,1)S(1)}, bf16[2048,128]{1,0:T(8,128)(2,1)S(1)}, u32[]{:S(2)}, u32[]{:S(2)}) collective-permute-start(bf16[2048,128]{1,0:T(8,128)(2,1)S(1)} %get-tuple-element.20.own), channel_id=1, source_target_pairs={{12,0},{0,4},{4,8},{8,12},{20,16},{24,20},{28,24},{16,28},{13,1},{... | collective-permute-start | bytes 1572872 | tf_op jit(solution)/shard_map/ppermute | solution.py:262
  21.5 19.3 %collective-permute-start.5 = (bf16[2048,128]{1,0:T(8,128)(2,1)S(1)}, bf16[2048,128]{1,0:T(8,128)(2,1)S(1)}, u32[]{:S(2)}, u32[]{:S(2)}) collective-permute-start(bf16[2048,128]{1,0:T(8,128)(2,1)S(1)} %collective-permute-done.3.ya), channel_id=1, source_target_pairs={{4,0},{8,4},{12,8},{0,12},{28,16},{16,20},{20,24},{24,28},{5,1},{9... | collective-permute-start | bytes 1572872 | tf_op jit(solution)/shard_map/ppermute | solution.py:262
  23.5 14.1 %all-to-all-start = ((f32[16,40,128]{2,1,0:T(8,128)}), f32[16,40,128]{2,1,0:T(8,128)S(1)}, u32[]{:S(2)}, u32[]{:S(2)}) async-start(f32[16,40,128]{2,1,0:T(8,128)} %get-tuple-element.17), calls=%async_computation | async-start | bytes 655360 | tf_op jit(solution)/shard_map/all_to_all | solution.py:266
  40.8 51.4 %copy-start = (f32[128]{0:T(128)S(1)}, f32[128]{0:T(128)}, u32[]{:S(2)}) copy-start(f32[128]{0:T(128)} %param.9) | copy-start | bytes 1540
  42.3 13.1 %collective-permute-start.6 = (bf16[1032,128]{1,0:T(8,128)(2,1)S(1)}, bf16[1032,128]{1,0:T(8,128)(2,1)S(1)}, u32[]{:S(2)}, u32[]{:S(2)}) collective-permute-start(bf16[1032,128]{1,0:T(8,128)(2,1)S(1)} %get-tuple-element.26), channel_id=1, source_target_pairs={{0,16},{16,0},{1,17},{17,1},{2,18},{18,2},{3,19},{19,3},{4,20},{20... | collective-permute-start | bytes 792584 | tf_op jit(solution)/shard_map/ppermute | solution.py:339
